TPU v7x, 32 devices: a whole 2x2x4 slice. The times are simulated.
32 devices in a mesh: horiz: 8 (over y, x, core), vert: 4 (over z).
Axes of the slice: x: 2, y: 2, z: 4, core: 2. Of those that a mesh axis runs over, the one named last changes fastest.
Arguments:
- velocity: float32 [3, 32, 256, 512], P(None, 'horiz', None, 'vert'), may hold values from -6 to 6
- dust: float32 [32, 256, 128], P('horiz', 'vert'), may hold values from 0.1 to 2
- eligible: int32 [32, 2], P('horiz'), may hold values 0 or 1
- terrain: int32 [32, 256], P('horiz', 'vert'), may hold values from 0 to 3
Outputs:
- velocity_next: float32 [3, 32, 256, 512], P(None, 'horiz', None, 'vert')
- dust_next: float32 [32, 256, 128], P('horiz', 'vert')
All inputs are finite; a program needn't handle non-finite values. No bound on the sum of `eligible` on one device may be relied on, other than what follows from the above.
Results may differ from a plain program's by a relative error of at most 0.0015.
Values may be sent and summed in bfloat16 or wider, within the bound.
No kernel may reach another device: no remote copies, remote signals or barrier semaphores. Data moves between devices by JAX's collectives and lax.ppermute only.
A program may use at most 64 MiB of HBM per device.

v0:
```python
import jax
import jax.numpy as jnp
from jax import lax
from jax.sharding import PartitionSpec as P

DSTEPS = 2


def extended(value, sides, width):
    for axis, dim in sides:
        size, length = (lax.axis_size(axis), value.shape[dim])
        up = [(i, (i + 1) % size) for i in range(size - 1)]
        down = [(j, i) for i, j in up]
        last = lax.slice_in_dim(value, length - width, length, axis=dim)
        first = lax.slice_in_dim(value, 0, width, axis=dim)
        before = lax.ppermute(last, axis, up)
        after = lax.ppermute(first, axis, down)
        value = jnp.concatenate([before, value, after], axis=dim)
    return value


def broadcast(block, axis, owner):
    block = jnp.where(lax.axis_index(axis) == owner, block, jnp.zeros_like(block))
    return lax.psum(block, axis)


def stencil_sum(padded, field):
    near = padded[2:, 1:-1, 1:-1] + padded[:-2, 1:-1, 1:-1]
    near = near + padded[1:-1, 2:, 1:-1] + padded[1:-1, :-2, 1:-1]
    near = near + padded[1:-1, 1:-1, 2:] + padded[1:-1, 1:-1, :-2]
    return near - 6.0 * field


def local(velocity, dust, eligible, terrain):
    outer = extended(velocity, (("horiz", 1), ("vert", 3)), 1)
    outer = jnp.pad(outer, ((0, 0), (0, 0), (1, 1), (0, 0)))
    velocity_next = velocity + 0.12 * jnp.stack(
        [stencil_sum(outer[comp], velocity[comp]) for comp in range(3)]
    )
    lowest = velocity_next.astype(jnp.bfloat16)
    strip = dust.shape[1]
    column = lax.axis_index("vert")
    whole = broadcast(lowest, "vert", 0)
    ground = lax.dynamic_slice_in_dim(whole, column * strip, strip, 2)
    ground = ground.astype(jnp.float32)
    wind_x, wind_y, wind_z = (ground[0], ground[1], ground[2] - 0.5)
    flags = lax.dynamic_slice_in_dim(jnp.repeat(eligible, 128, axis=1), column * strip, strip, 1)
    layer = lax.broadcasted_iota(jnp.int32, dust.shape, 2)
    surface = layer == terrain[:, :, None]
    speed = jnp.sqrt(wind_x * wind_x + wind_y * wind_y)
    lift = jnp.where(surface & (flags[:, :, None] == 1), 0.5 * jnp.maximum(speed - 1.0, 0.0), 0.0)
    solid = layer < terrain[:, :, None]
    conc = dust
    for step in range(DSTEPS):
        padded = extended(conc.astype(jnp.bfloat16), (("horiz", 0), ("vert", 1)), 1).astype(
            conc.dtype
        )
        padded = jnp.pad(padded, ((0, 0), (0, 0), (1, 1)))
        tend = -(
            jnp.maximum(wind_x, 0.0) * (conc - padded[:-2, 1:-1, 1:-1])
            + jnp.minimum(wind_x, 0.0) * (padded[2:, 1:-1, 1:-1] - conc)
        )
        tend = tend - (
            jnp.maximum(wind_y, 0.0) * (conc - padded[1:-1, :-2, 1:-1])
            + jnp.minimum(wind_y, 0.0) * (padded[1:-1, 2:, 1:-1] - conc)
        )
        tend = tend - (
            jnp.maximum(wind_z, 0.0) * (conc - padded[1:-1, 1:-1, :-2])
            + jnp.minimum(wind_z, 0.0) * (padded[1:-1, 1:-1, 2:] - conc)
        )
        tend = tend + 0.1 * stencil_sum(padded, conc)
        conc = jnp.where(solid, 0.0, conc + 0.15 * tend + lift)
    return (velocity_next, conc)


def solution(mesh):
    placed = (
        P(None, "horiz", None, "vert"),
        P("horiz", "vert", None),
        P("horiz", None),
        P("horiz", "vert"),
    )
    return jax.shard_map(
        local,
        mesh=mesh,
        in_specs=placed,
        out_specs=(P(None, "horiz", None, "vert"), P("horiz", "vert", None)),
        check_vma=False,
    )
```

profile of v0, /device:TPU:4, one launch (start us, length us, event | category | flops | bytes accessed | tf_op | source)
XLA Modules:
  0.0 121.2 jit_solution(18231747642894760731)
XLA Ops:
  7.2 0.0 all-reduce.5.cloned.1.call-start
  7.2 1.9 %copy.13 = f32[3,4,256,128]{2,3,1,0:T(8,128)S(1)} copy(f32[3,4,256,128]{3,2,1,0:T(8,128)} %param.4) | data formatting | bytes 3145728 | tf_op args[0]
  9.1 0.0 copy-start.1
  9.1 0.1 fusion.37
  9.2 1.9 %collective-permute-start = (f32[3,1,256,128]{2,3,1,0:T(8,128)S(1)}, f32[3,1,256,128]{2,3,1,0:T(8,128)S(1)}, u32[]{:S(2)}, u32[]{:S(2)}) collective-permute-start(f32[3,1,256,128]{2,3,1,0:T(8,128)S(1)} %get-tuple-element.15), channel_id=1, source_target_pairs={{0,4},{4,8},{8,12},{12,16},{16,20},{20,24},{24,28},{1,5},{5,9},{9,... | collective-permute-start | bytes 1179656 | tf_op jit(solution)/shard_map/ppermute | solution.py:16
  11.1 0.0 copy-start.5
  11.1 4.5 %collective-permute-start.1 = (f32[3,1,256,128]{2,3,1,0:T(8,128)S(1)}, f32[3,1,256,128]{2,3,1,0:T(8,128)S(1)}, u32[]{:S(2)}, u32[]{:S(2)}) collective-permute-start(f32[3,1,256,128]{2,3,1,0:T(8,128)S(1)} %get-tuple-element.16), channel_id=1, source_target_pairs={{4,0},{8,4},{12,8},{16,12},{20,16},{24,20},{28,24},{5,1},{9,5},{13... | collective-permute-start | bytes 1179656 | tf_op jit(solution)/shard_map/ppermute | solution.py:17
  15.7 0.0 copy-done.1
  15.7 0.1 copy.22
  15.8 4.7 %collective-permute-done = f32[3,1,256,128]{2,3,1,0:T(8,128)S(1)} collective-permute-done((f32[3,1,256,128]{2,3,1,0:T(8,128)S(1)}, f32[3,1,256,128]{2,3,1,0:T(8,128)S(1)}, u32[]{:S(2)}, u32[]{:S(2)}) %collective-permute-start) | collective-permute-done | bytes 393248 | tf_op jit(solution)/shard_map/ppermute | solution.py:16
  20.6 0.9 collective-permute-done.1
  21.5 3.5 %collective-permute-start.2 = (f32[3,6,256,1]{2,3,1,0:T(1,128)S(1)}, f32[3,6,256,1]{2,3,1,0:T(1,128)S(1)}, u32[]{:S(2)}, u32[]{:S(2)}) collective-permute-start(f32[3,6,256,1]{2,3,1,0:T(1,128)S(1)} %get-tuple-element.11), channel_id=1, source_target_pairs={{0,1},{1,2},{2,3},{4,5},{5,6},{6,7},{8,9},{9,10},{10,11},{12,13},{... | collective-permute-start | bytes 55304 | tf_op jit(solution)/shard_map/ppermute | solution.py:16
  25.0 1.3 %collective-permute-start.3 = (f32[3,6,256,1]{2,3,1,0:T(1,128)S(1)}, f32[3,6,256,1]{2,3,1,0:T(1,128)S(1)}, u32[]{:S(2)}, u32[]{:S(2)}) collective-permute-start(f32[3,6,256,1]{2,3,1,0:T(1,128)S(1)} %get-tuple-element.12), channel_id=1, source_target_pairs={{1,0},{2,1},{3,2},{5,4},{6,5},{7,6},{9,8},{10,9},{11,10},{13,12},{... | collective-permute-start | bytes 55304 | tf_op jit(solution)/shard_map/ppermute | solution.py:17
  26.3 0.6 fusion.41
  27.0 1.9 %collective-permute-start.4 = (bf16[1,64,128]{1,2,0:T(8,128)(2,1)}, bf16[1,64,128]{1,2,0:T(8,128)(2,1)}, u32[]{:S(2)}, u32[]{:S(2)}) collective-permute-start(bf16[1,64,128]{1,2,0:T(8,128)(2,1)} %get-tuple-element.23), channel_id=1, source_target_pairs={{0,4},{4,8},{8,12},{12,16},{16,20},{20,24},{24,28},{1,5},{5,9},{9,... | collective-permute-start | bytes 49160 | tf_op jit(solution)/shard_map/ppermute | solution.py:16
  28.9 4.5 %collective-permute-start.5 = (bf16[1,64,128]{1,2,0:T(8,128)(2,1)}, bf16[1,64,128]{1,2,0:T(8,128)(2,1)}, u32[]{:S(2)}, u32[]{:S(2)}) collective-permute-start(bf16[1,64,128]{1,2,0:T(8,128)(2,1)} %get-tuple-element.24), channel_id=1, source_target_pairs={{4,0},{8,4},{12,8},{16,12},{20,16},{24,20},{28,24},{5,1},{9,5},{13... | collective-permute-start | bytes 49160 | tf_op jit(solution)/shard_map/ppermute | solution.py:17
  33.4 0.0 copy-done.5
  33.4 0.1 copy.23
  33.5 0.0 collective-permute-done.2
  33.5 0.0 collective-permute-done.3
  33.5 3.3 %select_maximum_fusion = f32[3,6,258,130]{2,3,1,0:T(8,128)S(1)} fusion(f32[3,6,256,1]{2,3,1,0:T(1,128)S(1)} %collective-permute-done.3, f32[3,6,256,1]{2,3,1,0:T(1,128)S(1)} %collective-permute-done.2, f32[3,1,256,128]{2,3,1,0:T(8,128)S(1)} %collective-permute-done.1, f32[3,4,256,128]{2,3,1,0:T(8,128)S(1)} %copy.13, ...), kind=kLoop, calls=%fused_computation.2 | loop fusion | flops 7244640 | bytes 4811040 | tf_op jit(solution)/shard_map/concatenate | solution.py:18
  36.9 0.2 slice_bitcast_fusion.2
  37.1 0.8 fusion.7
  37.9 1.4 %fusion.10 = (f32[1,4,256,128]{2,3,1,0:T(8,128)S(1)}, f32[1,4,256,128]{2,3,1,0:T(8,128)S(1)}) fusion(f32[3,4,256,128]{2,3,1,0:T(8,128)S(1)} %copy.13, f32[6,258,130]{1,2,0:T(8,128)S(1)} %get-tuple-element.8, f32[6,258,130]{1,2,0:T(8,128)S(1)} %get-tuple-element.10), kind=kLoop, calls=%fused_computation.34 | loop fusion | flops 1835008 | bytes 8388608 | tf_op jit(solution)/shard_map/stack | solution.py:37
  39.3 1.2 %convert_select_fusion = (bf16[3,4,256,128]{2,3,1,0:T(8,128)(2,1)}, f32[3,4,256,128]{2,3,1,0:T(8,128)S(1)}) fusion(pred[]{:T(512)S(6)} %eq.16, f32[3,4,256,128]{2,3,1,0:T(8,128)S(1)} %copy.13, f32[1,4,256,128]{2,3,1,0:T(8,128)S(1)} %get-tuple-element.14, f32[1,4,256,128]{2,3,1,0:T(8,128)S(1)} %fusion.7, f32[1,4,256,128]{2,3,1,0:T(8,128)S(1)} %get-tuple-element.13), kind=kLoop, calls=%fused_computation.12 | loop fusion | flops 2359296 | bytes 5505025 | tf_op jit(solution)/shard_map/jit(_where)/select_n | solution.py:23
  40.6 0.0 all-reduce.5.cloned.1.call-update
  40.6 0.1 broadcast_bitcast_fusion
  40.7 0.0 collective-permute-done.4
  40.7 0.0 collective-permute-done.5
  40.7 0.8 pad_maximum_fusion
  41.5 0.0 copy-start.4
  41.5 0.1 fusion.39
  41.6 4.6 %collective-permute-start.6 = (bf16[6,1,128]{1,2,0:T(8,128)(2,1)S(1)}, bf16[6,1,128]{1,2,0:T(8,128)(2,1)S(1)}, u32[]{:S(2)}, u32[]{:S(2)}) collective-permute-start(bf16[6,1,128]{1,2,0:T(8,128)(2,1)S(1)} %get-tuple-element.19), channel_id=1, source_target_pairs={{0,1},{1,2},{2,3},{4,5},{5,6},{6,7},{8,9},{9,10},{10,11},{12,13},{... | collective-permute-start | bytes 4616 | tf_op jit(solution)/shard_map/ppermute | solution.py:16
  46.2 1.3 %collective-permute-start.7 = (bf16[6,1,128]{1,2,0:T(8,128)(2,1)S(1)}, bf16[6,1,128]{1,2,0:T(8,128)(2,1)S(1)}, u32[]{:S(2)}, u32[]{:S(2)}) collective-permute-start(bf16[6,1,128]{1,2,0:T(8,128)(2,1)S(1)} %get-tuple-element.20), channel_id=1, source_target_pairs={{1,0},{2,1},{3,2},{5,4},{6,5},{7,6},{9,8},{10,9},{11,10},{13,12},{... | collective-permute-start | bytes 4616 | tf_op jit(solution)/shard_map/ppermute | solution.py:17
  47.5 0.1 dynamic-slice_compare_fusion
  47.6 5.4 %collective-permute-done.6 = bf16[6,1,128]{1,2,0:T(8,128)(2,1)S(1)} collective-permute-done((bf16[6,1,128]{1,2,0:T(8,128)(2,1)S(1)}, bf16[6,1,128]{1,2,0:T(8,128)(2,1)S(1)}, u32[]{:S(2)}, u32[]{:S(2)}) %collective-permute-start.6) | collective-permute-done | bytes 1568 | tf_op jit(solution)/shard_map/ppermute | solution.py:16
  53.0 7.9 %collective-permute-done.7 = bf16[6,1,128]{1,2,0:T(8,128)(2,1)S(1)} collective-permute-done((bf16[6,1,128]{1,2,0:T(8,128)(2,1)S(1)}, bf16[6,1,128]{1,2,0:T(8,128)(2,1)S(1)}, u32[]{:S(2)}, u32[]{:S(2)}) %collective-permute-start.7) | collective-permute-done | bytes 1568 | tf_op jit(solution)/shard_map/ppermute | solution.py:17
  60.9 1.0 maximum_convert_fusion
  61.8 27.2 %all-reduce.5.cloned.1.call-done = bf16[3,4,256,128]{2,3,1,0:T(8,128)(2,1)} async-done(((bf16[3,4,256,128]{2,3,1,0:T(8,128)(2,1)}), bf16[3,4,256,128]{2,3,1,0:T(8,128)(2,1)}) %all-reduce.5.cloned.1.call-update) | async-done | bytes 786448 | tf_op jit(solution)/shard_map/psum | solution.py:24
  89.1 1.2 dynamic-slice_convert_fusion
  90.2 0.0 copy-done.4
  90.2 1.3 %fusion.34 = (bf16[4,64,128]{1,2,0:T(8,128)(2,1)S(1)}, f32[4,64,128]{1,2,0:T(8,128)}) fusion(pred[4,64]{1,0:T(4,128)(4,1)S(1)} %dynamic-slice_compare_fusion, f32[4,64,128]{1,2,0:T(8,128)S(1)} %copy.22, f32[6,66,128]{1,2,0:T(8,128)S(1)} %maximum_convert_fusion, f32[3,4,64,128]{2,3,1,0:T(8,128)S(1)} %dynamic-slice_convert_fusion, s32[4,64]{1,0:T(4,128)S(1)} %copy-done.4), kind=kLoop, calls=%fused_computation.94 | loop fusion | flops 1605632 | bytes 2689536 | tf_op jit(solution)/shard_map/convert_element_type | solution.py:55
  91.6 1.9 %collective-permute-start.8 = (bf16[1,64,128]{1,2,0:T(8,128)(2,1)S(1)}, bf16[1,64,128]{1,2,0:T(8,128)(2,1)S(1)}, u32[]{:S(2)}, u32[]{:S(2)}) collective-permute-start(bf16[1,64,128]{1,2,0:T(8,128)(2,1)S(1)} %get-tuple-element.21), channel_id=1, source_target_pairs={{0,4},{4,8},{8,12},{12,16},{16,20},{20,24},{24,28},{1,5},{5,9},{9,... | collective-permute-start | bytes 49160 | tf_op jit(solution)/shard_map/ppermute | solution.py:16
  93.5 4.5 %collective-permute-start.9 = (bf16[1,64,128]{1,2,0:T(8,128)(2,1)S(1)}, bf16[1,64,128]{1,2,0:T(8,128)(2,1)S(1)}, u32[]{:S(2)}, u32[]{:S(2)}) collective-permute-start(bf16[1,64,128]{1,2,0:T(8,128)(2,1)S(1)} %get-tuple-element.22), channel_id=1, source_target_pairs={{4,0},{8,4},{12,8},{16,12},{20,16},{24,20},{28,24},{5,1},{9,5},{13... | collective-permute-start | bytes 49160 | tf_op jit(solution)/shard_map/ppermute | solution.py:17
  98.0 0.0 collective-permute-done.8
  98.1 0.0 copy-start.2
  98.1 1.6 %collective-permute-done.9 = bf16[1,64,128]{1,2,0:T(8,128)(2,1)S(1)} collective-permute-done((bf16[1,64,128]{1,2,0:T(8,128)(2,1)S(1)}, bf16[1,64,128]{1,2,0:T(8,128)(2,1)S(1)}, u32[]{:S(2)}, u32[]{:S(2)}) %collective-permute-start.9) | collective-permute-done | bytes 16416 | tf_op jit(solution)/shard_map/ppermute | solution.py:17
  99.6 0.0 copy-start.3
  99.7 0.1 fusion.38
  99.8 3.1 %collective-permute-start.10 = (bf16[6,1,128]{1,2,0:T(8,128)(2,1)S(1)}, bf16[6,1,128]{1,2,0:T(8,128)(2,1)S(1)}, u32[]{:S(2)}, u32[]{:S(2)}) collective-permute-start(bf16[6,1,128]{1,2,0:T(8,128)(2,1)S(1)} %get-tuple-element.17), channel_id=1, source_target_pairs={{0,1},{1,2},{2,3},{4,5},{5,6},{6,7},{8,9},{9,10},{10,11},{12,13},{... | collective-permute-start | bytes 4616 | tf_op jit(solution)/shard_map/ppermute | solution.py:16
  102.9 1.3 %collective-permute-start.11 = (bf16[6,1,128]{1,2,0:T(8,128)(2,1)S(1)}, bf16[6,1,128]{1,2,0:T(8,128)(2,1)S(1)}, u32[]{:S(2)}, u32[]{:S(2)}) collective-permute-start(bf16[6,1,128]{1,2,0:T(8,128)(2,1)S(1)} %get-tuple-element.18), channel_id=1, source_target_pairs={{1,0},{2,1},{3,2},{5,4},{6,5},{7,6},{9,8},{10,9},{11,10},{13,12},{... | collective-permute-start | bytes 4616 | tf_op jit(solution)/shard_map/ppermute | solution.py:17
  104.2 0.0 copy-done.2
  104.2 0.0 copy-done.3
  104.2 0.0 copy-start
  104.2 1.6 %copy.24 = f32[3,4,256,128]{3,2,1,0:T(8,128)} copy(f32[3,4,256,128]{2,3,1,0:T(8,128)S(1)} %get-tuple-element.7) | data formatting | bytes 3145728
  105.9 2.0 %collective-permute-done.10 = bf16[6,1,128]{1,2,0:T(8,128)(2,1)S(1)} collective-permute-done((bf16[6,1,128]{1,2,0:T(8,128)(2,1)S(1)}, bf16[6,1,128]{1,2,0:T(8,128)(2,1)S(1)}, u32[]{:S(2)}, u32[]{:S(2)}) %collective-permute-start.10) | collective-permute-done | bytes 1568 | tf_op jit(solution)/shard_map/ppermute | solution.py:16
  107.9 4.2 %collective-permute-done.11 = bf16[6,1,128]{1,2,0:T(8,128)(2,1)S(1)} collective-permute-done((bf16[6,1,128]{1,2,0:T(8,128)(2,1)S(1)}, bf16[6,1,128]{1,2,0:T(8,128)(2,1)S(1)}, u32[]{:S(2)}, u32[]{:S(2)}) %collective-permute-start.11) | collective-permute-done | bytes 1568 | tf_op jit(solution)/shard_map/ppermute | solution.py:17
  112.0 1.0 maximum_convert_fusion.1
  113.0 0.0 copy-done
  113.0 0.6 fusion.24
  113.6 0.8 copy.25
  (5 shorter events, 0.1 us)
Async XLA Ops:
  7.2 81.9 %all-reduce.5.cloned.1.call-start = ((), (), s32[]{:S(2)}) async-start(), calls=%async_computation | async-start | bytes 1572864 | tf_op jit(solution)/shard_map/psum | solution.py:24
  9.1 6.6 %copy-start.1 = (f32[4,64,128]{2,1,0:T(8,128)S(1)}, f32[4,64,128]{2,1,0:T(8,128)}, u32[]{:S(2)}) copy-start(f32[4,64,128]{2,1,0:T(8,128)} %param.5) | copy-start | bytes 393220
  9.2 11.4 %collective-permute-start = (f32[3,1,256,128]{2,3,1,0:T(8,128)S(1)}, f32[3,1,256,128]{2,3,1,0:T(8,128)S(1)}, u32[]{:S(2)}, u32[]{:S(2)}) collective-permute-start(f32[3,1,256,128]{2,3,1,0:T(8,128)S(1)} %get-tuple-element.15), channel_id=1, source_target_pairs={{0,4},{4,8},{8,12},{12,16},{16,20},{20,24},{24,28},{1,5},{5,9},{9,... | collective-permute-start | bytes 1179656 | tf_op jit(solution)/shard_map/ppermute | solution.py:16
  11.1 22.3 %copy-start.5 = (s32[4,2]{0,1:T(2,128)S(1)}, s32[4,2]{0,1:T(2,128)}, u32[]{:S(2)}) copy-start(s32[4,2]{0,1:T(2,128)} %param.6) | copy-start | bytes 100
  11.1 10.4 %collective-permute-start.1 = (f32[3,1,256,128]{2,3,1,0:T(8,128)S(1)}, f32[3,1,256,128]{2,3,1,0:T(8,128)S(1)}, u32[]{:S(2)}, u32[]{:S(2)}) collective-permute-start(f32[3,1,256,128]{2,3,1,0:T(8,128)S(1)} %get-tuple-element.16), channel_id=1, source_target_pairs={{4,0},{8,4},{12,8},{16,12},{20,16},{24,20},{28,24},{5,1},{9,5},{13... | collective-permute-start | bytes 1179656 | tf_op jit(solution)/shard_map/ppermute | solution.py:17
  21.5 12.0 %collective-permute-start.2 = (f32[3,6,256,1]{2,3,1,0:T(1,128)S(1)}, f32[3,6,256,1]{2,3,1,0:T(1,128)S(1)}, u32[]{:S(2)}, u32[]{:S(2)}) collective-permute-start(f32[3,6,256,1]{2,3,1,0:T(1,128)S(1)} %get-tuple-element.11), channel_id=1, source_target_pairs={{0,1},{1,2},{2,3},{4,5},{5,6},{6,7},{8,9},{9,10},{10,11},{12,13},{... | collective-permute-start | bytes 55304 | tf_op jit(solution)/shard_map/ppermute | solution.py:16
  25.0 8.5 %collective-permute-start.3 = (f32[3,6,256,1]{2,3,1,0:T(1,128)S(1)}, f32[3,6,256,1]{2,3,1,0:T(1,128)S(1)}, u32[]{:S(2)}, u32[]{:S(2)}) collective-permute-start(f32[3,6,256,1]{2,3,1,0:T(1,128)S(1)} %get-tuple-element.12), channel_id=1, source_target_pairs={{1,0},{2,1},{3,2},{5,4},{6,5},{7,6},{9,8},{10,9},{11,10},{13,12},{... | collective-permute-start | bytes 55304 | tf_op jit(solution)/shard_map/ppermute | solution.py:17
  27.0 13.7 %collective-permute-start.4 = (bf16[1,64,128]{1,2,0:T(8,128)(2,1)}, bf16[1,64,128]{1,2,0:T(8,128)(2,1)}, u32[]{:S(2)}, u32[]{:S(2)}) collective-permute-start(bf16[1,64,128]{1,2,0:T(8,128)(2,1)} %get-tuple-element.23), channel_id=1, source_target_pairs={{0,4},{4,8},{8,12},{12,16},{16,20},{20,24},{24,28},{1,5},{5,9},{9,... | collective-permute-start | bytes 49160 | tf_op jit(solution)/shard_map/ppermute | solution.py:16
  28.9 11.8 %collective-permute-start.5 = (bf16[1,64,128]{1,2,0:T(8,128)(2,1)}, bf16[1,64,128]{1,2,0:T(8,128)(2,1)}, u32[]{:S(2)}, u32[]{:S(2)}) collective-permute-start(bf16[1,64,128]{1,2,0:T(8,128)(2,1)} %get-tuple-element.24), channel_id=1, source_target_pairs={{4,0},{8,4},{12,8},{16,12},{20,16},{24,20},{28,24},{5,1},{9,5},{13... | collective-permute-start | bytes 49160 | tf_op jit(solution)/shard_map/ppermute | solution.py:17
  41.5 48.7 %copy-start.4 = (s32[4,64]{1,0:T(4,128)S(1)}, s32[4,64]{1,0:T(4,128)}, u32[]{:S(2)}) copy-start(s32[4,64]{1,0:T(4,128)} %param.7) | copy-start | bytes 3076
  41.6 11.3 %collective-permute-start.6 = (bf16[6,1,128]{1,2,0:T(8,128)(2,1)S(1)}, bf16[6,1,128]{1,2,0:T(8,128)(2,1)S(1)}, u32[]{:S(2)}, u32[]{:S(2)}) collective-permute-start(bf16[6,1,128]{1,2,0:T(8,128)(2,1)S(1)} %get-tuple-element.19), channel_id=1, source_target_pairs={{0,1},{1,2},{2,3},{4,5},{5,6},{6,7},{8,9},{9,10},{10,11},{12,13},{... | collective-permute-start | bytes 4616 | tf_op jit(solution)/shard_map/ppermute | solution.py:16
  46.2 14.7 %collective-permute-start.7 = (bf16[6,1,128]{1,2,0:T(8,128)(2,1)S(1)}, bf16[6,1,128]{1,2,0:T(8,128)(2,1)S(1)}, u32[]{:S(2)}, u32[]{:S(2)}) collective-permute-start(bf16[6,1,128]{1,2,0:T(8,128)(2,1)S(1)} %get-tuple-element.20), channel_id=1, source_target_pairs={{1,0},{2,1},{3,2},{5,4},{6,5},{7,6},{9,8},{10,9},{11,10},{13,12},{... | collective-permute-start | bytes 4616 | tf_op jit(solution)/shard_map/ppermute | solution.py:17
  91.6 6.5 %collective-permute-start.8 = (bf16[1,64,128]{1,2,0:T(8,128)(2,1)S(1)}, bf16[1,64,128]{1,2,0:T(8,128)(2,1)S(1)}, u32[]{:S(2)}, u32[]{:S(2)}) collective-permute-start(bf16[1,64,128]{1,2,0:T(8,128)(2,1)S(1)} %get-tuple-element.21), channel_id=1, source_target_pairs={{0,4},{4,8},{8,12},{12,16},{16,20},{20,24},{24,28},{1,5},{5,9},{9,... | collective-permute-start | bytes 49160 | tf_op jit(solution)/shard_map/ppermute | solution.py:16
  93.5 6.1 %collective-permute-start.9 = (bf16[1,64,128]{1,2,0:T(8,128)(2,1)S(1)}, bf16[1,64,128]{1,2,0:T(8,128)(2,1)S(1)}, u32[]{:S(2)}, u32[]{:S(2)}) collective-permute-start(bf16[1,64,128]{1,2,0:T(8,128)(2,1)S(1)} %get-tuple-element.22), channel_id=1, source_target_pairs={{4,0},{8,4},{12,8},{16,12},{20,16},{24,20},{28,24},{5,1},{9,5},{13... | collective-permute-start | bytes 49160 | tf_op jit(solution)/shard_map/ppermute | solution.py:17
  98.1 6.2 %copy-start.2 = (bf16[1,64,128]{1,2,0:T(8,128)(2,1)}, bf16[1,64,128]{1,2,0:T(8,128)(2,1)S(1)}, u32[]{:S(2)}) copy-start(bf16[1,64,128]{1,2,0:T(8,128)(2,1)S(1)} %collective-permute-done.8) | copy-start | bytes 49156
  99.6 4.6 %copy-start.3 = (bf16[1,64,128]{1,2,0:T(8,128)(2,1)}, bf16[1,64,128]{1,2,0:T(8,128)(2,1)S(1)}, u32[]{:S(2)}) copy-start(bf16[1,64,128]{1,2,0:T(8,128)(2,1)S(1)} %collective-permute-done.9) | copy-start | bytes 49156
  99.8 8.1 %collective-permute-start.10 = (bf16[6,1,128]{1,2,0:T(8,128)(2,1)S(1)}, bf16[6,1,128]{1,2,0:T(8,128)(2,1)S(1)}, u32[]{:S(2)}, u32[]{:S(2)}) collective-permute-start(bf16[6,1,128]{1,2,0:T(8,128)(2,1)S(1)} %get-tuple-element.17), channel_id=1, source_target_pairs={{0,1},{1,2},{2,3},{4,5},{5,6},{6,7},{8,9},{9,10},{10,11},{12,13},{... | collective-permute-start | bytes 4616 | tf_op jit(solution)/shard_map/ppermute | solution.py:16
  102.9 9.1 %collective-permute-start.11 = (bf16[6,1,128]{1,2,0:T(8,128)(2,1)S(1)}, bf16[6,1,128]{1,2,0:T(8,128)(2,1)S(1)}, u32[]{:S(2)}, u32[]{:S(2)}) collective-permute-start(bf16[6,1,128]{1,2,0:T(8,128)(2,1)S(1)} %get-tuple-element.18), channel_id=1, source_target_pairs={{1,0},{2,1},{3,2},{5,4},{6,5},{7,6},{9,8},{10,9},{11,10},{13,12},{... | collective-permute-start | bytes 4616 | tf_op jit(solution)/shard_map/ppermute | solution.py:17
  104.2 8.8 %copy-start = (f32[4,64,128]{1,2,0:T(8,128)S(1)}, f32[4,64,128]{1,2,0:T(8,128)}, u32[]{:S(2)}) copy-start(f32[4,64,128]{1,2,0:T(8,128)} %get-tuple-element.5) | copy-start | bytes 393220
Sparse Core Ops, SparseCore 0:
  40.7 48.2 all-reduce.4
where the time goes:
time: 122 us; the launch traced here: 121 us
  waiting for transfers between devices  53.9 us (44%)
  starting transfers between devices  34.4 us (28%)
  between operations  14.3 us (12%)
  other arithmetic  12.8 us (10%)
  local copies, waits for them, and re-layouts  5.79 us (5%)
    psum x1, waiting for transfers between devices, broadcast(): return lax.psum(block, axis)  27.2 us
    ppermute x6, starting transfers between devices, extended(): after = lax.ppermute(first, axis, down)  17.5 us
    ppermute x6, starting transfers between devices, extended(): before = lax.ppermute(last, axis, up)  16.9 us
    ppermute x6, waiting for transfers between devices, extended(): after = lax.ppermute(first, axis, down)  14.5 us
    ppermute x6, waiting for transfers between devices, extended(): before = lax.ppermute(last, axis, up)  12.2 us
    unnamed x19, local copies, waits for them, and re-layouts  4.59 us
    concatenate x3, other arithmetic, extended(): value = jnp.concatenate([before, value, after], axis=dim)  4.18 us
  transfers between devices with their start and end apart: 13, of which 8 were waited for; matrix products, arithmetic and copies ran while one was open for 10% of the time, Pallas kernels for 0%

commit v1 on v0

v1 whole, which is shorter than its diff:
```python
import functools

import jax
import jax.numpy as jnp
from jax import lax
from jax.experimental import pallas as pl
from jax.experimental.pallas import tpu as pltpu
from jax.sharding import PartitionSpec as P

DSTEPS = 2
LANES = 128
EDGE = 8
BF = jnp.bfloat16
F32 = jnp.float32

VMEM = pl.BlockSpec(memory_space=pltpu.VMEM)


def call(kernel, out_shape, name, scratch=(), cost=1 << 20, **kwargs):
    return pl.pallas_call(
        kernel,
        out_shape=out_shape,
        scratch_shapes=list(scratch),
        compiler_params=pltpu.CompilerParams(vmem_limit_bytes=40 << 20),
        cost_estimate=pl.CostEstimate(flops=cost, bytes_accessed=cost, transcendentals=0),
        name=name,
        **kwargs,
    )


def shaped(*dims, dtype=BF):
    return jax.ShapeDtypeStruct(dims, dtype)


def iota(shape, dim):
    return lax.broadcasted_iota(jnp.int32, shape, dim)


def pick(shape, pairs):
    row, col = iota(shape, 0), iota(shape, 1)
    hit = functools.reduce(jnp.logical_or, [(row == r) & (col == c) for r, c in pairs])
    return jnp.where(hit, 1.0, 0.0).astype(BF)


def pack_strips(v_ref, *outs):
    ncomp, nx, ny, _ = v_ref.shape
    strips, up_ref, down_ref = (outs[:-2], outs[-2], outs[-1])
    size = ny // len(strips)
    for t, out in enumerate(strips):
        low, high = (max(t * size - EDGE, 0), min((t + 1) * size + EDGE, ny))
        start = low - (t * size - EDGE)
        for comp in range(ncomp):
            for x in range(nx):
                rows = v_ref[comp, x, low:high, :]
                parts = [rows]
                if start:
                    parts = [jnp.zeros((start, LANES), F32)] + parts
                if start + high - low < size + 2 * EDGE:
                    parts = parts + [jnp.zeros((size + 2 * EDGE - start - high + low, LANES), F32)]
                rows = jnp.concatenate(parts, 0) if len(parts) > 1 else rows
                out[comp * nx + x] = rows.astype(BF)
    up_ref[...] = v_ref[:, nx - 1].astype(BF)
    down_ref[...] = v_ref[:, 0].astype(BF)


def pack_faces(size, v_ref, dust_ref, terrain_ref, zm_ref, zp_ref, lay_ref, low, high):
    ncomp, nx, ny, nz = v_ref.shape
    ends = pick((16, nz), [(0, 0), (1, nz - 1)])
    low[...] = jnp.zeros_like(low)
    high[...] = jnp.zeros_like(high)
    for j in range(ncomp * nx):
        for half in range(ny // LANES):
            block = v_ref[j // nx, j % nx, half * LANES : (half + 1) * LANES, :].astype(BF)
            both = lax.dot_general(ends, block, (((1,), (1,)), ((), ())), preferred_element_type=F32)
            low[j : j + 1, half * LANES : (half + 1) * LANES] = both[0:1]
            high[j : j + 1, half * LANES : (half + 1) * LANES] = both[1:2]
    terrain = terrain_ref[...].astype(F32)
    terrain = jnp.concatenate([terrain, jnp.zeros((nx, LANES - size), F32)], 1)
    terrain = jnp.concatenate([terrain, jnp.zeros((16 - nx, LANES), F32)], 0)
    lane = iota((16, LANES), 1)
    whole = low[...]
    for t in range(lay_ref.shape[0]):
        shift = (EDGE - t * size) % ny
        moved = pltpu.roll(whole, shift, 1) if shift else whole
        row = lane + (t * size - EDGE)
        lay_ref[t] = jnp.where((row >= 0) & (row < ny), moved[:, :LANES], 0.0).astype(BF)
    nb = ny // LANES
    for half in range(nb):
        zm_ref[half * 16 : half * 16 + 16] = low[:, half * LANES : (half + 1) * LANES].astype(BF)
        zp_ref[half * 16 : half * 16 + 16] = high[:, half * LANES : (half + 1) * LANES].astype(BF)
    at = nb * 16
    zm_ref[at : at + nx * EDGE] = dust_ref[:, :EDGE].reshape(nx * EDGE, LANES).astype(BF)
    zp_ref[at : at + nx * EDGE] = dust_ref[:, size - EDGE :].reshape(nx * EDGE, LANES).astype(BF)
    at = at + nx * EDGE
    zm_ref[at : at + 16] = terrain.astype(BF)
    zp_ref[at : at + 16] = terrain.astype(BF)
    zm_ref[at + 16 : at + 32] = lay_ref[0]


def advance(v_ref, below_ref, above_ref, rm_ref, rp_ref, out_ref):
    _, nx, ny, nz = v_ref.shape
    comp = pl.program_id(0)
    row, lane = iota((LANES, nz), 0), iota((LANES, nz), 1)
    brow, blane = iota((LANES, nz), 0), iota((LANES, nz), 1)
    nb = ny // LANES
    for half in range(nb):
        a = half * LANES
        faces = jnp.concatenate(
            [
                rm_ref[half * 16 : half * 16 + 16].astype(F32),
                rp_ref[half * 16 : half * 16 + 16].astype(F32),
                jnp.zeros((LANES - 32, LANES), F32),
            ],
            0,
        )
        turned = faces.T.astype(BF)
        for x in range(nx):
            j = comp * nx + x
            place = ((brow == j) & (blane == nz - 1)) | ((brow == 16 + j) & (blane == 0))
            place = jnp.where(place, 1.0, 0.0).astype(BF)
            side = lax.dot_general(turned, place, (((1,), (0,)), ((), ())), preferred_element_type=F32)
            f = v_ref[0, x, a : a + LANES, :]
            near = side + jnp.where(lane == 0, 0.0, pltpu.roll(f, 1, 1))
            near = near + jnp.where(lane == nz - 1, 0.0, pltpu.roll(f, nz - 1, 1))
            prev = v_ref[0, x, a - 1 : a, :] if a else jnp.zeros((1, nz), F32)
            post = v_ref[0, x, a + LANES : a + LANES + 1, :] if a + LANES < ny else jnp.zeros((1, nz), F32)
            near = near + jnp.where(row == 0, prev, pltpu.roll(f, 1, 0))
            near = near + jnp.where(row == LANES - 1, post, pltpu.roll(f, LANES - 1, 0))
            near = near + (v_ref[0, x - 1, a : a + LANES, :] if x else below_ref[0, a : a + LANES, :].astype(F32))
            near = near + (
                v_ref[0, x + 1, a : a + LANES, :] if x < nx - 1 else above_ref[0, a : a + LANES, :].astype(F32)
            )
            out_ref[0, x, a : a + LANES, :] = f + 0.12 * (near - 6.0 * f)


def prepare(nstrips, *refs):
    strips = refs[:nstrips]
    lays = refs[nstrips : 2 * nstrips - 1]
    dust_ref, terrain_ref, eligible_ref, rm_ref, rp_ref = refs[2 * nstrips - 1 : 2 * nstrips + 4]
    wind_ref, conc_ref, cols_ref, up_ref, down_ref, edge_ref, raw = refs[2 * nstrips + 4 :]
    nx, size, nz = dust_ref.shape
    ncomp = strips[0].shape[0] // nx
    rows = size + 2 * EDGE
    place = lax.axis_index("vert")
    for t in range(nstrips):
        @pl.when(place == t)
        def _(t=t):
            raw[...] = strips[t][...]

    face = (rm_ref.shape[0] - 32 - nx * EDGE)
    zero = jnp.zeros((16, LANES), F32)
    layer = jnp.where(place == 0, rm_ref[face + nx * EDGE + 16 : face + nx * EDGE + 32].astype(F32), zero)
    layer = layer + jnp.where(place == 1, lays[0][1].astype(F32), zero)
    for got in lays[1:]:
        layer = layer + got[...].astype(F32)
    layer = jnp.concatenate([layer, jnp.zeros((LANES - 16, LANES), F32)], 0)
    turned = layer.T.astype(BF)[:rows]
    brow, blane = iota((LANES, nz), 0), iota((LANES, nz), 1)
    beside = jnp.where((brow == blane + 1) | (brow == blane - 1), 1.0, 0.0).astype(BF)
    for comp in range(ncomp):
        f = [raw[comp * nx + x].astype(F32) for x in range(nx)]
        for x in range(nx):
            j = comp * nx + x
            near = jnp.dot(raw[j], beside, preferred_element_type=F32)
            top = jnp.where((brow == j) & (blane == nz - 1), 1.0, 0.0).astype(BF)
            near = near + jnp.dot(turned, top, preferred_element_type=F32)
            near = near + pltpu.roll(f[x], 1, 0) + pltpu.roll(f[x], rows - 1, 0)
            if x:
                near = near + f[x - 1]
            if x < nx - 1:
                near = near + f[x + 1]
            wind = 0.28 * f[x] + 0.12 * near
            wind_ref[j] = wind
            if x == 0:
                down_ref[comp * rows : (comp + 1) * rows] = raw[j]
                down_ref[(ncomp + comp) * rows : (ncomp + comp + 1) * rows] = wind.astype(BF)
                edge_ref[comp] = raw[j]
            if x == nx - 1:
                up_ref[comp * rows : (comp + 1) * rows] = raw[j]
                up_ref[(ncomp + comp) * rows : (ncomp + comp + 1) * rows] = wind.astype(BF)
                edge_ref[ncomp + comp] = raw[j]
    for x in range(nx):
        before = rp_ref[face + x * EDGE : face + (x + 1) * EDGE].astype(F32)
        after = rm_ref[face + x * EDGE : face + (x + 1) * EDGE].astype(F32)
        conc_ref[x] = jnp.concatenate([before, dust_ref[x], after], 0)
    at = 2 * ncomp * rows
    up_ref[at : at + rows] = conc_ref[nx - 1].astype(BF)
    up_ref[at + rows : at + 2 * rows] = conc_ref[nx - 2].astype(BF)
    down_ref[at : at + rows] = conc_ref[0].astype(BF)
    down_ref[at + rows : at + 2 * rows] = conc_ref[1].astype(BF)
    at = at + 2 * rows
    lane = iota((nx, LANES), 1)
    own = terrain_ref[...].astype(F32)
    own = jnp.concatenate([own, jnp.zeros((nx, LANES - size), F32)], 1)
    here = face + nx * EDGE
    before = pltpu.roll(rp_ref[here : here + 16].astype(F32), (EDGE - size) % LANES, 1)[:nx]
    after = pltpu.roll(rm_ref[here : here + 16].astype(F32), (EDGE + size) % LANES, 1)[:nx]
    ground = jnp.where(lane < EDGE, before, jnp.where(lane < EDGE + size, pltpu.roll(own, EDGE, 1), after))
    y = lane + (place * size - EDGE)
    flags = jnp.zeros((nx, LANES), jnp.int32)
    blocks = eligible_ref.shape[1]
    for b in range(blocks):
        inside = (y >= b * 128) & (y < (b + 1) * 128)
        flags = jnp.where(inside, jnp.broadcast_to(eligible_ref[:, b : b + 1], (nx, LANES)), flags)
    lifted = jnp.where(flags == 1, ground, -1.0)
    cols_ref[...] = jnp.zeros_like(cols_ref)
    cols_ref[:nx] = ground
    cols_ref[EDGE : EDGE + nx] = lifted
    fill = jnp.zeros((14, LANES), F32)
    up_ref[at : at + 16] = jnp.concatenate([ground[nx - 1 :], lifted[nx - 1 :], fill], 0).astype(BF)
    down_ref[at : at + 16] = jnp.concatenate([ground[:1], lifted[:1], fill], 0).astype(BF)


def transport(ny, nhoriz, wind_ref, edge_ref, conc_ref, cols_ref, below_ref, above_ref, out_ref):
    nx, size, nz = out_ref.shape
    ncomp = edge_ref.shape[0] // 2
    rows = size + 2 * EDGE
    column, place = (lax.axis_index("horiz"), lax.axis_index("vert"))
    at = 2 * ncomp * rows
    here = at + 2 * rows

    def part(ref, i):
        return ref[i * rows : (i + 1) * rows].astype(F32)

    conc = [part(below_ref, 2 * ncomp + 1), part(below_ref, 2 * ncomp)]
    conc += [conc_ref[x] for x in range(nx)]
    conc += [part(above_ref, 2 * ncomp), part(above_ref, 2 * ncomp + 1)]
    table = jnp.concatenate(
        [
            below_ref[here : here + 16].astype(F32),
            cols_ref[...],
            above_ref[here : here + 16].astype(F32),
            jnp.zeros((LANES - 48, LANES), F32),
        ],
        0,
    ).T[:rows]
    ground = [0] + [16 + x for x in range(nx)] + [32]
    lifted = [1] + [16 + EDGE + x for x in range(nx)] + [33]
    layer = iota((rows, nz), 1).astype(F32)
    y = iota((rows, nz), 0) + (place * size - EDGE)
    inside = (y >= 0) & (y < ny)
    first, last = layer == 0.0, layer == nz - 1.0
    zero = jnp.zeros((rows, nz), F32)
    state = [None] * (nx + 2)
    for p in range(nx + 2):
        comps = []
        for comp in range(ncomp):
            if p == 0:
                w = part(below_ref, ncomp + comp) + 0.12 * edge_ref[comp].astype(F32)
            elif p == nx + 1:
                w = part(above_ref, ncomp + comp) + 0.12 * edge_ref[ncomp + comp].astype(F32)
            else:
                w = wind_ref[comp * nx + p - 1]
                if p == 1:
                    w = w + 0.12 * part(below_ref, comp)
                if p == nx:
                    w = w + 0.12 * part(above_ref, comp)
            comps.append(w)
        gu, gv, gw = comps
        speed = jnp.sqrt(gu * gu + gv * gv)
        rise = jnp.broadcast_to(table[:, lifted[p] : lifted[p] + 1], (rows, nz))
        base = jnp.broadcast_to(table[:, ground[p] : ground[p] + 1], (rows, nz))
        lift = jnp.where(layer == rise, 0.5 * jnp.maximum(speed - 1.0, 0.0), 0.0)
        keep = (layer >= base) & inside
        if p == 0:
            keep = keep & (column > 0)
        if p == nx + 1:
            keep = keep & (column < nhoriz - 1)
        coef = [
            (0.15 * (0.1 - jnp.minimum(a, 0.0)), 0.15 * (0.1 + jnp.maximum(a, 0.0)))
            for a in (gu, gv, gw - 0.5)
        ]
        state[p] = (coef, lift, keep)

    def step(p, c, below, above):
        coef, lift, keep = state[p]
        total = c + lift
        pairs = (
            (above, below),
            (pltpu.roll(c, rows - 1, 0), pltpu.roll(c, 1, 0)),
            (
                jnp.where(last, zero, pltpu.roll(c, nz - 1, 1)),
                jnp.where(first, zero, pltpu.roll(c, 1, 1)),
            ),
        )
        for (ahead, behind), (post, prev) in zip(coef, pairs):
            total = total + ahead * (post - c) - behind * (c - prev)
        return jnp.where(keep, total, 0.0)

    once = [step(p, conc[p + 1], conc[p], conc[p + 2]) for p in range(nx + 2)]
    for x in range(nx):
        twice = step(x + 1, once[x + 1], once[x], once[x + 2])
        out_ref[x] = twice[EDGE : EDGE + size]


def local(velocity, dust, eligible, terrain):
    ncomp, nx, ny, nz = velocity.shape
    size = dust.shape[1]
    nh, nv = (lax.axis_size("horiz"), lax.axis_size("vert"))
    rows = size + 2 * EDGE
    up = [(i, i + 1) for i in range(nh - 1)]
    down = [(j, i) for i, j in up]
    rise = [(i, i + 1) for i in range(nv - 1)]
    fall = [(j, i) for i, j in rise]
    nplane = ncomp * nx

    packed = call(
        pack_strips,
        [shaped(nplane, rows, LANES)] * nv + [shaped(ncomp, ny, nz)] * 2,
        "pack_strips",
    )(velocity)
    strips = list(packed[:nv])
    got = [strips[0]] + [lax.ppermute(strips[t], "vert", [(0, t)]) for t in range(1, nv)]
    below = lax.ppermute(packed[nv], "horiz", up)
    above = lax.ppermute(packed[nv + 1], "horiz", down)

    face = ny // LANES * 16
    zm, zp, lay = call(
        functools.partial(pack_faces, size),
        [shaped(face + nx * EDGE + 32, LANES), shaped(face + nx * EDGE + 16, LANES), shaped(nv, 16, LANES)],
        "pack_faces",
        [pltpu.VMEM((16, ny), F32)] * 2,
    )(velocity, dust, terrain)
    rm = lax.ppermute(zm, "vert", fall)
    rp = lax.ppermute(zp, "vert", rise)
    lays = [lay] + [lax.ppermute(lay[t], "vert", [(1, t)]) for t in range(2, nv)]

    whole = pl.BlockSpec(memory_space=pltpu.VMEM)
    velocity_next = call(
        advance,
        jax.ShapeDtypeStruct(velocity.shape, F32),
        "advance",
        grid=(ncomp,),
        in_specs=[
            pl.BlockSpec((1, nx, ny, nz), lambda i: (i, 0, 0, 0)),
            pl.BlockSpec((1, ny, nz), lambda i: (i, 0, 0)),
            pl.BlockSpec((1, ny, nz), lambda i: (i, 0, 0)),
            whole,
            whole,
        ],
        out_specs=pl.BlockSpec((1, nx, ny, nz), lambda i: (i, 0, 0, 0)),
    )(velocity, below, above, rm, rp)

    wire = (2 * ncomp + 2) * rows + 16
    wind, conc, cols, mu, md, edge = call(
        functools.partial(prepare, nv),
        [
            shaped(nplane, rows, LANES, dtype=F32),
            shaped(nx, rows, LANES, dtype=F32),
            shaped(16, LANES, dtype=F32),
            shaped(wire, LANES),
            shaped(wire, LANES),
            shaped(2 * ncomp, rows, LANES),
        ],
        "prepare",
        [pltpu.VMEM((nplane, rows, LANES), BF)],
    )(*got, *lays, dust, terrain, eligible, rm, rp)
    mu = lax.ppermute(mu, "horiz", up)
    md = lax.ppermute(md, "horiz", down)
    dust_next = call(
        functools.partial(transport, ny, nh),
        jax.ShapeDtypeStruct(dust.shape, F32),
        "transport",
    )(wind, edge, conc, cols, mu, md)
    return (velocity_next, dust_next)


def solution(mesh):
    placed = (
        P(None, "horiz", None, "vert"),
        P("horiz", "vert", None),
        P("horiz", None),
        P("horiz", "vert"),
    )
    return jax.shard_map(
        local,
        mesh=mesh,
        in_specs=placed,
        out_specs=(P(None, "horiz", None, "vert"), P("horiz", "vert", None)),
        check_vma=False,
    )
```

time: 122 us -> 44.1 us (0.36)
  the two profiles are of different devices: /device:TPU:4 before, /device:TPU:11 now
where the time goes in v1:
time: 44.1 us; the launch traced here: 43.8 us
  starting transfers between devices  26.8 us (61%)
  waiting for transfers between devices  8.45 us (19%)
  Pallas kernels  6.24 us (14%)
  local copies, waits for them, and re-layouts  1.51 us (3%)
  between operations  0.81 us (2%)
    ppermute x1, waiting for transfers between devices, local(): rp = lax.ppermute(zp, 'vert', rise)  5.53 us
    ppermute x2, starting transfers between devices, local(): lax.ppermute(lay[t], 'vert', [(1, t)])  5.51 us
    ppermute x1, starting transfers between devices, local(): below = lax.ppermute(packed[nv], 'horiz', up)  4.83 us
    ppermute x1, starting transfers between devices, local(): mu = lax.ppermute(mu, 'horiz', up)  4.54 us
    ppermute x1, starting transfers between devices, local(): rp = lax.ppermute(zp, 'vert', rise)  3.36 us
    ppermute x1, waiting for transfers between devices, local(): md = lax.ppermute(md, 'horiz', down)  2.9 us
    ppermute x3, starting transfers between devices, local(): lax.ppermute(strips[t], 'vert', [(0, t)])  2.76 us
    pallas_call x1, Pallas kernels, local(): call(advance, jax.ShapeDtypeStruct(velocity.shape, F32), 'advance', grid=...  2.72 us
  transfers between devices with their start and end apart: 11, of which 2 were waited for; matrix products, arithmetic and copies ran while one was open for 0% of the time, Pallas kernels for 9%

profile of v1, /device:TPU:11, one launch (start us, length us, event | category | flops | bytes accessed | tf_op | source)
XLA Modules:
  0.0 43.8 jit_solution(15938769743594437004)
XLA Ops:
  0.6 0.0 copy-start
  0.6 1.4 %copy-done = f32[3,4,256,128]{3,2,1,0:T(8,128)S(1)} copy-done((f32[3,4,256,128]{3,2,1,0:T(8,128)S(1)}, f32[3,4,256,128]{3,2,1,0:T(8,128)}, u32[]{:S(2)}) %copy-start) | copy-done | bytes 1572888
  2.0 0.0 copy-start.2
  2.0 0.0 copy-start.3
  2.0 0.0 copy-start.4
  2.0 1.0 %pack_strips.1 = (bf16[12,80,128]{2,1,0:T(8,128)(2,1)S(1)}, bf16[12,80,128]{2,1,0:T(8,128)(2,1)}, bf16[12,80,128]{2,1,0:T(8,128)(2,1)}, bf16[12,80,128]{2,1,0:T(...) custom-call(f32[3,4,256,128]{3,2,1,0:T(8,128)S(1)} %copy-done), custom_call_target="tpu_custom_call" | custom-call | flops 1048576 | bytes 1048576 | tf_op jit(solution)/shard_map/pack_strips/pallas_call | solution.py:307
  3.0 0.0 copy-start.1
  3.0 1.4 %collective-permute-start.4 = (bf16[12,80,128]{2,1,0:T(8,128)(2,1)}, bf16[12,80,128]{2,1,0:T(8,128)(2,1)S(1)}, u32[]{:S(2)}, u32[]{:S(2)}) collective-permute-start(bf16[12,80,128]{2,1,0:T(8,128)(2,1)} %get-tuple-element.22), channel_id=1, source_target_pairs={{0,1},{4,5},{8,9},{12,13},{16,17},{20,21},{24,25},{28,29}} | collective-permute-start | bytes 737288 | tf_op jit(solution)/shard_map/ppermute | solution.py:313
  4.4 0.7 %collective-permute-start.5 = (bf16[12,80,128]{2,1,0:T(8,128)(2,1)}, bf16[12,80,128]{2,1,0:T(8,128)(2,1)S(1)}, u32[]{:S(2)}, u32[]{:S(2)}) collective-permute-start(bf16[12,80,128]{2,1,0:T(8,128)(2,1)} %get-tuple-element.23), channel_id=1, source_target_pairs={{0,2},{4,6},{8,10},{12,14},{16,18},{20,22},{24,26},{28,30}} | collective-permute-start | bytes 737288 | tf_op jit(solution)/shard_map/ppermute | solution.py:313
  5.1 0.7 %collective-permute-start.6 = (bf16[12,80,128]{2,1,0:T(8,128)(2,1)S(1)}, bf16[12,80,128]{2,1,0:T(8,128)(2,1)S(1)}, u32[]{:S(2)}, u32[]{:S(2)}) collective-permute-start(bf16[12,80,128]{2,1,0:T(8,128)(2,1)S(1)} %get-tuple-element.24), channel_id=1, source_target_pairs={{0,3},{4,7},{8,11},{12,15},{16,19},{20,23},{24,27},{28,31}} | collective-permute-start | bytes 737288 | tf_op jit(solution)/shard_map/ppermute | solution.py:313
  5.8 0.0 copy-done.2
  5.8 0.0 copy-done.3
  5.8 0.6 %pack_faces.1 = (bf16[96,128]{1,0:T(8,128)(2,1)S(1)}, bf16[80,128]{1,0:T(8,128)(2,1)S(1)}, bf16[4,16,128]{2,1,0:T(8,128)(2,1)S(1)}) custom-call(f32[3,4,256,128]{3,2,1,0:T(8,128)S(1)} %copy-done, f32[4,64,128]{2,1,0:T(8,128)S(1)} %copy-done.2, s32[4,64]{1,0:T(4,128)S(1)} %copy-done.3), custom_call_target="tpu_custom_call" | custom-call | flops 1048576 | bytes 1048576 | tf_op jit(solution)/shard_map/pack_faces/pallas_call | solution.py:318
  6.4 4.2 %collective-permute-start.8 = (bf16[16,128]{1,0:T(8,128)(2,1)S(1)}, bf16[16,128]{1,0:T(8,128)(2,1)S(1)}, u32[]{:S(2)}, u32[]{:S(2)}) collective-permute-start(bf16[16,128]{1,0:T(8,128)(2,1)S(1)} %get-tuple-element.32), channel_id=1, source_target_pairs={{1,3},{5,7},{9,11},{13,15},{17,19},{21,23},{25,27},{29,31}} | collective-permute-start | bytes 12296 | tf_op jit(solution)/shard_map/ppermute | solution.py:326
  10.7 1.3 %collective-permute-start.7 = (bf16[16,128]{1,0:T(8,128)(2,1)S(1)}, bf16[16,128]{1,0:T(8,128)(2,1)S(1)}, u32[]{:S(2)}, u32[]{:S(2)}) collective-permute-start(bf16[16,128]{1,0:T(8,128)(2,1)S(1)} %get-tuple-element.33), channel_id=1, source_target_pairs={{1,2},{5,6},{9,10},{13,14},{17,18},{21,22},{25,26},{29,30}} | collective-permute-start | bytes 12296 | tf_op jit(solution)/shard_map/ppermute | solution.py:326
  12.0 0.0 collective-permute-done.8.refs_6_
  12.0 1.9 %collective-permute-start.2 = (bf16[96,128]{1,0:T(8,128)(2,1)S(1)}, bf16[96,128]{1,0:T(8,128)(2,1)S(1)}, u32[]{:S(2)}, u32[]{:S(2)}) collective-permute-start(bf16[96,128]{1,0:T(8,128)(2,1)S(1)} %get-tuple-element.19), channel_id=1, source_target_pairs={{1,0},{2,1},{3,2},{5,4},{6,5},{7,6},{9,8},{10,9},{11,10},{13,12},{... | collective-permute-start | bytes 73736 | tf_op jit(solution)/shard_map/ppermute | solution.py:324
  13.9 0.0 collective-permute-done.7.refs_5_
  13.9 3.4 %collective-permute-start.3 = (bf16[80,128]{1,0:T(8,128)(2,1)S(1)}, bf16[80,128]{1,0:T(8,128)(2,1)S(1)}, u32[]{:S(2)}, u32[]{:S(2)}) collective-permute-start(bf16[80,128]{1,0:T(8,128)(2,1)S(1)} %get-tuple-element.20), channel_id=1, source_target_pairs={{0,1},{1,2},{2,3},{4,5},{5,6},{6,7},{8,9},{9,10},{10,11},{12,13},{... | collective-permute-start | bytes 61448 | tf_op jit(solution)/shard_map/ppermute | solution.py:325
  17.3 5.5 %collective-permute-done.3.rp_ref.refs_11_ = bf16[80,128]{1,0:T(8,128)(2,1)S(1)} collective-permute-done((bf16[80,128]{1,0:T(8,128)(2,1)S(1)}, bf16[80,128]{1,0:T(8,128)(2,1)S(1)}, u32[]{:S(2)}, u32[]{:S(2)}) %collective-permute-start.3) | collective-permute-done | bytes 20512 | tf_op jit(solution)/shard_map/ppermute | solution.py:325
  22.8 4.8 %collective-permute-start = (bf16[3,256,128]{2,1,0:T(8,128)(2,1)}, bf16[3,256,128]{2,1,0:T(8,128)(2,1)S(1)}, u32[]{:S(2)}, u32[]{:S(2)}) collective-permute-start(bf16[3,256,128]{2,1,0:T(8,128)(2,1)} %get-tuple-element.17), channel_id=1, source_target_pairs={{0,4},{4,8},{8,12},{12,16},{16,20},{20,24},{24,28},{1,5},{5,9},{9,... | collective-permute-start | bytes 589832 | tf_op jit(solution)/shard_map/ppermute | solution.py:314
  27.7 0.0 collective-permute-done.2.rm_ref.refs_10_
  27.7 1.9 %collective-permute-start.1 = (bf16[3,256,128]{2,1,0:T(8,128)(2,1)}, bf16[3,256,128]{2,1,0:T(8,128)(2,1)S(1)}, u32[]{:S(2)}, u32[]{:S(2)}) collective-permute-start(bf16[3,256,128]{2,1,0:T(8,128)(2,1)} %get-tuple-element.18), channel_id=1, source_target_pairs={{4,0},{8,4},{12,8},{16,12},{20,16},{24,20},{28,24},{5,1},{9,5},{13... | collective-permute-start | bytes 589832 | tf_op jit(solution)/shard_map/ppermute | solution.py:315
  29.6 0.0 copy-done.4
  29.6 0.1 copy.6.refs_9_
  29.7 0.0 collective-permute-done.4.refs_1_
  29.7 0.0 collective-permute-done.5.refs_2_
  29.7 0.0 collective-permute-done.6.refs_3_
  29.7 0.5 %prepare.1 = (f32[12,80,128]{2,1,0:T(8,128)S(1)}, f32[4,80,128]{2,1,0:T(8,128)S(1)}, f32[16,128]{1,0:T(8,128)S(1)}, bf16[656,128]{1,0:T(8,128)(2,1)S(1)}, bf16[6...) custom-call(bf16[12,80,128]{2,1,0:T(8,128)(2,1)S(1)} %get-tuple-element.21.refs_0_, ...), custom_call_target="tpu_custom_call" | custom-call | flops 1048576 | bytes 1048576 | tf_op jit(solution)/shard_map/prepare/pallas_call | solution.py:345
  30.2 4.5 %collective-permute-start.9 = (bf16[656,128]{1,0:T(8,128)(2,1)S(1)}, bf16[656,128]{1,0:T(8,128)(2,1)S(1)}, u32[]{:S(2)}, u32[]{:S(2)}) collective-permute-start(bf16[656,128]{1,0:T(8,128)(2,1)S(1)} %get-tuple-element.30), channel_id=1, source_target_pairs={{0,4},{4,8},{8,12},{12,16},{16,20},{20,24},{24,28},{1,5},{5,9},{9,... | collective-permute-start | bytes 503816 | tf_op jit(solution)/shard_map/ppermute | solution.py:358
  34.8 1.9 %collective-permute-start.10 = (bf16[656,128]{1,0:T(8,128)(2,1)S(1)}, bf16[656,128]{1,0:T(8,128)(2,1)S(1)}, u32[]{:S(2)}, u32[]{:S(2)}) collective-permute-start(bf16[656,128]{1,0:T(8,128)(2,1)S(1)} %get-tuple-element.31), channel_id=1, source_target_pairs={{4,0},{8,4},{12,8},{16,12},{20,16},{24,20},{28,24},{5,1},{9,5},{13... | collective-permute-start | bytes 503816 | tf_op jit(solution)/shard_map/ppermute | solution.py:359
  36.7 0.0 collective-permute-done.below_ref
  36.7 0.0 collective-permute-done.1.above_ref
  36.7 0.0 copy-done.1
  36.7 2.7 %advance.1 = f32[3,4,256,128]{3,2,1,0:T(8,128)} custom-call(f32[3,4,256,128]{3,2,1,0:T(8,128)S(1)} %copy-done.1, bf16[3,256,128]{2,1,0:T(8,128)(2,1)S(1)} %collective-permute-done.below_ref, bf16[3,256,128]{2,1,0:T(8,128)(2,1)S(1)} %collective-permute-done.1.above_ref, bf16[96,128]{1,0:T(8,128)(2,1)S(1)} %collective-permute-done.2.rm_ref.refs_10_, ...), custom_call_target="tpu_custom_call" | custom-call | flops 1048576 | bytes 1048576 | tf_op jit(solution)/shard_map/advance/pallas_call | solution.py:329
  39.5 0.0 collective-permute-done.9.below_ref
  39.5 2.9 %collective-permute-done.10.above_ref = bf16[656,128]{1,0:T(8,128)(2,1)S(1)} collective-permute-done((bf16[656,128]{1,0:T(8,128)(2,1)S(1)}, bf16[656,128]{1,0:T(8,128)(2,1)S(1)}, u32[]{:S(2)}, u32[]{:S(2)}) %collective-permute-start.10) | collective-permute-done | bytes 167968 | tf_op jit(solution)/shard_map/ppermute | solution.py:359
  42.4 1.4 %transport.1 = f32[4,64,128]{2,1,0:T(8,128)} custom-call(f32[12,80,128]{2,1,0:T(8,128)S(1)} %get-tuple-element.26.wind_ref, bf16[6,80,128]{2,1,0:T(8,128)(2,1)S(1)} %get-tuple-element.27.edge_ref, f32[4,80,128]{2,1,0:T(8,128)S(1)} %get-tuple-element.28.conc_ref, f32[16,128]{1,0:T(8,128)S(1)} %get-tuple-element.29.cols_ref, ...), custom_call_target="tpu_custom_call" | custom-call | flops 1048576 | bytes 1048576 | tf_op jit(solution)/shard_map/transport/pallas_call | solution.py:360
  (1 shorter events, 0.0 us)
Async XLA Ops:
  0.6 1.4 %copy-start = (f32[3,4,256,128]{3,2,1,0:T(8,128)S(1)}, f32[3,4,256,128]{3,2,1,0:T(8,128)}, u32[]{:S(2)}) copy-start(f32[3,4,256,128]{3,2,1,0:T(8,128)} %v_ref.5) | copy-start | bytes 4718596
  2.0 3.8 %copy-start.2 = (f32[4,64,128]{2,1,0:T(8,128)S(1)}, f32[4,64,128]{2,1,0:T(8,128)}, u32[]{:S(2)}) copy-start(f32[4,64,128]{2,1,0:T(8,128)} %refs_7_.1) | copy-start | bytes 393220
  2.0 3.8 %copy-start.3 = (s32[4,64]{1,0:T(4,128)S(1)}, s32[4,64]{1,0:T(4,128)}, u32[]{:S(2)}) copy-start(s32[4,64]{1,0:T(4,128)} %refs_8_.1) | copy-start | bytes 3076
  2.0 27.5 %copy-start.4 = (s32[4,2]{0,1:T(2,128)S(1)}, s32[4,2]{0,1:T(2,128)}, u32[]{:S(2)}) copy-start(s32[4,2]{0,1:T(2,128)} %param.6) | copy-start | bytes 100
  3.0 33.7 %copy-start.1 = (f32[3,4,256,128]{3,2,1,0:T(8,128)S(1)}, f32[3,4,256,128]{3,2,1,0:T(8,128)}, u32[]{:S(2)}) copy-start(f32[3,4,256,128]{3,2,1,0:T(8,128)} %v_ref.5) | copy-start | bytes 4718596
  3.0 26.7 %collective-permute-start.4 = (bf16[12,80,128]{2,1,0:T(8,128)(2,1)}, bf16[12,80,128]{2,1,0:T(8,128)(2,1)S(1)}, u32[]{:S(2)}, u32[]{:S(2)}) collective-permute-start(bf16[12,80,128]{2,1,0:T(8,128)(2,1)} %get-tuple-element.22), channel_id=1, source_target_pairs={{0,1},{4,5},{8,9},{12,13},{16,17},{20,21},{24,25},{28,29}} | collective-permute-start | bytes 737288 | tf_op jit(solution)/shard_map/ppermute | solution.py:313
  4.4 25.3 %collective-permute-start.5 = (bf16[12,80,128]{2,1,0:T(8,128)(2,1)}, bf16[12,80,128]{2,1,0:T(8,128)(2,1)S(1)}, u32[]{:S(2)}, u32[]{:S(2)}) collective-permute-start(bf16[12,80,128]{2,1,0:T(8,128)(2,1)} %get-tuple-element.23), channel_id=1, source_target_pairs={{0,2},{4,6},{8,10},{12,14},{16,18},{20,22},{24,26},{28,30}} | collective-permute-start | bytes 737288 | tf_op jit(solution)/shard_map/ppermute | solution.py:313
  5.1 24.6 %collective-permute-start.6 = (bf16[12,80,128]{2,1,0:T(8,128)(2,1)S(1)}, bf16[12,80,128]{2,1,0:T(8,128)(2,1)S(1)}, u32[]{:S(2)}, u32[]{:S(2)}) collective-permute-start(bf16[12,80,128]{2,1,0:T(8,128)(2,1)S(1)} %get-tuple-element.24), channel_id=1, source_target_pairs={{0,3},{4,7},{8,11},{12,15},{16,19},{20,23},{24,27},{28,31}} | collective-permute-start | bytes 737288 | tf_op jit(solution)/shard_map/ppermute | solution.py:313
  6.4 5.5 %collective-permute-start.8 = (bf16[16,128]{1,0:T(8,128)(2,1)S(1)}, bf16[16,128]{1,0:T(8,128)(2,1)S(1)}, u32[]{:S(2)}, u32[]{:S(2)}) collective-permute-start(bf16[16,128]{1,0:T(8,128)(2,1)S(1)} %get-tuple-element.32), channel_id=1, source_target_pairs={{1,3},{5,7},{9,11},{13,15},{17,19},{21,23},{25,27},{29,31}} | collective-permute-start | bytes 12296 | tf_op jit(solution)/shard_map/ppermute | solution.py:326
  10.7 3.2 %collective-permute-start.7 = (bf16[16,128]{1,0:T(8,128)(2,1)S(1)}, bf16[16,128]{1,0:T(8,128)(2,1)S(1)}, u32[]{:S(2)}, u32[]{:S(2)}) collective-permute-start(bf16[16,128]{1,0:T(8,128)(2,1)S(1)} %get-tuple-element.33), channel_id=1, source_target_pairs={{1,2},{5,6},{9,10},{13,14},{17,18},{21,22},{25,26},{29,30}} | collective-permute-start | bytes 12296 | tf_op jit(solution)/shard_map/ppermute | solution.py:326
  12.0 15.7 %collective-permute-start.2 = (bf16[96,128]{1,0:T(8,128)(2,1)S(1)}, bf16[96,128]{1,0:T(8,128)(2,1)S(1)}, u32[]{:S(2)}, u32[]{:S(2)}) collective-permute-start(bf16[96,128]{1,0:T(8,128)(2,1)S(1)} %get-tuple-element.19), channel_id=1, source_target_pairs={{1,0},{2,1},{3,2},{5,4},{6,5},{7,6},{9,8},{10,9},{11,10},{13,12},{... | collective-permute-start | bytes 73736 | tf_op jit(solution)/shard_map/ppermute | solution.py:324
  13.9 8.9 %collective-permute-start.3 = (bf16[80,128]{1,0:T(8,128)(2,1)S(1)}, bf16[80,128]{1,0:T(8,128)(2,1)S(1)}, u32[]{:S(2)}, u32[]{:S(2)}) collective-permute-start(bf16[80,128]{1,0:T(8,128)(2,1)S(1)} %get-tuple-element.20), channel_id=1, source_target_pairs={{0,1},{1,2},{2,3},{4,5},{5,6},{6,7},{8,9},{9,10},{10,11},{12,13},{... | collective-permute-start | bytes 61448 | tf_op jit(solution)/shard_map/ppermute | solution.py:325
  22.8 13.9 %collective-permute-start = (bf16[3,256,128]{2,1,0:T(8,128)(2,1)}, bf16[3,256,128]{2,1,0:T(8,128)(2,1)S(1)}, u32[]{:S(2)}, u32[]{:S(2)}) collective-permute-start(bf16[3,256,128]{2,1,0:T(8,128)(2,1)} %get-tuple-element.17), channel_id=1, source_target_pairs={{0,4},{4,8},{8,12},{12,16},{16,20},{20,24},{24,28},{1,5},{5,9},{9,... | collective-permute-start | bytes 589832 | tf_op jit(solution)/shard_map/ppermute | solution.py:314
  27.7 9.1 %collective-permute-start.1 = (bf16[3,256,128]{2,1,0:T(8,128)(2,1)}, bf16[3,256,128]{2,1,0:T(8,128)(2,1)S(1)}, u32[]{:S(2)}, u32[]{:S(2)}) collective-permute-start(bf16[3,256,128]{2,1,0:T(8,128)(2,1)} %get-tuple-element.18), channel_id=1, source_target_pairs={{4,0},{8,4},{12,8},{16,12},{20,16},{24,20},{28,24},{5,1},{9,5},{13... | collective-permute-start | bytes 589832 | tf_op jit(solution)/shard_map/ppermute | solution.py:315
  30.2 9.2 %collective-permute-start.9 = (bf16[656,128]{1,0:T(8,128)(2,1)S(1)}, bf16[656,128]{1,0:T(8,128)(2,1)S(1)}, u32[]{:S(2)}, u32[]{:S(2)}) collective-permute-start(bf16[656,128]{1,0:T(8,128)(2,1)S(1)} %get-tuple-element.30), channel_id=1, source_target_pairs={{0,4},{4,8},{8,12},{12,16},{16,20},{20,24},{24,28},{1,5},{5,9},{9,... | collective-permute-start | bytes 503816 | tf_op jit(solution)/shard_map/ppermute | solution.py:358
  34.8 7.6 %collective-permute-start.10 = (bf16[656,128]{1,0:T(8,128)(2,1)S(1)}, bf16[656,128]{1,0:T(8,128)(2,1)S(1)}, u32[]{:S(2)}, u32[]{:S(2)}) collective-permute-start(bf16[656,128]{1,0:T(8,128)(2,1)S(1)} %get-tuple-element.31), channel_id=1, source_target_pairs={{4,0},{8,4},{12,8},{16,12},{20,16},{24,20},{28,24},{5,1},{9,5},{13... | collective-permute-start | bytes 503816 | tf_op jit(solution)/shard_map/ppermute | solution.py:359

commit v2 on v1

v2 whole, which is shorter than its diff:
```python
import functools

import jax
import jax.numpy as jnp
from jax import lax
from jax.experimental import pallas as pl
from jax.experimental.pallas import tpu as pltpu
from jax.sharding import PartitionSpec as P

DSTEPS = 2
LANES = 128
EDGE = 8
BF = jnp.bfloat16
F32 = jnp.float32

VMEM = pl.BlockSpec(memory_space=pltpu.VMEM)


def call(kernel, out_shape, name, scratch=(), cost=1 << 20, **kwargs):
    return pl.pallas_call(
        kernel,
        out_shape=out_shape,
        scratch_shapes=list(scratch),
        compiler_params=pltpu.CompilerParams(vmem_limit_bytes=40 << 20),
        cost_estimate=pl.CostEstimate(flops=cost, bytes_accessed=cost, transcendentals=0),
        name=name,
        **kwargs,
    )


def shaped(*dims, dtype=BF):
    return jax.ShapeDtypeStruct(dims, dtype)


def iota(shape, dim):
    return lax.broadcasted_iota(jnp.int32, shape, dim)


def pick(shape, pairs):
    row, col = iota(shape, 0), iota(shape, 1)
    hit = functools.reduce(jnp.logical_or, [(row == r) & (col == c) for r, c in pairs])
    return jnp.where(hit, 1.0, 0.0).astype(BF)


def pack_strips(size, v_ref, *refs):
    outs, (buf, side, sems) = (refs[:-3], refs[-3:])
    ncomp, nx, ny, nz = v_ref.shape

    @pl.when(lax.axis_index("vert") == 0)
    def _():
        copies = [pltpu.make_async_copy(v_ref.at[c], buf.at[c], sems.at[c]) for c in range(ncomp)]
        for copy in copies:
            copy.start()
        side[...] = jnp.zeros_like(side)
        for comp in range(ncomp):
            copies[comp].wait()
            for t, out in enumerate(outs):
                for x in range(nx):
                    j = comp * nx + x
                    out[j * size : (j + 1) * size] = buf[comp, x, t * size : (t + 1) * size, :].astype(BF)
                    for i, y in enumerate(halo_rows(t * size, size)):
                        if 0 <= y < ny:
                            side[t, i * 16 + j : i * 16 + j + 1] = buf[comp, x, y : y + 1, :]
        for t, out in enumerate(outs):
            out[ncomp * nx * size :] = side[t].astype(BF)


def halo_rows(start, size):
    return (start - 2, start - 1, start + size, start + size + 1)


def pack_sides(v_ref, rm_ref, far_ref, near_ref):
    del rm_ref
    nx = v_ref.shape[1]
    odd = lax.rem(lax.axis_index("horiz"), 2) == 1

    @pl.when(odd)
    def _():
        near_ref[...] = v_ref[:, 0].astype(BF)
        far_ref[...] = v_ref[:, nx - 1].astype(BF)

    @pl.when(jnp.logical_not(odd))
    def _():
        near_ref[...] = v_ref[:, nx - 1].astype(BF)
        far_ref[...] = v_ref[:, 0].astype(BF)


def pack_ends(size, v_ref, dust_ref, terrain_ref, strip_ref, zm_ref, zp_ref, lay_ref, low, high):
    del strip_ref
    ncomp, nx, ny, nz = v_ref.shape
    ends = pick((16, nz), [(0, 0), (1, nz - 1)])
    low[...] = jnp.zeros_like(low)
    high[...] = jnp.zeros_like(high)
    nb = ny // LANES
    for j in range(ncomp * nx):
        for half in range(nb):
            block = v_ref[j // nx, j % nx, half * LANES : (half + 1) * LANES, :].astype(BF)
            both = lax.dot_general(ends, block, (((1,), (1,)), ((), ())), preferred_element_type=F32)
            low[j : j + 1, half * LANES : (half + 1) * LANES] = both[0:1]
            high[j : j + 1, half * LANES : (half + 1) * LANES] = both[1:2]
    terrain = terrain_ref[...].astype(F32)
    terrain = jnp.concatenate([terrain, jnp.zeros((nx, LANES - size), F32)], 1)
    terrain = jnp.concatenate([terrain, jnp.zeros((16 - nx, LANES), F32)], 0)
    lane = iota((16, LANES), 1)
    whole = low[...]
    for t in range(lay_ref.shape[0]):
        shift = (EDGE - t * size) % ny
        moved = pltpu.roll(whole, shift, 1) if shift else whole
        row = lane + (t * size - EDGE)
        lay_ref[t] = jnp.where((row >= 0) & (row < ny), moved[:, :LANES], 0.0).astype(BF)
    for half in range(nb):
        zm_ref[half * 16 : half * 16 + 16] = low[:, half * LANES : (half + 1) * LANES].astype(BF)
        zp_ref[half * 16 : half * 16 + 16] = high[:, half * LANES : (half + 1) * LANES].astype(BF)
    at = nb * 16
    zm_ref[at : at + nx * EDGE] = dust_ref[:, :EDGE].reshape(nx * EDGE, LANES).astype(BF)
    zp_ref[at : at + nx * EDGE] = dust_ref[:, size - EDGE :].reshape(nx * EDGE, LANES).astype(BF)
    at = at + nx * EDGE
    zm_ref[at : at + 16] = terrain.astype(BF)
    zp_ref[at : at + 16] = terrain.astype(BF)
    zm_ref[at + 16 : at + 32] = lay_ref[0]
    zp_ref[at + 16 : at + 32] = lay_ref[min(2, lay_ref.shape[0] - 1)]


def advance(v_ref, far_ref, near_ref, rm_ref, rp_ref, out_ref, buf, sems):
    ncomp, nx, ny, nz = v_ref.shape
    odd = lax.rem(lax.axis_index("horiz"), 2) == 1
    row, lane = iota((LANES, nz), 0), iota((LANES, nz), 1)
    nb = ny // LANES
    turned = []
    for half in range(nb):
        faces = jnp.concatenate(
            [
                rm_ref[half * 16 : half * 16 + 16].astype(F32),
                rp_ref[half * 16 : half * 16 + 16].astype(F32),
                jnp.zeros((LANES - 32, LANES), F32),
            ],
            0,
        )
        turned.append(faces.T.astype(BF))
    copies = []
    for comp in range(ncomp):
        for half in range(nb):
            a = half * LANES
            span = slice(a, a + LANES)
            near, far = (near_ref[comp, span, :].astype(F32), far_ref[comp, span, :].astype(F32))
            below = jnp.where(odd, near, far)
            above = jnp.where(odd, far, near)
            for x in range(nx):
                j = comp * nx + x
                place = ((row == j) & (lane == nz - 1)) | ((row == 16 + j) & (lane == 0))
                place = jnp.where(place, 1.0, 0.0).astype(BF)
                sums = lax.dot_general(turned[half], place, (((1,), (0,)), ((), ())), preferred_element_type=F32)
                f = v_ref[comp, x, span, :]
                sums = sums + jnp.where(lane == 0, 0.0, pltpu.roll(f, 1, 1))
                sums = sums + jnp.where(lane == nz - 1, 0.0, pltpu.roll(f, nz - 1, 1))
                prev = v_ref[comp, x, a - 1 : a, :] if a else jnp.zeros((1, nz), F32)
                post = v_ref[comp, x, a + LANES : a + LANES + 1, :] if half < nb - 1 else jnp.zeros((1, nz), F32)
                sums = sums + jnp.where(row == 0, prev, pltpu.roll(f, 1, 0))
                sums = sums + jnp.where(row == LANES - 1, post, pltpu.roll(f, LANES - 1, 0))
                sums = sums + (v_ref[comp, x - 1, span, :] if x else below)
                sums = sums + (v_ref[comp, x + 1, span, :] if x < nx - 1 else above)
                buf[comp, x, span, :] = f + 0.12 * (sums - 6.0 * f)
        copies.append(pltpu.make_async_copy(buf.at[comp], out_ref.at[comp], sems.at[comp]))
        copies[-1].start()
    for copy in copies:
        copy.wait()


def prepare(nstrips, *refs):
    strips = refs[:nstrips]
    nlay = max(nstrips - 2, 1)
    lays = refs[nstrips : nstrips + nlay]
    dust_ref, terrain_ref, eligible_ref, rm_ref, rp_ref = refs[nstrips + nlay : nstrips + nlay + 5]
    wind_ref, conc_ref, cols_ref, far_ref, near_ref, edge_ref, frame = refs[nstrips + nlay + 5 :]
    nx, size, nz = dust_ref.shape
    nplane = frame.shape[0]
    ncomp = nplane // nx
    rows = size + 2 * EDGE
    place = lax.axis_index("vert")
    odd = lax.rem(lax.axis_index("horiz"), 2) == 1
    frame[:, :EDGE] = jnp.zeros((nplane, EDGE, nz), F32)
    frame[:, EDGE + size :] = jnp.zeros((nplane, EDGE, nz), F32)
    for t in range(nstrips):
        @pl.when(place == t)
        def _(t=t):
            beside = strips[t][nplane * size :].astype(F32)
            for j in range(nplane):
                frame[j, EDGE : EDGE + size] = strips[t][j * size : (j + 1) * size].astype(F32)
                for i, y in enumerate(halo_rows(EDGE, size)):
                    frame[j, y : y + 1] = beside[i * 16 + j : i * 16 + j + 1]

    face = rm_ref.shape[0] - 32 - nx * EDGE
    last = face + nx * EDGE + 16
    zero = jnp.zeros((16, LANES), F32)
    layer = jnp.where(place == 0, rm_ref[last : last + 16].astype(F32), zero)
    layer = layer + jnp.where(place == 1, lays[0][min(1, nstrips - 1)].astype(F32), zero)
    layer = layer + jnp.where(place == 2, rp_ref[last : last + 16].astype(F32), zero)
    for got in lays[1:]:
        layer = layer + got[...].astype(F32)
    layer = jnp.concatenate([layer, jnp.zeros((LANES - 16, LANES), F32)], 0)
    turned = layer.T.astype(BF)[:rows]
    brow, blane = iota((LANES, nz), 0), iota((LANES, nz), 1)
    beside = jnp.where((brow == blane + 1) | (brow == blane - 1), 1.0, 0.0).astype(BF)
    edges = {}
    for comp in range(ncomp):
        f = [frame[comp * nx + x] for x in range(nx)]
        for x in range(nx):
            j = comp * nx + x
            raw = f[x].astype(BF)
            near = jnp.dot(raw, beside, preferred_element_type=F32)
            top = jnp.where((brow == j) & (blane == nz - 1), 1.0, 0.0).astype(BF)
            near = near + jnp.dot(turned, top, preferred_element_type=F32)
            near = near + pltpu.roll(f[x], 1, 0) + pltpu.roll(f[x], rows - 1, 0)
            if x:
                near = near + f[x - 1]
            if x < nx - 1:
                near = near + f[x + 1]
            wind = 0.28 * f[x] + 0.12 * near
            wind_ref[j] = wind
            if x == 0:
                edge_ref[comp] = raw
            if x == nx - 1:
                edge_ref[ncomp + comp] = raw
    for x in range(nx):
        before = rp_ref[face + x * EDGE : face + (x + 1) * EDGE].astype(F32)
        after = rm_ref[face + x * EDGE : face + (x + 1) * EDGE].astype(F32)
        conc_ref[x] = jnp.concatenate([before, dust_ref[x], after], 0)
    lane = iota((nx, LANES), 1)
    own = terrain_ref[...].astype(F32)
    own = jnp.concatenate([own, jnp.zeros((nx, LANES - size), F32)], 1)
    here = face + nx * EDGE
    before = pltpu.roll(rp_ref[here : here + 16].astype(F32), (EDGE - size) % LANES, 1)[:nx]
    after = pltpu.roll(rm_ref[here : here + 16].astype(F32), (EDGE + size) % LANES, 1)[:nx]
    ground = jnp.where(lane < EDGE, before, jnp.where(lane < EDGE + size, pltpu.roll(own, EDGE, 1), after))
    y = lane + (place * size - EDGE)
    flags = jnp.zeros((nx, LANES), jnp.int32)
    for b in range(eligible_ref.shape[1]):
        inside = (y >= b * 128) & (y < (b + 1) * 128)
        flags = jnp.where(inside, jnp.broadcast_to(eligible_ref[:, b : b + 1], (nx, LANES)), flags)
    lifted = jnp.where(flags == 1, ground, -1.0)
    cols_ref[...] = jnp.zeros_like(cols_ref)
    cols_ref[:nx] = ground
    cols_ref[EDGE : EDGE + nx] = lifted
    fill = jnp.zeros((14, LANES), F32)

    def send(ref, x, inner):
        for comp in range(ncomp):
            ref[comp * rows : (comp + 1) * rows] = edge_ref[(ncomp if x else 0) + comp]
            ref[(ncomp + comp) * rows : (ncomp + comp + 1) * rows] = wind_ref[comp * nx + x].astype(BF)
        at = 2 * ncomp * rows
        ref[at : at + rows] = conc_ref[x].astype(BF)
        ref[at + rows : at + 2 * rows] = conc_ref[inner].astype(BF)
        at = at + 2 * rows
        ref[at : at + 16] = jnp.concatenate([ground[x : x + 1], lifted[x : x + 1], fill], 0).astype(BF)

    @pl.when(odd)
    def _():
        send(near_ref, 0, 1)
        send(far_ref, nx - 1, nx - 2)

    @pl.when(jnp.logical_not(odd))
    def _():
        send(near_ref, nx - 1, nx - 2)
        send(far_ref, 0, 1)


def transport(ny, nhoriz, wind_ref, edge_ref, conc_ref, cols_ref, far_ref, near_ref, out_ref):
    nx, size, nz = out_ref.shape
    ncomp = edge_ref.shape[0] // 2
    rows = size + 2 * EDGE
    column, place = (lax.axis_index("horiz"), lax.axis_index("vert"))
    odd = lax.rem(column, 2) == 1
    here = 2 * (ncomp + 1) * rows

    def below(start, n):
        return jnp.where(odd, near_ref[start : start + n].astype(F32), far_ref[start : start + n].astype(F32))

    def above(start, n):
        return jnp.where(odd, far_ref[start : start + n].astype(F32), near_ref[start : start + n].astype(F32))

    def part(side, i):
        return side(i * rows, rows)

    conc = [part(below, 2 * ncomp + 1), part(below, 2 * ncomp)]
    conc += [conc_ref[x] for x in range(nx)]
    conc += [part(above, 2 * ncomp), part(above, 2 * ncomp + 1)]
    table = jnp.concatenate(
        [below(here, 16), cols_ref[...], above(here, 16), jnp.zeros((LANES - 48, LANES), F32)], 0
    ).T[:rows]
    ground = [0] + [16 + x for x in range(nx)] + [32]
    lifted = [1] + [16 + EDGE + x for x in range(nx)] + [33]
    layer = iota((rows, nz), 1).astype(F32)
    y = iota((rows, nz), 0) + (place * size - EDGE)
    inside = (y >= 0) & (y < ny)
    first, last = layer == 0.0, layer == nz - 1.0
    zero = jnp.zeros((rows, nz), F32)
    state = [None] * (nx + 2)
    for p in range(nx + 2):
        comps = []
        for comp in range(ncomp):
            if p == 0:
                w = part(below, ncomp + comp) + 0.12 * edge_ref[comp].astype(F32)
            elif p == nx + 1:
                w = part(above, ncomp + comp) + 0.12 * edge_ref[ncomp + comp].astype(F32)
            else:
                w = wind_ref[comp * nx + p - 1]
                if p == 1:
                    w = w + 0.12 * part(below, comp)
                if p == nx:
                    w = w + 0.12 * part(above, comp)
            comps.append(w)
        gu, gv, gw = comps
        speed = jnp.sqrt(gu * gu + gv * gv)
        rise = jnp.broadcast_to(table[:, lifted[p] : lifted[p] + 1], (rows, nz))
        base = jnp.broadcast_to(table[:, ground[p] : ground[p] + 1], (rows, nz))
        lift = jnp.where(layer == rise, 0.5 * jnp.maximum(speed - 1.0, 0.0), 0.0)
        keep = (layer >= base) & inside
        if p == 0:
            keep = keep & (column > 0)
        if p == nx + 1:
            keep = keep & (column < nhoriz - 1)
        coef = [
            (0.15 * (0.1 - jnp.minimum(a, 0.0)), 0.15 * (0.1 + jnp.maximum(a, 0.0)))
            for a in (gu, gv, gw - 0.5)
        ]
        state[p] = (coef, lift, keep)

    def step(p, c, behind, ahead):
        coef, lift, keep = state[p]
        total = c + lift
        pairs = (
            (ahead, behind),
            (pltpu.roll(c, rows - 1, 0), pltpu.roll(c, 1, 0)),
            (
                jnp.where(last, zero, pltpu.roll(c, nz - 1, 1)),
                jnp.where(first, zero, pltpu.roll(c, 1, 1)),
            ),
        )
        for (forward, back), (post, prev) in zip(coef, pairs):
            total = total + forward * (post - c) - back * (c - prev)
        return jnp.where(keep, total, 0.0)

    once = [step(p, conc[p + 1], conc[p], conc[p + 2]) for p in range(nx + 2)]
    for x in range(nx):
        twice = step(x + 1, once[x + 1], once[x], once[x + 2])
        out_ref[x] = twice[EDGE : EDGE + size]


def local(velocity, dust, eligible, terrain):
    ncomp, nx, ny, nz = velocity.shape
    size = dust.shape[1]
    nh, nv = (lax.axis_size("horiz"), lax.axis_size("vert"))
    rows = size + 2 * EDGE
    rise = [(i, i + 1) for i in range(nv - 1)]
    fall = [(j, i) for i, j in rise]
    near_pairs = [p for i in range(0, nh - 1, 2) for p in ((i, i + 1), (i + 1, i))]
    far_pairs = [p for i in range(1, nh - 1, 2) for p in ((i, i + 1), (i + 1, i))]
    nplane = ncomp * nx
    anywhere = pl.BlockSpec(memory_space=pl.ANY)

    strips = call(
        functools.partial(pack_strips, size),
        [shaped(nplane * size + 64, LANES)] * nv,
        "pack_strips",
        [
            pltpu.VMEM((ncomp, nx, ny, nz), F32),
            pltpu.VMEM((nv, 64, LANES), F32),
            pltpu.SemaphoreType.DMA((ncomp,)),
        ],
        in_specs=[anywhere],
        out_specs=[VMEM] * nv,
    )(pltpu.with_memory_space_constraint(velocity, pltpu.HBM))
    got = [strips[0]] + [lax.ppermute(strips[t], "vert", [(0, t)]) for t in range(1, nv)]

    face = ny // LANES * 16
    zm, zp, lay = call(
        functools.partial(pack_ends, size),
        [shaped(face + nx * EDGE + 32, LANES)] * 2 + [shaped(nv, 16, LANES)],
        "pack_ends",
        [pltpu.VMEM((16, ny), F32)] * 2,
        in_specs=[VMEM] * 3 + [anywhere],
    )(velocity, dust, terrain, strips[-1])
    rm = lax.ppermute(zm, "vert", fall)
    rp = lax.ppermute(zp, "vert", rise)
    lays = [lay] + [lax.ppermute(lay[t], "vert", [(1, t)]) for t in range(3, nv)]

    far, near = call(pack_sides, [shaped(ncomp, ny, nz)] * 2, "pack_sides", in_specs=[VMEM, anywhere])(
        velocity, rm
    )
    far = lax.ppermute(far, "horiz", far_pairs)
    near = lax.ppermute(near, "horiz", near_pairs)

    velocity_next = call(
        advance,
        jax.ShapeDtypeStruct(velocity.shape, F32),
        "advance",
        [pltpu.VMEM((ncomp, nx, ny, nz), F32), pltpu.SemaphoreType.DMA((ncomp,))],
        in_specs=[VMEM] * 5,
        out_specs=anywhere,
    )(velocity, far, near, rm, rp)

    wire = (2 * ncomp + 2) * rows + 16
    wind, conc, cols, mf, mn, edge = call(
        functools.partial(prepare, nv),
        [
            shaped(nplane, rows, LANES, dtype=F32),
            shaped(nx, rows, LANES, dtype=F32),
            shaped(16, LANES, dtype=F32),
            shaped(wire, LANES),
            shaped(wire, LANES),
            shaped(2 * ncomp, rows, LANES),
        ],
        "prepare",
        [pltpu.VMEM((nplane, rows, LANES), F32)],
    )(*got, *lays, dust, terrain, eligible, rm, rp)
    mf = lax.ppermute(mf, "horiz", far_pairs)
    mn = lax.ppermute(mn, "horiz", near_pairs)
    dust_next = call(
        functools.partial(transport, ny, nh),
        jax.ShapeDtypeStruct(dust.shape, F32),
        "transport",
    )(wind, edge, conc, cols, mf, mn)
    return (velocity_next, dust_next)


def solution(mesh):
    placed = (
        P(None, "horiz", None, "vert"),
        P("horiz", "vert", None),
        P("horiz", None),
        P("horiz", "vert"),
    )
    return jax.shard_map(
        local,
        mesh=mesh,
        in_specs=placed,
        out_specs=(P(None, "horiz", None, "vert"), P("horiz", "vert", None)),
        check_vma=False,
    )
```

time: 44.1 us -> 37.2 us (0.84)
  the two profiles are of different devices: /device:TPU:11 before, /device:TPU:20 now
where the time goes in v2:
time: 37.2 us; the launch traced here: 36.9 us
  starting transfers between devices  16.3 us (44%)
  waiting for transfers between devices  11.9 us (32%)
  Pallas kernels  6.22 us (17%)
  local copies, waits for them, and re-layouts  1.76 us (5%)
  between operations  0.76 us (2%)
    ppermute x3, waiting for transfers between devices, local(): lax.ppermute(strips[t], 'vert', [(0, t)])  9.06 us
    ppermute x1, starting transfers between devices, local(): rp = lax.ppermute(zp, 'vert', rise)  3.48 us
    ppermute x1, waiting for transfers between devices, local(): mf = lax.ppermute(mf, 'horiz', far_pairs)  2.82 us
    ppermute x3, starting transfers between devices, local(): lax.ppermute(strips[t], 'vert', [(0, t)])  2.64 us
    ppermute x1, starting transfers between devices, local(): rm = lax.ppermute(zm, 'vert', fall)  2.36 us
    ppermute x1, starting transfers between devices, local(): far = lax.ppermute(far, 'horiz', far_pairs)  2.21 us
    pallas_call x1, Pallas kernels, local(): call(advance, jax.ShapeDtypeStruct(velocity.shape, F32), 'advance', [pltp...  2.06 us
    ppermute x1, starting transfers between devices, local(): mf = lax.ppermute(mf, 'horiz', far_pairs)  1.92 us
  transfers between devices with their start and end apart: 10, of which 2 were waited for; matrix products, arithmetic and copies ran while one was open for 0% of the time, Pallas kernels for 11%

profile of v2, /device:TPU:20, one launch (start us, length us, event | category | flops | bytes accessed | tf_op | source)
XLA Modules:
  0.0 36.9 jit_solution(16045345911976863623)
XLA Ops:
  0.6 0.0 copy-start
  0.6 0.7 %pack_strips.1 = (bf16[832,128]{1,0:T(8,128)(2,1)S(1)}, bf16[832,128]{1,0:T(8,128)(2,1)}, bf16[832,128]{1,0:T(8,128)(2,1)S(1)}, bf16[832,128]{1,0:T(8,128)(2,1)S(1)}) custom-call(f32[3,4,256,128]{3,2,1,0:T(8,128)} %v_ref.7), custom_call_target="tpu_custom_call" | custom-call | flops 1048576 | bytes 1048576 | tf_op jit(solution)/shard_map/pack_strips/pallas_call | solution.py:361
  1.4 0.7 %collective-permute-start.6 = (bf16[832,128]{1,0:T(8,128)(2,1)S(1)}, bf16[832,128]{1,0:T(8,128)(2,1)S(1)}, u32[]{:S(2)}, u32[]{:S(2)}) collective-permute-start(bf16[832,128]{1,0:T(8,128)(2,1)S(1)} %get-tuple-element.17.strip_ref), channel_id=1, source_target_pairs={{0,3},{4,7},{8,11},{12,15},{16,19},{20,23},{24,27},{28,31}} | collective-permute-start | bytes 638984 | tf_op jit(solution)/shard_map/ppermute | solution.py:373
  2.1 0.1 copy-done
  2.1 0.0 copy-start.1
  2.1 0.9 %copy-done.1 = f32[4,64,128]{2,1,0:T(8,128)S(1)} copy-done((f32[4,64,128]{2,1,0:T(8,128)S(1)}, f32[4,64,128]{2,1,0:T(8,128)}, u32[]{:S(2)}) %copy-start.1) | copy-done | bytes 131096
  3.0 0.0 copy-start.3
  3.0 0.7 %copy-done.3 = s32[4,64]{1,0:T(4,128)S(1)} copy-done((s32[4,64]{1,0:T(4,128)S(1)}, s32[4,64]{1,0:T(4,128)}, u32[]{:S(2)}) %copy-start.3) | copy-done | bytes 1048
  3.7 0.0 copy-start.5
  3.7 0.0 copy-start.2
  3.7 0.0 copy-start.4
  3.7 0.6 %pack_ends.1 = (bf16[96,128]{1,0:T(8,128)(2,1)S(1)}, bf16[96,128]{1,0:T(8,128)(2,1)S(1)}, bf16[4,16,128]{2,1,0:T(8,128)(2,1)S(1)}) custom-call(f32[3,4,256,128]{3,2,1,0:T(8,128)S(1)} %copy-done, f32[4,64,128]{2,1,0:T(8,128)S(1)} %copy-done.1, s32[4,64]{1,0:T(4,128)S(1)} %copy-done.3, bf16[832,128]{1,0:T(8,128)(2,1)S(1)} %get-tuple-element.17.strip_ref), custom_call_target="tpu_custom_call" | custom-call | flops 1048576 | bytes 1048576 | tf_op jit(solution)/shard_map/pack_ends/pallas_call | solution.py:376
  4.3 2.4 %collective-permute-start = (bf16[96,128]{1,0:T(8,128)(2,1)S(1)}, bf16[96,128]{1,0:T(8,128)(2,1)S(1)}, u32[]{:S(2)}, u32[]{:S(2)}) collective-permute-start(bf16[96,128]{1,0:T(8,128)(2,1)S(1)} %get-tuple-element.18), channel_id=1, source_target_pairs={{1,0},{2,1},{3,2},{5,4},{6,5},{7,6},{9,8},{10,9},{11,10},{13,12},{... | collective-permute-start | bytes 73736 | tf_op jit(solution)/shard_map/ppermute | solution.py:383
  6.7 3.5 %collective-permute-start.3 = (bf16[96,128]{1,0:T(8,128)(2,1)S(1)}, bf16[96,128]{1,0:T(8,128)(2,1)S(1)}, u32[]{:S(2)}, u32[]{:S(2)}) collective-permute-start(bf16[96,128]{1,0:T(8,128)(2,1)S(1)} %get-tuple-element.21), channel_id=1, source_target_pairs={{0,1},{1,2},{2,3},{4,5},{5,6},{6,7},{8,9},{9,10},{10,11},{12,13},{... | collective-permute-start | bytes 73736 | tf_op jit(solution)/shard_map/ppermute | solution.py:384
  10.2 0.7 %collective-permute-start.4 = (bf16[832,128]{1,0:T(8,128)(2,1)}, bf16[832,128]{1,0:T(8,128)(2,1)S(1)}, u32[]{:S(2)}, u32[]{:S(2)}) collective-permute-start(bf16[832,128]{1,0:T(8,128)(2,1)} %get-tuple-element.23), channel_id=1, source_target_pairs={{0,1},{4,5},{8,9},{12,13},{16,17},{20,21},{24,25},{28,29}} | collective-permute-start | bytes 638984 | tf_op jit(solution)/shard_map/ppermute | solution.py:373
  10.8 1.3 %collective-permute-start.5 = (bf16[832,128]{1,0:T(8,128)(2,1)S(1)}, bf16[832,128]{1,0:T(8,128)(2,1)S(1)}, u32[]{:S(2)}, u32[]{:S(2)}) collective-permute-start(bf16[832,128]{1,0:T(8,128)(2,1)S(1)} %get-tuple-element.24), channel_id=1, source_target_pairs={{0,2},{4,6},{8,10},{12,14},{16,18},{20,22},{24,26},{28,30}} | collective-permute-start | bytes 638984 | tf_op jit(solution)/shard_map/ppermute | solution.py:373
  12.2 0.0 collective-permute-done.rm_ref.refs_9_
  12.2 0.7 %collective-permute-start.7 = (bf16[16,128]{1,0:T(8,128)(2,1)S(1)}, bf16[16,128]{1,0:T(8,128)(2,1)S(1)}, u32[]{:S(2)}, u32[]{:S(2)}) collective-permute-start(bf16[16,128]{1,0:T(8,128)(2,1)S(1)} %slice_bitcast_fusion), channel_id=1, source_target_pairs={{1,3},{5,7},{9,11},{13,15},{17,19},{21,23},{25,27},{29,31}} | collective-permute-start | bytes 12296 | tf_op jit(solution)/shard_map/ppermute | solution.py:385
  12.8 0.8 %pack_sides.1 = (bf16[3,256,128]{2,1,0:T(8,128)(2,1)}, bf16[3,256,128]{2,1,0:T(8,128)(2,1)}) custom-call(f32[3,4,256,128]{3,2,1,0:T(8,128)S(1)} %copy-done, bf16[96,128]{1,0:T(8,128)(2,1)S(1)} %collective-permute-done.rm_ref.refs_9_), custom_call_target="tpu_custom_call" | custom-call | flops 1048576 | bytes 1048576 | tf_op jit(solution)/shard_map/pack_sides/pallas_call | solution.py:387
  13.6 0.0 collective-permute-done.7.refs_5_
  13.6 2.2 %collective-permute-start.1 = (bf16[3,256,128]{2,1,0:T(8,128)(2,1)}, bf16[3,256,128]{2,1,0:T(8,128)(2,1)S(1)}, u32[]{:S(2)}, u32[]{:S(2)}) collective-permute-start(bf16[3,256,128]{2,1,0:T(8,128)(2,1)} %get-tuple-element.19), channel_id=1, source_target_pairs={{4,8},{8,4},{12,16},{16,12},{20,24},{24,20},{5,9},{9,5},{13,17},{1... | collective-permute-start | bytes 589832 | tf_op jit(solution)/shard_map/ppermute | solution.py:390
  15.9 0.0 collective-permute-done.3.rp_ref.refs_10_
  15.9 1.4 %collective-permute-start.2 = (bf16[3,256,128]{2,1,0:T(8,128)(2,1)}, bf16[3,256,128]{2,1,0:T(8,128)(2,1)S(1)}, u32[]{:S(2)}, u32[]{:S(2)}) collective-permute-start(bf16[3,256,128]{2,1,0:T(8,128)(2,1)} %get-tuple-element.20), channel_id=1, source_target_pairs={{0,4},{4,0},{8,12},{12,8},{16,20},{20,16},{24,28},{28,24},{1,5},{5... | collective-permute-start | bytes 589832 | tf_op jit(solution)/shard_map/ppermute | solution.py:391
  17.2 0.0 copy-done.5
  17.2 0.1 copy.6.refs_8_
  17.3 0.0 collective-permute-done.4.refs_1_
  17.3 9.1 %collective-permute-done.5.refs_2_ = bf16[832,128]{1,0:T(8,128)(2,1)S(1)} collective-permute-done((bf16[832,128]{1,0:T(8,128)(2,1)S(1)}, bf16[832,128]{1,0:T(8,128)(2,1)S(1)}, u32[]{:S(2)}, u32[]{:S(2)}) %collective-permute-start.5) | collective-permute-done | bytes 213024 | tf_op jit(solution)/shard_map/ppermute | solution.py:373
  26.4 0.0 collective-permute-done.6.refs_3_
  26.4 0.0 copy-done.2
  26.4 0.0 copy-done.4
  26.4 0.6 %prepare.1 = (f32[12,80,128]{2,1,0:T(8,128)S(1)}, f32[4,80,128]{2,1,0:T(8,128)S(1)}, f32[16,128]{1,0:T(8,128)S(1)}, bf16[656,128]{1,0:T(8,128)(2,1)S(1)}, bf16[6...) custom-call(bf16[832,128]{1,0:T(8,128)(2,1)S(1)} %get-tuple-element.22.refs_0_, ...), custom_call_target="tpu_custom_call" | custom-call | flops 1048576 | bytes 1048576 | tf_op jit(solution)/shard_map/prepare/pallas_call | solution.py:403
  27.0 1.9 %collective-permute-start.8 = (bf16[656,128]{1,0:T(8,128)(2,1)S(1)}, bf16[656,128]{1,0:T(8,128)(2,1)S(1)}, u32[]{:S(2)}, u32[]{:S(2)}) collective-permute-start(bf16[656,128]{1,0:T(8,128)(2,1)S(1)} %get-tuple-element.30), channel_id=1, source_target_pairs={{4,8},{8,4},{12,16},{16,12},{20,24},{24,20},{5,9},{9,5},{13,17},{1... | collective-permute-start | bytes 503816 | tf_op jit(solution)/shard_map/ppermute | solution.py:416
  28.9 1.7 %collective-permute-start.9 = (bf16[656,128]{1,0:T(8,128)(2,1)S(1)}, bf16[656,128]{1,0:T(8,128)(2,1)S(1)}, u32[]{:S(2)}, u32[]{:S(2)}) collective-permute-start(bf16[656,128]{1,0:T(8,128)(2,1)S(1)} %get-tuple-element.31), channel_id=1, source_target_pairs={{0,4},{4,0},{8,12},{12,8},{16,20},{20,16},{24,28},{28,24},{1,5},{5... | collective-permute-start | bytes 503816 | tf_op jit(solution)/shard_map/ppermute | solution.py:417
  30.5 0.0 collective-permute-done.1.far_ref
  30.5 0.0 collective-permute-done.2.near_ref
  30.5 2.1 %advance.1 = f32[3,4,256,128]{3,2,1,0:T(8,128)} custom-call(f32[3,4,256,128]{3,2,1,0:T(8,128)S(1)} %copy-done, bf16[3,256,128]{2,1,0:T(8,128)(2,1)S(1)} %collective-permute-done.1.far_ref, bf16[3,256,128]{2,1,0:T(8,128)(2,1)S(1)} %collective-permute-done.2.near_ref, bf16[96,128]{1,0:T(8,128)(2,1)S(1)} %collective-permute-done.rm_ref.refs_9_, ...), custom_call_target="tpu_custom_call" | custom-call | flops 1048576 | bytes 1048576 | tf_op jit(solution)/shard_map/advance/pallas_call | solution.py:393
  32.6 2.8 %collective-permute-done.8.far_ref = bf16[656,128]{1,0:T(8,128)(2,1)S(1)} collective-permute-done((bf16[656,128]{1,0:T(8,128)(2,1)S(1)}, bf16[656,128]{1,0:T(8,128)(2,1)S(1)}, u32[]{:S(2)}, u32[]{:S(2)}) %collective-permute-start.8) | collective-permute-done | bytes 167968 | tf_op jit(solution)/shard_map/ppermute | solution.py:416
  35.4 0.0 collective-permute-done.9.near_ref
  35.4 1.5 %transport.1 = f32[4,64,128]{2,1,0:T(8,128)} custom-call(f32[12,80,128]{2,1,0:T(8,128)S(1)} %get-tuple-element.26.wind_ref, bf16[6,80,128]{2,1,0:T(8,128)(2,1)S(1)} %get-tuple-element.27.edge_ref, f32[4,80,128]{2,1,0:T(8,128)S(1)} %get-tuple-element.28.conc_ref, f32[16,128]{1,0:T(8,128)S(1)} %get-tuple-element.29.cols_ref, ...), custom_call_target="tpu_custom_call" | custom-call | flops 1048576 | bytes 1048576 | tf_op jit(solution)/shard_map/transport/pallas_call | solution.py:418
  (1 shorter events, 0.0 us)
Async XLA Ops:
  0.6 1.5 %copy-start = (f32[3,4,256,128]{3,2,1,0:T(8,128)S(1)}, f32[3,4,256,128]{3,2,1,0:T(8,128)}, u32[]{:S(2)}) copy-start(f32[3,4,256,128]{3,2,1,0:T(8,128)} %v_ref.7) | copy-start | bytes 4718596
  1.4 25.0 %collective-permute-start.6 = (bf16[832,128]{1,0:T(8,128)(2,1)S(1)}, bf16[832,128]{1,0:T(8,128)(2,1)S(1)}, u32[]{:S(2)}, u32[]{:S(2)}) collective-permute-start(bf16[832,128]{1,0:T(8,128)(2,1)S(1)} %get-tuple-element.17.strip_ref), channel_id=1, source_target_pairs={{0,3},{4,7},{8,11},{12,15},{16,19},{20,23},{24,27},{28,31}} | collective-permute-start | bytes 638984 | tf_op jit(solution)/shard_map/ppermute | solution.py:373
  2.1 0.9 %copy-start.1 = (f32[4,64,128]{2,1,0:T(8,128)S(1)}, f32[4,64,128]{2,1,0:T(8,128)}, u32[]{:S(2)}) copy-start(f32[4,64,128]{2,1,0:T(8,128)} %refs_6_.1) | copy-start | bytes 393220
  3.0 0.7 %copy-start.3 = (s32[4,64]{1,0:T(4,128)S(1)}, s32[4,64]{1,0:T(4,128)}, u32[]{:S(2)}) copy-start(s32[4,64]{1,0:T(4,128)} %refs_7_.1) | copy-start | bytes 3076
  3.7 13.5 %copy-start.5 = (s32[4,2]{0,1:T(2,128)S(1)}, s32[4,2]{0,1:T(2,128)}, u32[]{:S(2)}) copy-start(s32[4,2]{0,1:T(2,128)} %param.6) | copy-start | bytes 100
  3.7 22.7 %copy-start.2 = (f32[4,64,128]{2,1,0:T(8,128)S(1)}, f32[4,64,128]{2,1,0:T(8,128)}, u32[]{:S(2)}) copy-start(f32[4,64,128]{2,1,0:T(8,128)} %refs_6_.1) | copy-start | bytes 393220
  3.7 22.7 %copy-start.4 = (s32[4,64]{1,0:T(4,128)S(1)}, s32[4,64]{1,0:T(4,128)}, u32[]{:S(2)}) copy-start(s32[4,64]{1,0:T(4,128)} %refs_7_.1) | copy-start | bytes 3076
  4.3 7.9 %collective-permute-start = (bf16[96,128]{1,0:T(8,128)(2,1)S(1)}, bf16[96,128]{1,0:T(8,128)(2,1)S(1)}, u32[]{:S(2)}, u32[]{:S(2)}) collective-permute-start(bf16[96,128]{1,0:T(8,128)(2,1)S(1)} %get-tuple-element.18), channel_id=1, source_target_pairs={{1,0},{2,1},{3,2},{5,4},{6,5},{7,6},{9,8},{10,9},{11,10},{13,12},{... | collective-permute-start | bytes 73736 | tf_op jit(solution)/shard_map/ppermute | solution.py:383
  6.7 9.2 %collective-permute-start.3 = (bf16[96,128]{1,0:T(8,128)(2,1)S(1)}, bf16[96,128]{1,0:T(8,128)(2,1)S(1)}, u32[]{:S(2)}, u32[]{:S(2)}) collective-permute-start(bf16[96,128]{1,0:T(8,128)(2,1)S(1)} %get-tuple-element.21), channel_id=1, source_target_pairs={{0,1},{1,2},{2,3},{4,5},{5,6},{6,7},{8,9},{9,10},{10,11},{12,13},{... | collective-permute-start | bytes 73736 | tf_op jit(solution)/shard_map/ppermute | solution.py:384
  10.2 7.2 %collective-permute-start.4 = (bf16[832,128]{1,0:T(8,128)(2,1)}, bf16[832,128]{1,0:T(8,128)(2,1)S(1)}, u32[]{:S(2)}, u32[]{:S(2)}) collective-permute-start(bf16[832,128]{1,0:T(8,128)(2,1)} %get-tuple-element.23), channel_id=1, source_target_pairs={{0,1},{4,5},{8,9},{12,13},{16,17},{20,21},{24,25},{28,29}} | collective-permute-start | bytes 638984 | tf_op jit(solution)/shard_map/ppermute | solution.py:373
  10.8 15.5 %collective-permute-start.5 = (bf16[832,128]{1,0:T(8,128)(2,1)S(1)}, bf16[832,128]{1,0:T(8,128)(2,1)S(1)}, u32[]{:S(2)}, u32[]{:S(2)}) collective-permute-start(bf16[832,128]{1,0:T(8,128)(2,1)S(1)} %get-tuple-element.24), channel_id=1, source_target_pairs={{0,2},{4,6},{8,10},{12,14},{16,18},{20,22},{24,26},{28,30}} | collective-permute-start | bytes 638984 | tf_op jit(solution)/shard_map/ppermute | solution.py:373
  12.2 1.5 %collective-permute-start.7 = (bf16[16,128]{1,0:T(8,128)(2,1)S(1)}, bf16[16,128]{1,0:T(8,128)(2,1)S(1)}, u32[]{:S(2)}, u32[]{:S(2)}) collective-permute-start(bf16[16,128]{1,0:T(8,128)(2,1)S(1)} %slice_bitcast_fusion), channel_id=1, source_target_pairs={{1,3},{5,7},{9,11},{13,15},{17,19},{21,23},{25,27},{29,31}} | collective-permute-start | bytes 12296 | tf_op jit(solution)/shard_map/ppermute | solution.py:385
  13.6 16.9 %collective-permute-start.1 = (bf16[3,256,128]{2,1,0:T(8,128)(2,1)}, bf16[3,256,128]{2,1,0:T(8,128)(2,1)S(1)}, u32[]{:S(2)}, u32[]{:S(2)}) collective-permute-start(bf16[3,256,128]{2,1,0:T(8,128)(2,1)} %get-tuple-element.19), channel_id=1, source_target_pairs={{4,8},{8,4},{12,16},{16,12},{20,24},{24,20},{5,9},{9,5},{13,17},{1... | collective-permute-start | bytes 589832 | tf_op jit(solution)/shard_map/ppermute | solution.py:390
  15.9 14.7 %collective-permute-start.2 = (bf16[3,256,128]{2,1,0:T(8,128)(2,1)}, bf16[3,256,128]{2,1,0:T(8,128)(2,1)S(1)}, u32[]{:S(2)}, u32[]{:S(2)}) collective-permute-start(bf16[3,256,128]{2,1,0:T(8,128)(2,1)} %get-tuple-element.20), channel_id=1, source_target_pairs={{0,4},{4,0},{8,12},{12,8},{16,20},{20,16},{24,28},{28,24},{1,5},{5... | collective-permute-start | bytes 589832 | tf_op jit(solution)/shard_map/ppermute | solution.py:391
  27.0 8.5 %collective-permute-start.8 = (bf16[656,128]{1,0:T(8,128)(2,1)S(1)}, bf16[656,128]{1,0:T(8,128)(2,1)S(1)}, u32[]{:S(2)}, u32[]{:S(2)}) collective-permute-start(bf16[656,128]{1,0:T(8,128)(2,1)S(1)} %get-tuple-element.30), channel_id=1, source_target_pairs={{4,8},{8,4},{12,16},{16,12},{20,24},{24,20},{5,9},{9,5},{13,17},{1... | collective-permute-start | bytes 503816 | tf_op jit(solution)/shard_map/ppermute | solution.py:416
  28.9 6.6 %collective-permute-start.9 = (bf16[656,128]{1,0:T(8,128)(2,1)S(1)}, bf16[656,128]{1,0:T(8,128)(2,1)S(1)}, u32[]{:S(2)}, u32[]{:S(2)}) collective-permute-start(bf16[656,128]{1,0:T(8,128)(2,1)S(1)} %get-tuple-element.31), channel_id=1, source_target_pairs={{0,4},{4,0},{8,12},{12,8},{16,20},{20,16},{24,28},{28,24},{1,5},{5... | collective-permute-start | bytes 503816 | tf_op jit(solution)/shard_map/ppermute | solution.py:417

commit v3 on v2

--- a/solution.py
+++ b/solution.py
@@ -42,7 +42,7 @@
     return jnp.where(hit, 1.0, 0.0).astype(BF)
 
 
-def pack_strips(size, v_ref, *refs):
+def pack_low(size, v_ref, *refs):
     outs, (buf, side, sems) = (refs[:-3], refs[-3:])
     ncomp, nx, ny, nz = v_ref.shape
 
@@ -65,12 +65,28 @@
             out[ncomp * nx * size :] = side[t].astype(BF)
 
 
+def gate(*refs):
+    del refs
+
+
+def turn_faces(v_ref, comp, ends, outs):
+    _, nx, ny, _ = v_ref.shape
+    for x in range(nx):
+        j = comp * nx + x
+        for half in range(ny // LANES):
+            span = slice(half * LANES, (half + 1) * LANES)
+            block = v_ref[comp, x, span, :].astype(BF)
+            rows = lax.dot_general(ends, block, (((1,), (1,)), ((), ())), preferred_element_type=F32)
+            for i, out in enumerate(outs):
+                out[j : j + 1, span] = rows[i : i + 1]
+
+
 def halo_rows(start, size):
     return (start - 2, start - 1, start + size, start + size + 1)
 
 
-def pack_sides(v_ref, rm_ref, far_ref, near_ref):
-    del rm_ref
+def pack_sides(v_ref, after_ref, far_ref, near_ref):
+    del after_ref
     nx = v_ref.shape[1]
     odd = lax.rem(lax.axis_index("horiz"), 2) == 1
 
@@ -85,57 +101,75 @@
         far_ref[...] = v_ref[:, 0].astype(BF)
 
 
-def pack_ends(size, v_ref, dust_ref, terrain_ref, strip_ref, zm_ref, zp_ref, lay_ref, low, high):
-    del strip_ref
+def pack_ends(size, nstrips, v_ref, dust_ref, terrain_ref, after_ref, first_ref, second_ref, mine_ref, *refs):
+    del after_ref
+    lays, (low, high, dusts, land, sems) = (refs[:-5], refs[-5:])
     ncomp, nx, ny, nz = v_ref.shape
-    ends = pick((16, nz), [(0, 0), (1, nz - 1)])
+    odd = lax.rem(lax.axis_index("vert"), 2) == 1
+    copies = [
+        pltpu.make_async_copy(dust_ref.at[:, :EDGE], dusts.at[0], sems.at[0]),
+        pltpu.make_async_copy(dust_ref.at[:, size - EDGE :], dusts.at[1], sems.at[1]),
+        pltpu.make_async_copy(terrain_ref, land, sems.at[2]),
+    ]
+    for copy in copies:
+        copy.start()
     low[...] = jnp.zeros_like(low)
     high[...] = jnp.zeros_like(high)
-    nb = ny // LANES
-    for j in range(ncomp * nx):
-        for half in range(nb):
-            block = v_ref[j // nx, j % nx, half * LANES : (half + 1) * LANES, :].astype(BF)
-            both = lax.dot_general(ends, block, (((1,), (1,)), ((), ())), preferred_element_type=F32)
-            low[j : j + 1, half * LANES : (half + 1) * LANES] = both[0:1]
-            high[j : j + 1, half * LANES : (half + 1) * LANES] = both[1:2]
-    terrain = terrain_ref[...].astype(F32)
-    terrain = jnp.concatenate([terrain, jnp.zeros((nx, LANES - size), F32)], 1)
-    terrain = jnp.concatenate([terrain, jnp.zeros((16 - nx, LANES), F32)], 0)
+    ends = pick((16, nz), [(0, 0), (1, nz - 1)])
+    for comp in range(ncomp):
+        turn_faces(v_ref, comp, ends, [low, high])
     lane = iota((16, LANES), 1)
     whole = low[...]
-    for t in range(lay_ref.shape[0]):
+    for t in range(nstrips):
         shift = (EDGE - t * size) % ny
         moved = pltpu.roll(whole, shift, 1) if shift else whole
         row = lane + (t * size - EDGE)
-        lay_ref[t] = jnp.where((row >= 0) & (row < ny), moved[:, :LANES], 0.0).astype(BF)
-    for half in range(nb):
-        zm_ref[half * 16 : half * 16 + 16] = low[:, half * LANES : (half + 1) * LANES].astype(BF)
-        zp_ref[half * 16 : half * 16 + 16] = high[:, half * LANES : (half + 1) * LANES].astype(BF)
-    at = nb * 16
-    zm_ref[at : at + nx * EDGE] = dust_ref[:, :EDGE].reshape(nx * EDGE, LANES).astype(BF)
-    zp_ref[at : at + nx * EDGE] = dust_ref[:, size - EDGE :].reshape(nx * EDGE, LANES).astype(BF)
-    at = at + nx * EDGE
-    zm_ref[at : at + 16] = terrain.astype(BF)
-    zp_ref[at : at + 16] = terrain.astype(BF)
-    zm_ref[at + 16 : at + 32] = lay_ref[0]
-    zp_ref[at + 16 : at + 32] = lay_ref[min(2, lay_ref.shape[0] - 1)]
-
-
-def advance(v_ref, far_ref, near_ref, rm_ref, rp_ref, out_ref, buf, sems):
+        part = jnp.where((row >= 0) & (row < ny), moved[:, :LANES], 0.0).astype(BF)
+        if t < 3:
+            mine_ref[t] = part
+        else:
+            lays[t - 3][...] = part
+    for copy in copies:
+        copy.wait()
+    terrain = land[...].astype(F32)
+    terrain = jnp.concatenate([terrain, jnp.zeros((nx, LANES - size), F32)], 1)
+    terrain = jnp.concatenate([terrain, jnp.zeros((16 - nx, LANES), F32)], 0)
+
+    def send(ref, face, which, layer):
+        for half in range(ny // LANES):
+            ref[half * 16 : half * 16 + 16] = face[:, half * LANES : (half + 1) * LANES].astype(BF)
+        at = ny // LANES * 16
+        ref[at : at + nx * EDGE] = dusts[which].reshape(nx * EDGE, LANES).astype(BF)
+        at = at + nx * EDGE
+        ref[at : at + 16] = terrain.astype(BF)
+        ref[at + 16 : at + 32] = mine_ref[layer]
+
+    @pl.when(odd)
+    def _():
+        send(first_ref, low, 0, 0)
+        send(second_ref, high, 1, 2)
+
+    @pl.when(jnp.logical_not(odd))
+    def _():
+        send(first_ref, high, 1, 2)
+        send(second_ref, low, 0, 0)
+
+
+def sorted_ends(first_ref, second_ref, start, n):
+    odd = lax.rem(lax.axis_index("vert"), 2) == 1
+    first, second = (first_ref[start : start + n].astype(F32), second_ref[start : start + n].astype(F32))
+    return (jnp.where(odd, second, first), jnp.where(odd, first, second))
+
+
+def advance(v_ref, far_ref, near_ref, first_ref, second_ref, out_ref, buf, sems):
     ncomp, nx, ny, nz = v_ref.shape
     odd = lax.rem(lax.axis_index("horiz"), 2) == 1
     row, lane = iota((LANES, nz), 0), iota((LANES, nz), 1)
     nb = ny // LANES
     turned = []
     for half in range(nb):
-        faces = jnp.concatenate(
-            [
-                rm_ref[half * 16 : half * 16 + 16].astype(F32),
-                rp_ref[half * 16 : half * 16 + 16].astype(F32),
-                jnp.zeros((LANES - 32, LANES), F32),
-            ],
-            0,
-        )
+        over, under = sorted_ends(first_ref, second_ref, half * 16, 16)
+        faces = jnp.concatenate([over, under, jnp.zeros((LANES - 32, LANES), F32)], 0)
         turned.append(faces.T.astype(BF))
     copies = []
     for comp in range(ncomp):
@@ -168,9 +202,9 @@
 
 def prepare(nstrips, *refs):
     strips = refs[:nstrips]
-    nlay = max(nstrips - 2, 1)
+    nlay = 1 + max(nstrips - 3, 0)
     lays = refs[nstrips : nstrips + nlay]
-    dust_ref, terrain_ref, eligible_ref, rm_ref, rp_ref = refs[nstrips + nlay : nstrips + nlay + 5]
+    dust_ref, terrain_ref, eligible_ref, first_ref, second_ref = refs[nstrips + nlay : nstrips + nlay + 5]
     wind_ref, conc_ref, cols_ref, far_ref, near_ref, edge_ref, frame = refs[nstrips + nlay + 5 :]
     nx, size, nz = dust_ref.shape
     nplane = frame.shape[0]
@@ -189,12 +223,12 @@
                 for i, y in enumerate(halo_rows(EDGE, size)):
                     frame[j, y : y + 1] = beside[i * 16 + j : i * 16 + j + 1]
 
-    face = rm_ref.shape[0] - 32 - nx * EDGE
-    last = face + nx * EDGE + 16
+    face = first_ref.shape[0] - 32 - nx * EDGE
+    over, under = sorted_ends(first_ref, second_ref, face, nx * EDGE + 32)
     zero = jnp.zeros((16, LANES), F32)
-    layer = jnp.where(place == 0, rm_ref[last : last + 16].astype(F32), zero)
+    layer = jnp.where(place == 0, over[nx * EDGE + 16 :], zero)
     layer = layer + jnp.where(place == 1, lays[0][min(1, nstrips - 1)].astype(F32), zero)
-    layer = layer + jnp.where(place == 2, rp_ref[last : last + 16].astype(F32), zero)
+    layer = layer + jnp.where(place == 2, under[nx * EDGE + 16 :], zero)
     for got in lays[1:]:
         layer = layer + got[...].astype(F32)
     layer = jnp.concatenate([layer, jnp.zeros((LANES - 16, LANES), F32)], 0)
@@ -222,15 +256,14 @@
             if x == nx - 1:
                 edge_ref[ncomp + comp] = raw
     for x in range(nx):
-        before = rp_ref[face + x * EDGE : face + (x + 1) * EDGE].astype(F32)
-        after = rm_ref[face + x * EDGE : face + (x + 1) * EDGE].astype(F32)
+        before, after = (under[x * EDGE : (x + 1) * EDGE], over[x * EDGE : (x + 1) * EDGE])
         conc_ref[x] = jnp.concatenate([before, dust_ref[x], after], 0)
     lane = iota((nx, LANES), 1)
     own = terrain_ref[...].astype(F32)
     own = jnp.concatenate([own, jnp.zeros((nx, LANES - size), F32)], 1)
-    here = face + nx * EDGE
-    before = pltpu.roll(rp_ref[here : here + 16].astype(F32), (EDGE - size) % LANES, 1)[:nx]
-    after = pltpu.roll(rm_ref[here : here + 16].astype(F32), (EDGE + size) % LANES, 1)[:nx]
+    land = slice(nx * EDGE, nx * EDGE + 16)
+    before = pltpu.roll(under[land], (EDGE - size) % LANES, 1)[:nx]
+    after = pltpu.roll(over[land], (EDGE + size) % LANES, 1)[:nx]
     ground = jnp.where(lane < EDGE, before, jnp.where(lane < EDGE + size, pltpu.roll(own, EDGE, 1), after))
     y = lane + (place * size - EDGE)
     flags = jnp.zeros((nx, LANES), jnp.int32)
@@ -241,17 +274,21 @@
     cols_ref[...] = jnp.zeros_like(cols_ref)
     cols_ref[:nx] = ground
     cols_ref[EDGE : EDGE + nx] = lifted
-    fill = jnp.zeros((14, LANES), F32)
+    fill = jnp.zeros((16 - 2 * ncomp - 4, LANES), F32)
+    strip, first, last = (slice(EDGE, EDGE + size), slice(EDGE - 1, EDGE), slice(EDGE + size, EDGE + size + 1))
 
     def send(ref, x, inner):
         for comp in range(ncomp):
-            ref[comp * rows : (comp + 1) * rows] = edge_ref[(ncomp if x else 0) + comp]
-            ref[(ncomp + comp) * rows : (ncomp + comp + 1) * rows] = wind_ref[comp * nx + x].astype(BF)
-        at = 2 * ncomp * rows
-        ref[at : at + rows] = conc_ref[x].astype(BF)
-        ref[at + rows : at + 2 * rows] = conc_ref[inner].astype(BF)
-        at = at + 2 * rows
-        ref[at : at + 16] = jnp.concatenate([ground[x : x + 1], lifted[x : x + 1], fill], 0).astype(BF)
+            j = comp * nx + x
+            ref[comp * size : (comp + 1) * size] = frame[j, strip].astype(BF)
+            ref[(ncomp + comp) * size : (ncomp + comp + 1) * size] = wind_ref[j, strip].astype(BF)
+        at = 2 * ncomp * size
+        ref[at : at + size] = conc_ref[x, strip].astype(BF)
+        ref[at + size : at + 2 * size] = conc_ref[inner, strip].astype(BF)
+        at = at + 2 * size
+        rows = [frame[comp * nx + x, first] for comp in range(ncomp)] + [conc_ref[x, first]]
+        rows += [frame[comp * nx + x, last] for comp in range(ncomp)] + [conc_ref[x, last]]
+        ref[at : at + 16] = jnp.concatenate(rows + [ground[x : x + 1], lifted[x : x + 1], fill], 0).astype(BF)
 
     @pl.when(odd)
     def _():
@@ -270,7 +307,8 @@
     rows = size + 2 * EDGE
     column, place = (lax.axis_index("horiz"), lax.axis_index("vert"))
     odd = lax.rem(column, 2) == 1
-    here = 2 * (ncomp + 1) * rows
+    here = 2 * (ncomp + 1) * size
+    low = iota((EDGE, nz), 0)
 
     def below(start, n):
         return jnp.where(odd, near_ref[start : start + n].astype(F32), far_ref[start : start + n].astype(F32))
@@ -278,17 +316,22 @@
     def above(start, n):
         return jnp.where(odd, far_ref[start : start + n].astype(F32), near_ref[start : start + n].astype(F32))
 
-    def part(side, i):
-        return side(i * rows, rows)
-
-    conc = [part(below, 2 * ncomp + 1), part(below, 2 * ncomp)]
+    def part(side, i, halo=None):
+        head, tail = (jnp.zeros((EDGE, nz), F32),) * 2
+        if halo is not None:
+            rest = ends[side]
+            head = jnp.where(low == EDGE - 1, rest[halo : halo + 1], head)
+            tail = jnp.where(low == 0, rest[ncomp + 1 + halo : ncomp + 2 + halo], tail)
+        return jnp.concatenate([head, side(i * size, size), tail], 0)
+
+    ends = {below: below(here, 16), above: above(here, 16)}
+    conc = [part(below, 2 * ncomp + 1), part(below, 2 * ncomp, ncomp)]
     conc += [conc_ref[x] for x in range(nx)]
-    conc += [part(above, 2 * ncomp), part(above, 2 * ncomp + 1)]
-    table = jnp.concatenate(
-        [below(here, 16), cols_ref[...], above(here, 16), jnp.zeros((LANES - 48, LANES), F32)], 0
-    ).T[:rows]
-    ground = [0] + [16 + x for x in range(nx)] + [32]
-    lifted = [1] + [16 + EDGE + x for x in range(nx)] + [33]
+    conc += [part(above, 2 * ncomp, ncomp), part(above, 2 * ncomp + 1)]
+    table = jnp.concatenate([ends[below], cols_ref[...], ends[above], jnp.zeros((LANES - 48, LANES), F32)], 0).T[:rows]
+    mark = 2 * (ncomp + 1)
+    ground = [mark] + [16 + x for x in range(nx)] + [32 + mark]
+    lifted = [mark + 1] + [16 + EDGE + x for x in range(nx)] + [33 + mark]
     layer = iota((rows, nz), 1).astype(F32)
     y = iota((rows, nz), 0) + (place * size - EDGE)
     inside = (y >= 0) & (y < ny)
@@ -305,9 +348,9 @@
             else:
                 w = wind_ref[comp * nx + p - 1]
                 if p == 1:
-                    w = w + 0.12 * part(below, comp)
+                    w = w + 0.12 * part(below, comp, comp)
                 if p == nx:
-                    w = w + 0.12 * part(above, comp)
+                    w = w + 0.12 * part(above, comp, comp)
             comps.append(w)
         gu, gv, gw = comps
         speed = jnp.sqrt(gu * gu + gv * gv)
@@ -346,22 +389,23 @@
         out_ref[x] = twice[EDGE : EDGE + size]
 
 
+def pairs(size, start):
+    return [p for i in range(start, size - 1, 2) for p in ((i, i + 1), (i + 1, i))]
+
+
 def local(velocity, dust, eligible, terrain):
     ncomp, nx, ny, nz = velocity.shape
     size = dust.shape[1]
     nh, nv = (lax.axis_size("horiz"), lax.axis_size("vert"))
     rows = size + 2 * EDGE
-    rise = [(i, i + 1) for i in range(nv - 1)]
-    fall = [(j, i) for i, j in rise]
-    near_pairs = [p for i in range(0, nh - 1, 2) for p in ((i, i + 1), (i + 1, i))]
-    far_pairs = [p for i in range(1, nh - 1, 2) for p in ((i, i + 1), (i + 1, i))]
+    near_pairs, far_pairs = (pairs(nh, 0), pairs(nh, 1))
     nplane = ncomp * nx
     anywhere = pl.BlockSpec(memory_space=pl.ANY)
 
     strips = call(
-        functools.partial(pack_strips, size),
+        functools.partial(pack_low, size),
         [shaped(nplane * size + 64, LANES)] * nv,
-        "pack_strips",
+        "pack_low",
         [
             pltpu.VMEM((ncomp, nx, ny, nz), F32),
             pltpu.VMEM((nv, 64, LANES), F32),
@@ -370,23 +414,38 @@
         in_specs=[anywhere],
         out_specs=[VMEM] * nv,
     )(pltpu.with_memory_space_constraint(velocity, pltpu.HBM))
-    got = [strips[0]] + [lax.ppermute(strips[t], "vert", [(0, t)]) for t in range(1, nv)]
-
-    face = ny // LANES * 16
-    zm, zp, lay = call(
-        functools.partial(pack_ends, size),
-        [shaped(face + nx * EDGE + 32, LANES)] * 2 + [shaped(nv, 16, LANES)],
+    ends = ny // LANES * 16 + nx * EDGE + 32
+    first, second, mine, *lays = call(
+        functools.partial(pack_ends, size, nv),
+        [shaped(ends, LANES)] * 2 + [shaped(3, 16, LANES)] + [shaped(16, LANES)] * (nv - 3),
         "pack_ends",
-        [pltpu.VMEM((16, ny), F32)] * 2,
-        in_specs=[VMEM] * 3 + [anywhere],
-    )(velocity, dust, terrain, strips[-1])
-    rm = lax.ppermute(zm, "vert", fall)
-    rp = lax.ppermute(zp, "vert", rise)
-    lays = [lay] + [lax.ppermute(lay[t], "vert", [(1, t)]) for t in range(3, nv)]
-
-    far, near = call(pack_sides, [shaped(ncomp, ny, nz)] * 2, "pack_sides", in_specs=[VMEM, anywhere])(
-        velocity, rm
+        [pltpu.VMEM((16, ny), F32)] * 2
+        + [pltpu.VMEM((2, nx, EDGE, nz), F32), pltpu.VMEM((nx, size), jnp.int32), pltpu.SemaphoreType.DMA((3,))],
+        in_specs=[VMEM, anywhere, anywhere, anywhere],
+    )(
+        velocity,
+        pltpu.with_memory_space_constraint(dust, pltpu.HBM),
+        pltpu.with_memory_space_constraint(terrain, pltpu.HBM),
+        strips[-1],
     )
+    first = lax.ppermute(first, "vert", pairs(nv, 0))
+    second = lax.ppermute(second, "vert", pairs(nv, 1))
+    lays = [mine] + [lax.ppermute(lay, "vert", [(1, t + 3)]) for t, lay in enumerate(lays)]
+
+    sent = call(
+        gate,
+        [jax.ShapeDtypeStruct(rows.shape, rows.dtype) for rows in strips[1:]],
+        "gate",
+        in_specs=[anywhere] * nv,
+        out_specs=[anywhere] * (nv - 1),
+        input_output_aliases={t: t for t in range(nv - 1)},
+    )(*strips[1:], first)
+    got = [lax.ppermute(sent[t - 1], "vert", [(0, t)]) for t in range(nv - 1, 0, -1)]
+    got = [strips[0]] + got[::-1]
+
+    far, near = call(
+        pack_sides, [shaped(ncomp, ny, nz)] * 2, "pack_sides", cost=1 << 26, in_specs=[VMEM, anywhere]
+    )(velocity, sent[-1])
     far = lax.ppermute(far, "horiz", far_pairs)
     near = lax.ppermute(near, "horiz", near_pairs)
 
@@ -397,9 +456,9 @@
         [pltpu.VMEM((ncomp, nx, ny, nz), F32), pltpu.SemaphoreType.DMA((ncomp,))],
         in_specs=[VMEM] * 5,
         out_specs=anywhere,
-    )(velocity, far, near, rm, rp)
-
-    wire = (2 * ncomp + 2) * rows + 16
+    )(velocity, far, near, first, second)
+
+    wire = (2 * ncomp + 2) * size + 16
     wind, conc, cols, mf, mn, edge = call(
         functools.partial(prepare, nv),
         [
@@ -412,7 +471,7 @@
         ],
         "prepare",
         [pltpu.VMEM((nplane, rows, LANES), F32)],
-    )(*got, *lays, dust, terrain, eligible, rm, rp)
+    )(*got, *lays, dust, terrain, eligible, first, second)
     mf = lax.ppermute(mf, "horiz", far_pairs)
     mn = lax.ppermute(mn, "horiz", near_pairs)
     dust_next = call(

time: 37.2 us -> 33.9 us (0.911)
  the two profiles are of different devices: /device:TPU:20 before, /device:TPU:28 now
where the time goes in v3:
time: 33.9 us; the launch traced here: 33.5 us
  starting transfers between devices  12.2 us (36%)
  waiting for transfers between devices  12 us (35%)
  Pallas kernels  7.03 us (21%)
  local copies, waits for them, and re-layouts  1.46 us (4%)
  between operations  0.77 us (2%)
    ppermute x1, waiting for transfers between devices, local(): lax.ppermute(lay, 'vert', [(1, t + 3)])  4.33 us
    ppermute x1, waiting for transfers between devices, local(): first = lax.ppermute(first, 'vert', pairs(nv, 0))  3.38 us
    ppermute x3, waiting for transfers between devices, local(): lax.ppermute(sent[t - 1], 'vert', [(0, t)])  3.18 us
    pallas_call x1, Pallas kernels, local(): call(advance, jax.ShapeDtypeStruct(velocity.shape, F32), 'advance', [pltp...  3.03 us
    ppermute x3, starting transfers between devices, local(): lax.ppermute(sent[t - 1], 'vert', [(0, t)])  2.63 us
    ppermute x1, starting transfers between devices, local(): mf = lax.ppermute(mf, 'horiz', far_pairs)  1.92 us
    ppermute x1, starting transfers between devices, local(): far = lax.ppermute(far, 'horiz', far_pairs)  1.91 us
    ppermute x1, starting transfers between devices, local(): near = lax.ppermute(near, 'horiz', near_pairs)  1.66 us
  transfers between devices with their start and end apart: 10, of which 4 were waited for; matrix products, arithmetic and copies ran while one was open for 0% of the time, Pallas kernels for 13%

profile of v3, /device:TPU:28, one launch (start us, length us, event | category | flops | bytes accessed | tf_op | source)
XLA Modules:
  0.0 33.5 jit_solution(12688132217925988881)
XLA Ops:
  0.6 0.0 copy-start
  0.7 1.4 %copy-done = f32[3,4,256,128]{3,2,1,0:T(8,128)S(1)} copy-done((f32[3,4,256,128]{3,2,1,0:T(8,128)S(1)}, f32[3,4,256,128]{3,2,1,0:T(8,128)}, u32[]{:S(2)}) %copy-start) | copy-done | bytes 1572888
  2.0 1.1 %pack_ends.1 = (bf16[96,128]{1,0:T(8,128)(2,1)S(1)}, bf16[96,128]{1,0:T(8,128)(2,1)S(1)}, bf16[3,16,128]{2,1,0:T(8,128)(2,1)S(1)}, bf16[16,128]{1,0:T(8,128)(2,1)S(1)}) custom-call(f32[3,4,256,128]{3,2,1,0:T(8,128)S(1)} %copy-done, f32[4,64,128]{2,1,0:T(8,128)} %refs_6_.1, s32[4,64]{1,0:T(4,128)} %refs_7_.1, ...), custom_call_target="tpu_custom_call" | custom-call | flops 1048576 | bytes 1048576 | tf_op jit(solution)/shard_map/pack_ends/pallas_call | solution.py:418
  3.1 0.0 copy-start.3
  3.1 0.0 copy-start.1
  3.2 0.0 copy-start.2
  3.2 0.5 %collective-permute-start = (bf16[96,128]{1,0:T(8,128)(2,1)S(1)}, bf16[96,128]{1,0:T(8,128)(2,1)S(1)}, u32[]{:S(2)}, u32[]{:S(2)}) collective-permute-start(bf16[96,128]{1,0:T(8,128)(2,1)S(1)} %get-tuple-element.24), channel_id=1, source_target_pairs={{0,1},{1,0},{2,3},{3,2},{4,5},{5,4},{6,7},{7,6},{8,9},{9,8},{10,11... | collective-permute-start | bytes 73736 | tf_op jit(solution)/shard_map/ppermute | solution.py:431
  3.7 3.4 %collective-permute-done.refs_3_.first_ref.refs_9_ = bf16[96,128]{1,0:T(8,128)(2,1)S(1)} collective-permute-done((bf16[96,128]{1,0:T(8,128)(2,1)S(1)}, bf16[96,128]{1,0:T(8,128)(2,1)S(1)}, u32[]{:S(2)}, u32[]{:S(2)}) %collective-permute-start) | collective-permute-done | bytes 24608 | tf_op jit(solution)/shard_map/ppermute | solution.py:431
  7.1 0.7 %collective-permute-start.4 = (bf16[832,128]{1,0:T(8,128)(2,1)S(1)}, bf16[832,128]{1,0:T(8,128)(2,1)S(1)}, u32[]{:S(2)}, u32[]{:S(2)}) collective-permute-start(bf16[832,128]{1,0:T(8,128)(2,1)S(1)} %get-tuple-element.30), channel_id=1, source_target_pairs={{0,1},{4,5},{8,9},{12,13},{16,17},{20,21},{24,25},{28,29}} | collective-permute-start | bytes 638984 | tf_op jit(solution)/shard_map/ppermute | solution.py:443
  7.7 0.7 %collective-permute-start.5 = (bf16[832,128]{1,0:T(8,128)(2,1)S(1)}, bf16[832,128]{1,0:T(8,128)(2,1)S(1)}, u32[]{:S(2)}, u32[]{:S(2)}) collective-permute-start(bf16[832,128]{1,0:T(8,128)(2,1)S(1)} %get-tuple-element.31), channel_id=1, source_target_pairs={{0,2},{4,6},{8,10},{12,14},{16,18},{20,22},{24,26},{28,30}} | collective-permute-start | bytes 638984 | tf_op jit(solution)/shard_map/ppermute | solution.py:443
  8.4 1.3 %collective-permute-start.6 = (bf16[832,128]{1,0:T(8,128)(2,1)S(1)}, bf16[832,128]{1,0:T(8,128)(2,1)S(1)}, u32[]{:S(2)}, u32[]{:S(2)}) collective-permute-start(bf16[832,128]{1,0:T(8,128)(2,1)S(1)} %get-tuple-element.25.after_ref), channel_id=1, source_target_pairs={{0,3},{4,7},{8,11},{12,15},{16,19},{20,23},{24,27},{28,31}} | collective-permute-start | bytes 638984 | tf_op jit(solution)/shard_map/ppermute | solution.py:443
  9.7 0.7 %collective-permute-start.3 = (bf16[96,128]{1,0:T(8,128)(2,1)S(1)}, bf16[96,128]{1,0:T(8,128)(2,1)S(1)}, u32[]{:S(2)}, u32[]{:S(2)}) collective-permute-start(bf16[96,128]{1,0:T(8,128)(2,1)S(1)} %get-tuple-element.28), channel_id=1, source_target_pairs={{1,2},{2,1},{5,6},{6,5},{9,10},{10,9},{13,14},{14,13},{17,18},{18,... | collective-permute-start | bytes 73736 | tf_op jit(solution)/shard_map/ppermute | solution.py:432
  10.4 1.3 %collective-permute-start.7 = (bf16[16,128]{1,0:T(8,128)(2,1)S(1)}, bf16[16,128]{1,0:T(8,128)(2,1)S(1)}, u32[]{:S(2)}, u32[]{:S(2)}) collective-permute-start(bf16[16,128]{1,0:T(8,128)(2,1)S(1)} %get-tuple-element.33), channel_id=1, source_target_pairs={{1,3},{5,7},{9,11},{13,15},{17,19},{21,23},{25,27},{29,31}} | collective-permute-start | bytes 12296 | tf_op jit(solution)/shard_map/ppermute | solution.py:433
  11.7 0.8 %pack_sides.1 = (bf16[3,256,128]{2,1,0:T(8,128)(2,1)}, bf16[3,256,128]{2,1,0:T(8,128)(2,1)}) custom-call(f32[3,4,256,128]{3,2,1,0:T(8,128)S(1)} %copy-done, bf16[832,128]{1,0:T(8,128)(2,1)S(1)} %get-tuple-element.25.after_ref), custom_call_target="tpu_custom_call" | custom-call | flops 67108864 | bytes 67108864 | tf_op jit(solution)/shard_map/pack_sides/pallas_call | solution.py:446
  12.5 4.3 %collective-permute-done.7.refs_5_ = bf16[16,128]{1,0:T(8,128)(2,1)S(1)} collective-permute-done((bf16[16,128]{1,0:T(8,128)(2,1)S(1)}, bf16[16,128]{1,0:T(8,128)(2,1)S(1)}, u32[]{:S(2)}, u32[]{:S(2)}) %collective-permute-start.7) | collective-permute-done | bytes 4128 | tf_op jit(solution)/shard_map/ppermute | solution.py:433
  16.8 1.9 %collective-permute-start.1 = (bf16[3,256,128]{2,1,0:T(8,128)(2,1)}, bf16[3,256,128]{2,1,0:T(8,128)(2,1)S(1)}, u32[]{:S(2)}, u32[]{:S(2)}) collective-permute-start(bf16[3,256,128]{2,1,0:T(8,128)(2,1)} %get-tuple-element.26), channel_id=1, source_target_pairs={{4,8},{8,4},{12,16},{16,12},{20,24},{24,20},{5,9},{9,5},{13,17},{1... | collective-permute-start | bytes 589832 | tf_op jit(solution)/shard_map/ppermute | solution.py:449
  18.7 0.0 collective-permute-done.3.second_ref.refs_10_
  18.8 1.7 %collective-permute-start.2 = (bf16[3,256,128]{2,1,0:T(8,128)(2,1)}, bf16[3,256,128]{2,1,0:T(8,128)(2,1)}, u32[]{:S(2)}, u32[]{:S(2)}) collective-permute-start(bf16[3,256,128]{2,1,0:T(8,128)(2,1)} %get-tuple-element.27), channel_id=1, source_target_pairs={{0,4},{4,0},{8,12},{12,8},{16,20},{20,16},{24,28},{28,24},{1,5},{5... | collective-permute-start | bytes 589832 | tf_op jit(solution)/shard_map/ppermute | solution.py:450
  20.4 0.0 copy-done.3
  20.4 0.1 copy.9.refs_8_
  20.5 0.0 collective-permute-done.4.refs_1_
  20.5 0.0 collective-permute-done.5.refs_2_
  20.5 3.2 %collective-permute-done.6.refs_3_ = bf16[832,128]{1,0:T(8,128)(2,1)S(1)} collective-permute-done((bf16[832,128]{1,0:T(8,128)(2,1)S(1)}, bf16[832,128]{1,0:T(8,128)(2,1)S(1)}, u32[]{:S(2)}, u32[]{:S(2)}) %collective-permute-start.6) | collective-permute-done | bytes 213024 | tf_op jit(solution)/shard_map/ppermute | solution.py:443
  23.7 0.0 copy-done.1
  23.7 0.0 copy-done.2
  23.7 0.6 %prepare.1 = (f32[12,80,128]{2,1,0:T(8,128)S(1)}, f32[4,80,128]{2,1,0:T(8,128)S(1)}, f32[16,128]{1,0:T(8,128)S(1)}, bf16[528,128]{1,0:T(8,128)(2,1)S(1)}, bf16[5...) custom-call(bf16[832,128]{1,0:T(8,128)(2,1)S(1)} %get-tuple-element.29.refs_0_, ...), custom_call_target="tpu_custom_call" | custom-call | flops 1048576 | bytes 1048576 | tf_op jit(solution)/shard_map/prepare/pallas_call | solution.py:462
  24.3 1.9 %collective-permute-start.8 = (bf16[528,128]{1,0:T(8,128)(2,1)S(1)}, bf16[528,128]{1,0:T(8,128)(2,1)S(1)}, u32[]{:S(2)}, u32[]{:S(2)}) collective-permute-start(bf16[528,128]{1,0:T(8,128)(2,1)S(1)} %get-tuple-element.38), channel_id=1, source_target_pairs={{4,8},{8,4},{12,16},{16,12},{20,24},{24,20},{5,9},{9,5},{13,17},{1... | collective-permute-start | bytes 405512 | tf_op jit(solution)/shard_map/ppermute | solution.py:475
  26.2 1.7 %collective-permute-start.9 = (bf16[528,128]{1,0:T(8,128)(2,1)S(1)}, bf16[528,128]{1,0:T(8,128)(2,1)S(1)}, u32[]{:S(2)}, u32[]{:S(2)}) collective-permute-start(bf16[528,128]{1,0:T(8,128)(2,1)S(1)} %get-tuple-element.39), channel_id=1, source_target_pairs={{0,4},{4,0},{8,12},{12,8},{16,20},{20,16},{24,28},{28,24},{1,5},{5... | collective-permute-start | bytes 405512 | tf_op jit(solution)/shard_map/ppermute | solution.py:476
  27.9 0.0 collective-permute-done.1.far_ref
  27.9 0.0 collective-permute-done.2.near_ref
  27.9 3.0 %advance.1 = f32[3,4,256,128]{3,2,1,0:T(8,128)} custom-call(f32[3,4,256,128]{3,2,1,0:T(8,128)S(1)} %copy-done, bf16[3,256,128]{2,1,0:T(8,128)(2,1)S(1)} %collective-permute-done.1.far_ref, bf16[3,256,128]{2,1,0:T(8,128)(2,1)} %collective-permute-done.2.near_ref, bf16[96,128]{1,0:T(8,128)(2,1)S(1)} %collective-permute-done.refs_3_.first_ref.refs_9_, ...), custom_call_target="tpu_custom_call" | custom-call | flops 1048576 | bytes 1048576 | tf_op jit(solution)/shard_map/advance/pallas_call | solution.py:452
  30.9 1.1 %collective-permute-done.8.far_ref = bf16[528,128]{1,0:T(8,128)(2,1)S(1)} collective-permute-done((bf16[528,128]{1,0:T(8,128)(2,1)S(1)}, bf16[528,128]{1,0:T(8,128)(2,1)S(1)}, u32[]{:S(2)}, u32[]{:S(2)}) %collective-permute-start.8) | collective-permute-done | bytes 135200 | tf_op jit(solution)/shard_map/ppermute | solution.py:475
  32.0 0.0 collective-permute-done.9.near_ref
  32.0 1.5 %transport.1 = f32[4,64,128]{2,1,0:T(8,128)} custom-call(f32[12,80,128]{2,1,0:T(8,128)S(1)} %get-tuple-element.34.wind_ref, bf16[6,80,128]{2,1,0:T(8,128)(2,1)S(1)} %get-tuple-element.35.edge_ref, f32[4,80,128]{2,1,0:T(8,128)S(1)} %get-tuple-element.36.conc_ref, f32[16,128]{1,0:T(8,128)S(1)} %get-tuple-element.37.cols_ref, ...), custom_call_target="tpu_custom_call" | custom-call | flops 1048576 | bytes 1048576 | tf_op jit(solution)/shard_map/transport/pallas_call | solution.py:477
  (2 shorter events, 0.0 us)
Async XLA Ops:
  0.6 1.4 %copy-start = (f32[3,4,256,128]{3,2,1,0:T(8,128)S(1)}, f32[3,4,256,128]{3,2,1,0:T(8,128)}, u32[]{:S(2)}) copy-start(f32[3,4,256,128]{3,2,1,0:T(8,128)} %v_ref.7) | copy-start | bytes 4718596
  3.1 17.3 %copy-start.3 = (s32[4,2]{0,1:T(2,128)S(1)}, s32[4,2]{0,1:T(2,128)}, u32[]{:S(2)}) copy-start(s32[4,2]{0,1:T(2,128)} %param.6) | copy-start | bytes 100
  3.1 20.5 %copy-start.1 = (f32[4,64,128]{2,1,0:T(8,128)S(1)}, f32[4,64,128]{2,1,0:T(8,128)}, u32[]{:S(2)}) copy-start(f32[4,64,128]{2,1,0:T(8,128)} %refs_6_.1) | copy-start | bytes 393220
  3.2 20.5 %copy-start.2 = (s32[4,64]{1,0:T(4,128)S(1)}, s32[4,64]{1,0:T(4,128)}, u32[]{:S(2)}) copy-start(s32[4,64]{1,0:T(4,128)} %refs_7_.1) | copy-start | bytes 3076
  3.2 3.9 %collective-permute-start = (bf16[96,128]{1,0:T(8,128)(2,1)S(1)}, bf16[96,128]{1,0:T(8,128)(2,1)S(1)}, u32[]{:S(2)}, u32[]{:S(2)}) collective-permute-start(bf16[96,128]{1,0:T(8,128)(2,1)S(1)} %get-tuple-element.24), channel_id=1, source_target_pairs={{0,1},{1,0},{2,3},{3,2},{4,5},{5,4},{6,7},{7,6},{8,9},{9,8},{10,11... | collective-permute-start | bytes 73736 | tf_op jit(solution)/shard_map/ppermute | solution.py:431
  7.1 13.4 %collective-permute-start.4 = (bf16[832,128]{1,0:T(8,128)(2,1)S(1)}, bf16[832,128]{1,0:T(8,128)(2,1)S(1)}, u32[]{:S(2)}, u32[]{:S(2)}) collective-permute-start(bf16[832,128]{1,0:T(8,128)(2,1)S(1)} %get-tuple-element.30), channel_id=1, source_target_pairs={{0,1},{4,5},{8,9},{12,13},{16,17},{20,21},{24,25},{28,29}} | collective-permute-start | bytes 638984 | tf_op jit(solution)/shard_map/ppermute | solution.py:443
  7.7 12.8 %collective-permute-start.5 = (bf16[832,128]{1,0:T(8,128)(2,1)S(1)}, bf16[832,128]{1,0:T(8,128)(2,1)S(1)}, u32[]{:S(2)}, u32[]{:S(2)}) collective-permute-start(bf16[832,128]{1,0:T(8,128)(2,1)S(1)} %get-tuple-element.31), channel_id=1, source_target_pairs={{0,2},{4,6},{8,10},{12,14},{16,18},{20,22},{24,26},{28,30}} | collective-permute-start | bytes 638984 | tf_op jit(solution)/shard_map/ppermute | solution.py:443
  8.4 15.3 %collective-permute-start.6 = (bf16[832,128]{1,0:T(8,128)(2,1)S(1)}, bf16[832,128]{1,0:T(8,128)(2,1)S(1)}, u32[]{:S(2)}, u32[]{:S(2)}) collective-permute-start(bf16[832,128]{1,0:T(8,128)(2,1)S(1)} %get-tuple-element.25.after_ref), channel_id=1, source_target_pairs={{0,3},{4,7},{8,11},{12,15},{16,19},{20,23},{24,27},{28,31}} | collective-permute-start | bytes 638984 | tf_op jit(solution)/shard_map/ppermute | solution.py:443
  9.7 9.0 %collective-permute-start.3 = (bf16[96,128]{1,0:T(8,128)(2,1)S(1)}, bf16[96,128]{1,0:T(8,128)(2,1)S(1)}, u32[]{:S(2)}, u32[]{:S(2)}) collective-permute-start(bf16[96,128]{1,0:T(8,128)(2,1)S(1)} %get-tuple-element.28), channel_id=1, source_target_pairs={{1,2},{2,1},{5,6},{6,5},{9,10},{10,9},{13,14},{14,13},{17,18},{18,... | collective-permute-start | bytes 73736 | tf_op jit(solution)/shard_map/ppermute | solution.py:432
  10.4 6.4 %collective-permute-start.7 = (bf16[16,128]{1,0:T(8,128)(2,1)S(1)}, bf16[16,128]{1,0:T(8,128)(2,1)S(1)}, u32[]{:S(2)}, u32[]{:S(2)}) collective-permute-start(bf16[16,128]{1,0:T(8,128)(2,1)S(1)} %get-tuple-element.33), channel_id=1, source_target_pairs={{1,3},{5,7},{9,11},{13,15},{17,19},{21,23},{25,27},{29,31}} | collective-permute-start | bytes 12296 | tf_op jit(solution)/shard_map/ppermute | solution.py:433
  16.8 11.0 %collective-permute-start.1 = (bf16[3,256,128]{2,1,0:T(8,128)(2,1)}, bf16[3,256,128]{2,1,0:T(8,128)(2,1)S(1)}, u32[]{:S(2)}, u32[]{:S(2)}) collective-permute-start(bf16[3,256,128]{2,1,0:T(8,128)(2,1)} %get-tuple-element.26), channel_id=1, source_target_pairs={{4,8},{8,4},{12,16},{16,12},{20,24},{24,20},{5,9},{9,5},{13,17},{1... | collective-permute-start | bytes 589832 | tf_op jit(solution)/shard_map/ppermute | solution.py:449
  18.8 9.1 %collective-permute-start.2 = (bf16[3,256,128]{2,1,0:T(8,128)(2,1)}, bf16[3,256,128]{2,1,0:T(8,128)(2,1)}, u32[]{:S(2)}, u32[]{:S(2)}) collective-permute-start(bf16[3,256,128]{2,1,0:T(8,128)(2,1)} %get-tuple-element.27), channel_id=1, source_target_pairs={{0,4},{4,0},{8,12},{12,8},{16,20},{20,16},{24,28},{28,24},{1,5},{5... | collective-permute-start | bytes 589832 | tf_op jit(solution)/shard_map/ppermute | solution.py:450
  24.3 7.8 %collective-permute-start.8 = (bf16[528,128]{1,0:T(8,128)(2,1)S(1)}, bf16[528,128]{1,0:T(8,128)(2,1)S(1)}, u32[]{:S(2)}, u32[]{:S(2)}) collective-permute-start(bf16[528,128]{1,0:T(8,128)(2,1)S(1)} %get-tuple-element.38), channel_id=1, source_target_pairs={{4,8},{8,4},{12,16},{16,12},{20,24},{24,20},{5,9},{9,5},{13,17},{1... | collective-permute-start | bytes 405512 | tf_op jit(solution)/shard_map/ppermute | solution.py:475
  26.2 5.8 %collective-permute-start.9 = (bf16[528,128]{1,0:T(8,128)(2,1)S(1)}, bf16[528,128]{1,0:T(8,128)(2,1)S(1)}, u32[]{:S(2)}, u32[]{:S(2)}) collective-permute-start(bf16[528,128]{1,0:T(8,128)(2,1)S(1)} %get-tuple-element.39), channel_id=1, source_target_pairs={{0,4},{4,0},{8,12},{12,8},{16,20},{20,16},{24,28},{28,24},{1,5},{5... | collective-permute-start | bytes 405512 | tf_op jit(solution)/shard_map/ppermute | solution.py:476

commit v4 on v3

--- a/solution.py
+++ b/solution.py
@@ -42,33 +42,6 @@
     return jnp.where(hit, 1.0, 0.0).astype(BF)
 
 
-def pack_low(size, v_ref, *refs):
-    outs, (buf, side, sems) = (refs[:-3], refs[-3:])
-    ncomp, nx, ny, nz = v_ref.shape
-
-    @pl.when(lax.axis_index("vert") == 0)
-    def _():
-        copies = [pltpu.make_async_copy(v_ref.at[c], buf.at[c], sems.at[c]) for c in range(ncomp)]
-        for copy in copies:
-            copy.start()
-        side[...] = jnp.zeros_like(side)
-        for comp in range(ncomp):
-            copies[comp].wait()
-            for t, out in enumerate(outs):
-                for x in range(nx):
-                    j = comp * nx + x
-                    out[j * size : (j + 1) * size] = buf[comp, x, t * size : (t + 1) * size, :].astype(BF)
-                    for i, y in enumerate(halo_rows(t * size, size)):
-                        if 0 <= y < ny:
-                            side[t, i * 16 + j : i * 16 + j + 1] = buf[comp, x, y : y + 1, :]
-        for t, out in enumerate(outs):
-            out[ncomp * nx * size :] = side[t].astype(BF)
-
-
-def gate(*refs):
-    del refs
-
-
 def turn_faces(v_ref, comp, ends, outs):
     _, nx, ny, _ = v_ref.shape
     for x in range(nx):
@@ -101,18 +74,78 @@
         far_ref[...] = v_ref[:, 0].astype(BF)
 
 
+def start_all(copies):
+    for copy in copies:
+        copy.start()
+    return copies
+
+
+def wait_all(copies):
+    for copy in copies:
+        copy.wait()
+
+
+def write_ends(ref, at, face, dust, land, layer):
+    nx, size = land.shape
+    ny = face.shape[1]
+    terrain = jnp.concatenate([land.astype(F32), jnp.zeros((nx, LANES - size), F32)], 1)
+    terrain = jnp.concatenate([terrain, jnp.zeros((16 - nx, LANES), F32)], 0)
+    for half in range(ny // LANES):
+        ref[at + half * 16 : at + half * 16 + 16] = face[:, half * LANES : (half + 1) * LANES].astype(BF)
+    at = at + ny // LANES * 16
+    ref[at : at + nx * EDGE] = dust.reshape(nx * EDGE, LANES).astype(BF)
+    at = at + nx * EDGE
+    ref[at : at + 16] = terrain.astype(BF)
+    ref[at + 16 : at + 32] = layer
+
+
+def pack_low(size, v_ref, dust_ref, terrain_ref, *refs):
+    outs, (buf, high, side, dusts, land, sems) = (refs[:-6], refs[-6:])
+    ncomp, nx, ny, nz = v_ref.shape
+    nplane = ncomp * nx
+
+    @pl.when(lax.axis_index("vert") == 0)
+    def _():
+        planes = start_all(
+            [pltpu.make_async_copy(v_ref.at[j // nx, j % nx], buf.at[j // nx, j % nx], sems.at[j]) for j in range(nplane)]
+        )
+        small = start_all(
+            [
+                pltpu.make_async_copy(dust_ref.at[:, size - EDGE :], dusts, sems.at[nplane]),
+                pltpu.make_async_copy(terrain_ref, land, sems.at[nplane + 1]),
+            ]
+        )
+        side[...] = jnp.zeros_like(side)
+        high[...] = jnp.zeros_like(high)
+        end = pick((16, nz), [(0, nz - 1)])
+        for comp in range(ncomp):
+            wait_all(planes[comp * nx : (comp + 1) * nx])
+            turn_faces(buf, comp, end, [high])
+            for x in range(nx):
+                j = comp * nx + x
+                for t, out in enumerate(outs):
+                    out[j * size : (j + 1) * size] = buf[comp, x, t * size : (t + 1) * size, :].astype(BF)
+                    for i, y in enumerate(halo_rows(t * size, size)):
+                        if 0 <= y < ny:
+                            side[t, i * 16 + j : i * 16 + j + 1] = buf[comp, x, y : y + 1, :]
+        for t, out in enumerate(outs):
+            out[nplane * size : nplane * size + 64] = side[t].astype(BF)
+        wait_all(small)
+        write_ends(outs[1], nplane * size + 64, high, dusts[...], land[...], jnp.zeros((16, LANES), BF))
+
+
 def pack_ends(size, nstrips, v_ref, dust_ref, terrain_ref, after_ref, first_ref, second_ref, mine_ref, *refs):
     del after_ref
     lays, (low, high, dusts, land, sems) = (refs[:-5], refs[-5:])
     ncomp, nx, ny, nz = v_ref.shape
     odd = lax.rem(lax.axis_index("vert"), 2) == 1
-    copies = [
-        pltpu.make_async_copy(dust_ref.at[:, :EDGE], dusts.at[0], sems.at[0]),
-        pltpu.make_async_copy(dust_ref.at[:, size - EDGE :], dusts.at[1], sems.at[1]),
-        pltpu.make_async_copy(terrain_ref, land, sems.at[2]),
-    ]
-    for copy in copies:
-        copy.start()
+    small = start_all(
+        [
+            pltpu.make_async_copy(dust_ref.at[:, :EDGE], dusts.at[0], sems.at[0]),
+            pltpu.make_async_copy(dust_ref.at[:, size - EDGE :], dusts.at[1], sems.at[1]),
+            pltpu.make_async_copy(terrain_ref, land, sems.at[2]),
+        ]
+    )
     low[...] = jnp.zeros_like(low)
     high[...] = jnp.zeros_like(high)
     ends = pick((16, nz), [(0, 0), (1, nz - 1)])
@@ -129,46 +162,36 @@
             mine_ref[t] = part
         else:
             lays[t - 3][...] = part
-    for copy in copies:
-        copy.wait()
-    terrain = land[...].astype(F32)
-    terrain = jnp.concatenate([terrain, jnp.zeros((nx, LANES - size), F32)], 1)
-    terrain = jnp.concatenate([terrain, jnp.zeros((16 - nx, LANES), F32)], 0)
-
-    def send(ref, face, which, layer):
-        for half in range(ny // LANES):
-            ref[half * 16 : half * 16 + 16] = face[:, half * LANES : (half + 1) * LANES].astype(BF)
-        at = ny // LANES * 16
-        ref[at : at + nx * EDGE] = dusts[which].reshape(nx * EDGE, LANES).astype(BF)
-        at = at + nx * EDGE
-        ref[at : at + 16] = terrain.astype(BF)
-        ref[at + 16 : at + 32] = mine_ref[layer]
+    wait_all(small)
 
     @pl.when(odd)
     def _():
-        send(first_ref, low, 0, 0)
-        send(second_ref, high, 1, 2)
+        write_ends(first_ref, 0, low, dusts[0], land[...], mine_ref[0])
+        write_ends(second_ref, 0, high, dusts[1], land[...], mine_ref[2])
 
     @pl.when(jnp.logical_not(odd))
     def _():
-        send(first_ref, high, 1, 2)
-        send(second_ref, low, 0, 0)
-
-
-def sorted_ends(first_ref, second_ref, start, n):
-    odd = lax.rem(lax.axis_index("vert"), 2) == 1
+        write_ends(first_ref, 0, high, dusts[1], land[...], mine_ref[2])
+        write_ends(second_ref, 0, low, dusts[0], land[...], mine_ref[0])
+
+
+def sorted_ends(first_ref, second_ref, strip_ref, start, n):
+    place = lax.axis_index("vert")
+    odd = lax.rem(place, 2) == 1
+    base = strip_ref.shape[0] - first_ref.shape[0] + start
     first, second = (first_ref[start : start + n].astype(F32), second_ref[start : start + n].astype(F32))
-    return (jnp.where(odd, second, first), jnp.where(odd, first, second))
-
-
-def advance(v_ref, far_ref, near_ref, first_ref, second_ref, out_ref, buf, sems):
+    below = jnp.where(place == 1, strip_ref[base : base + n].astype(F32), jnp.where(odd, first, second))
+    return (jnp.where(odd, second, first), below)
+
+
+def advance(v_ref, far_ref, near_ref, first_ref, second_ref, strip_ref, out_ref, buf, sems):
     ncomp, nx, ny, nz = v_ref.shape
     odd = lax.rem(lax.axis_index("horiz"), 2) == 1
     row, lane = iota((LANES, nz), 0), iota((LANES, nz), 1)
     nb = ny // LANES
     turned = []
     for half in range(nb):
-        over, under = sorted_ends(first_ref, second_ref, half * 16, 16)
+        over, under = sorted_ends(first_ref, second_ref, strip_ref, half * 16, 16)
         faces = jnp.concatenate([over, under, jnp.zeros((LANES - 32, LANES), F32)], 0)
         turned.append(faces.T.astype(BF))
     copies = []
@@ -201,7 +224,7 @@
 
 
 def prepare(nstrips, *refs):
-    strips = refs[:nstrips]
+    strips = refs[:1] + refs[nstrips - 1 : 0 : -1]
     nlay = 1 + max(nstrips - 3, 0)
     lays = refs[nstrips : nstrips + nlay]
     dust_ref, terrain_ref, eligible_ref, first_ref, second_ref = refs[nstrips + nlay : nstrips + nlay + 5]
@@ -217,14 +240,14 @@
     for t in range(nstrips):
         @pl.when(place == t)
         def _(t=t):
-            beside = strips[t][nplane * size :].astype(F32)
+            beside = strips[t][nplane * size : nplane * size + 64].astype(F32)
             for j in range(nplane):
                 frame[j, EDGE : EDGE + size] = strips[t][j * size : (j + 1) * size].astype(F32)
                 for i, y in enumerate(halo_rows(EDGE, size)):
                     frame[j, y : y + 1] = beside[i * 16 + j : i * 16 + j + 1]
 
     face = first_ref.shape[0] - 32 - nx * EDGE
-    over, under = sorted_ends(first_ref, second_ref, face, nx * EDGE + 32)
+    over, under = sorted_ends(first_ref, second_ref, strips[1], face, nx * EDGE + 32)
     zero = jnp.zeros((16, LANES), F32)
     layer = jnp.where(place == 0, over[nx * EDGE + 16 :], zero)
     layer = layer + jnp.where(place == 1, lays[0][min(1, nstrips - 1)].astype(F32), zero)
@@ -402,50 +425,42 @@
     nplane = ncomp * nx
     anywhere = pl.BlockSpec(memory_space=pl.ANY)
 
+    ends = ny // LANES * 16 + nx * EDGE + 32
+    strip = nplane * size + 64
+    held = [pltpu.with_memory_space_constraint(array, pltpu.HBM) for array in (velocity, dust, terrain)]
     strips = call(
         functools.partial(pack_low, size),
-        [shaped(nplane * size + 64, LANES)] * nv,
+        [shaped(strip + (ends if t == 1 else 0), LANES) for t in range(nv)],
         "pack_low",
         [
             pltpu.VMEM((ncomp, nx, ny, nz), F32),
+            pltpu.VMEM((16, ny), F32),
             pltpu.VMEM((nv, 64, LANES), F32),
-            pltpu.SemaphoreType.DMA((ncomp,)),
+            pltpu.VMEM((nx, EDGE, nz), F32),
+            pltpu.VMEM((nx, size), jnp.int32),
+            pltpu.SemaphoreType.DMA((nplane + 2,)),
         ],
-        in_specs=[anywhere],
+        in_specs=[anywhere] * 3,
         out_specs=[VMEM] * nv,
-    )(pltpu.with_memory_space_constraint(velocity, pltpu.HBM))
-    ends = ny // LANES * 16 + nx * EDGE + 32
+    )(*held)
+    got = [lax.ppermute(strips[t], "vert", [(0, t)]) for t in range(nv - 1, 0, -1)]
+    got = [strips[0]] + got
+
     first, second, mine, *lays = call(
         functools.partial(pack_ends, size, nv),
         [shaped(ends, LANES)] * 2 + [shaped(3, 16, LANES)] + [shaped(16, LANES)] * (nv - 3),
         "pack_ends",
         [pltpu.VMEM((16, ny), F32)] * 2
         + [pltpu.VMEM((2, nx, EDGE, nz), F32), pltpu.VMEM((nx, size), jnp.int32), pltpu.SemaphoreType.DMA((3,))],
-        in_specs=[VMEM, anywhere, anywhere, anywhere],
-    )(
-        velocity,
-        pltpu.with_memory_space_constraint(dust, pltpu.HBM),
-        pltpu.with_memory_space_constraint(terrain, pltpu.HBM),
-        strips[-1],
-    )
-    first = lax.ppermute(first, "vert", pairs(nv, 0))
+        in_specs=[VMEM] + [anywhere] * 3,
+    )(velocity, *held[1:], strips[-1])
+    first = lax.ppermute(first, "vert", pairs(nv, 0)[1:])
     second = lax.ppermute(second, "vert", pairs(nv, 1))
     lays = [mine] + [lax.ppermute(lay, "vert", [(1, t + 3)]) for t, lay in enumerate(lays)]
 
-    sent = call(
-        gate,
-        [jax.ShapeDtypeStruct(rows.shape, rows.dtype) for rows in strips[1:]],
-        "gate",
-        in_specs=[anywhere] * nv,
-        out_specs=[anywhere] * (nv - 1),
-        input_output_aliases={t: t for t in range(nv - 1)},
-    )(*strips[1:], first)
-    got = [lax.ppermute(sent[t - 1], "vert", [(0, t)]) for t in range(nv - 1, 0, -1)]
-    got = [strips[0]] + got[::-1]
-
     far, near = call(
         pack_sides, [shaped(ncomp, ny, nz)] * 2, "pack_sides", cost=1 << 26, in_specs=[VMEM, anywhere]
-    )(velocity, sent[-1])
+    )(velocity, lays[-1])
     far = lax.ppermute(far, "horiz", far_pairs)
     near = lax.ppermute(near, "horiz", near_pairs)
 
@@ -454,9 +469,9 @@
         jax.ShapeDtypeStruct(velocity.shape, F32),
         "advance",
         [pltpu.VMEM((ncomp, nx, ny, nz), F32), pltpu.SemaphoreType.DMA((ncomp,))],
-        in_specs=[VMEM] * 5,
+        in_specs=[VMEM] * 6,
         out_specs=anywhere,
-    )(velocity, far, near, first, second)
+    )(velocity, far, near, first, second, got[-1])
 
     wire = (2 * ncomp + 2) * size + 16
     wind, conc, cols, mf, mn, edge = call(

time: 33.9 us -> 31.8 us (0.938)
  the two profiles are of different devices: /device:TPU:28 before, /device:TPU:19 now
where the time goes in v4:
time: 31.8 us; the launch traced here: 31.5 us
  starting transfers between devices  20.3 us (64%)
  Pallas kernels  6.86 us (22%)
  waiting for transfers between devices  3.46 us (11%)
  between operations  0.82 us (3%)
    ppermute x1, starting transfers between devices, local(): second = lax.ppermute(second, 'vert', pairs(nv, 1))  4.89 us
    ppermute x1, starting transfers between devices, local(): far = lax.ppermute(far, 'horiz', far_pairs)  4.51 us
    ppermute x1, starting transfers between devices, local(): first = lax.ppermute(first, 'vert', pairs(nv, 0)[1:])  3.84 us
    ppermute x1, starting transfers between devices, local(): mf = lax.ppermute(mf, 'horiz', far_pairs)  3.06 us
    ppermute x1, waiting for transfers between devices, local(): mf = lax.ppermute(mf, 'horiz', far_pairs)  2.82 us
    ppermute x3, starting transfers between devices, local(): lax.ppermute(strips[t], 'vert', [(0, t)])  2.77 us
    pallas_call x1, Pallas kernels, local(): call(advance, jax.ShapeDtypeStruct(velocity.shape, F32), 'advance', [pltp...  2.1 us
    pallas_call x1, Pallas kernels, local(): call(functools.partial(transport, ny, nh), jax.ShapeDtypeStruct(dust.shap...  1.47 us
  transfers between devices with their start and end apart: 10, of which 2 were waited for; matrix products, arithmetic and copies ran while one was open for 0% of the time, Pallas kernels for 15%

profile of v4, /device:TPU:19, one launch (start us, length us, event | category | flops | bytes accessed | tf_op | source)
XLA Modules:
  0.0 31.5 jit_solution(11007655501848071968)
XLA Ops:
  0.6 0.0 copy-start
  0.6 0.8 %pack_low.1 = (bf16[832,128]{1,0:T(8,128)(2,1)S(1)}, bf16[928,128]{1,0:T(8,128)(2,1)S(1)}, bf16[832,128]{1,0:T(8,128)(2,1)}, bf16[832,128]{1,0:T(8,128)(2,1)S(1)}) custom-call(f32[3,4,256,128]{3,2,1,0:T(8,128)} %v_ref.7, f32[4,64,128]{2,1,0:T(8,128)} %refs_6_.1, s32[4,64]{1,0:T(4,128)} %refs_7_.1), custom_call_target="tpu_custom_call" | custom-call | flops 1048576 | bytes 1048576 | tf_op jit(solution)/shard_map/pack_low/pallas_call | solution.py:431
  1.5 0.7 %collective-permute-start.5 = (bf16[928,128]{1,0:T(8,128)(2,1)S(1)}, bf16[928,128]{1,0:T(8,128)(2,1)S(1)}, u32[]{:S(2)}, u32[]{:S(2)}) collective-permute-start(bf16[928,128]{1,0:T(8,128)(2,1)S(1)} %get-tuple-element.24), channel_id=1, source_target_pairs={{0,1},{4,5},{8,9},{12,13},{16,17},{20,21},{24,25},{28,29}} | collective-permute-start | bytes 712712 | tf_op jit(solution)/shard_map/ppermute | solution.py:446
  2.2 0.7 %collective-permute-start.6 = (bf16[832,128]{1,0:T(8,128)(2,1)S(1)}, bf16[832,128]{1,0:T(8,128)(2,1)S(1)}, u32[]{:S(2)}, u32[]{:S(2)}) collective-permute-start(bf16[832,128]{1,0:T(8,128)(2,1)S(1)} %get-tuple-element.18.after_ref), channel_id=1, source_target_pairs={{0,3},{4,7},{8,11},{12,15},{16,19},{20,23},{24,27},{28,31}} | collective-permute-start | bytes 638984 | tf_op jit(solution)/shard_map/ppermute | solution.py:446
  2.8 0.0 copy-start.3
  2.8 0.0 copy-start.1
  2.9 0.0 copy-start.2
  2.9 1.4 %collective-permute-start.7 = (bf16[832,128]{1,0:T(8,128)(2,1)}, bf16[832,128]{1,0:T(8,128)(2,1)S(1)}, u32[]{:S(2)}, u32[]{:S(2)}) collective-permute-start(bf16[832,128]{1,0:T(8,128)(2,1)} %get-tuple-element.26), channel_id=1, source_target_pairs={{0,2},{4,6},{8,10},{12,14},{16,18},{20,22},{24,26},{28,30}} | collective-permute-start | bytes 638984 | tf_op jit(solution)/shard_map/ppermute | solution.py:446
  4.3 0.0 copy-done
  4.3 1.1 %pack_ends.1 = (bf16[96,128]{1,0:T(8,128)(2,1)S(1)}, bf16[96,128]{1,0:T(8,128)(2,1)S(1)}, bf16[3,16,128]{2,1,0:T(8,128)(2,1)S(1)}, bf16[16,128]{1,0:T(8,128)(2,1)S(1)}) custom-call(f32[3,4,256,128]{3,2,1,0:T(8,128)S(1)} %copy-done, f32[4,64,128]{2,1,0:T(8,128)} %refs_6_.1, s32[4,64]{1,0:T(4,128)} %refs_7_.1, bf16[832,128]{1,0:T(8,128)(2,1)S(1)} %get-tuple-element.18.after_ref), custom_call_target="tpu_custom_call" | custom-call | flops 1048576 | bytes 1048576 | tf_op jit(solution)/shard_map/pack_ends/pallas_call | solution.py:449
  5.4 0.7 %collective-permute-start = (bf16[16,128]{1,0:T(8,128)(2,1)S(1)}, bf16[16,128]{1,0:T(8,128)(2,1)S(1)}, u32[]{:S(2)}, u32[]{:S(2)}) collective-permute-start(bf16[16,128]{1,0:T(8,128)(2,1)S(1)} %get-tuple-element.19), channel_id=1, source_target_pairs={{1,3},{5,7},{9,11},{13,15},{17,19},{21,23},{25,27},{29,31}} | collective-permute-start | bytes 12296 | tf_op jit(solution)/shard_map/ppermute | solution.py:459
  6.1 3.8 %collective-permute-start.3 = (bf16[96,128]{1,0:T(8,128)(2,1)S(1)}, bf16[96,128]{1,0:T(8,128)(2,1)S(1)}, u32[]{:S(2)}, u32[]{:S(2)}) collective-permute-start(bf16[96,128]{1,0:T(8,128)(2,1)S(1)} %get-tuple-element.22), channel_id=1, source_target_pairs={{1,0},{2,3},{3,2},{5,4},{6,7},{7,6},{9,8},{10,11},{11,10},{13,12},... | collective-permute-start | bytes 73736 | tf_op jit(solution)/shard_map/ppermute | solution.py:457
  9.9 0.0 collective-permute-done.after_ref.refs_5_
  9.9 4.9 %collective-permute-start.4 = (bf16[96,128]{1,0:T(8,128)(2,1)S(1)}, bf16[96,128]{1,0:T(8,128)(2,1)S(1)}, u32[]{:S(2)}, u32[]{:S(2)}) collective-permute-start(bf16[96,128]{1,0:T(8,128)(2,1)S(1)} %get-tuple-element.23), channel_id=1, source_target_pairs={{1,2},{2,1},{5,6},{6,5},{9,10},{10,9},{13,14},{14,13},{17,18},{18,... | collective-permute-start | bytes 73736 | tf_op jit(solution)/shard_map/ppermute | solution.py:458
  14.8 0.8 %pack_sides.1 = (bf16[3,256,128]{2,1,0:T(8,128)(2,1)}, bf16[3,256,128]{2,1,0:T(8,128)(2,1)}) custom-call(f32[3,4,256,128]{3,2,1,0:T(8,128)S(1)} %copy-done, bf16[16,128]{1,0:T(8,128)(2,1)S(1)} %collective-permute-done.after_ref.refs_5_), custom_call_target="tpu_custom_call" | custom-call | flops 67108864 | bytes 67108864 | tf_op jit(solution)/shard_map/pack_sides/pallas_call | solution.py:461
  15.7 0.0 collective-permute-done.3.first_ref.refs_9_
  15.7 4.5 %collective-permute-start.1 = (bf16[3,256,128]{2,1,0:T(8,128)(2,1)}, bf16[3,256,128]{2,1,0:T(8,128)(2,1)S(1)}, u32[]{:S(2)}, u32[]{:S(2)}) collective-permute-start(bf16[3,256,128]{2,1,0:T(8,128)(2,1)} %get-tuple-element.20), channel_id=1, source_target_pairs={{4,8},{8,4},{12,16},{16,12},{20,24},{24,20},{5,9},{9,5},{13,17},{1... | collective-permute-start | bytes 589832 | tf_op jit(solution)/shard_map/ppermute | solution.py:464
  20.2 0.6 %collective-permute-done.4.second_ref.refs_10_ = bf16[96,128]{1,0:T(8,128)(2,1)S(1)} collective-permute-done((bf16[96,128]{1,0:T(8,128)(2,1)S(1)}, bf16[96,128]{1,0:T(8,128)(2,1)S(1)}, u32[]{:S(2)}, u32[]{:S(2)}) %collective-permute-start.4) | collective-permute-done | bytes 24608 | tf_op jit(solution)/shard_map/ppermute | solution.py:458
  20.8 0.5 %collective-permute-start.2 = (bf16[3,256,128]{2,1,0:T(8,128)(2,1)}, bf16[3,256,128]{2,1,0:T(8,128)(2,1)S(1)}, u32[]{:S(2)}, u32[]{:S(2)}) collective-permute-start(bf16[3,256,128]{2,1,0:T(8,128)(2,1)} %get-tuple-element.21), channel_id=1, source_target_pairs={{0,4},{4,0},{8,12},{12,8},{16,20},{20,16},{24,28},{28,24},{1,5},{5... | collective-permute-start | bytes 589832 | tf_op jit(solution)/shard_map/ppermute | solution.py:465
  21.3 0.0 copy-done.3
  21.3 0.1 copy.6.refs_8_
  21.4 0.0 collective-permute-done.6.refs_1_
  21.4 0.0 collective-permute-done.7.refs_2_
  21.4 0.0 collective-permute-done.5.strip_ref.refs_3_
  21.4 0.0 copy-done.1
  21.4 0.0 copy-done.2
  21.4 0.6 %prepare.1 = (f32[12,80,128]{2,1,0:T(8,128)S(1)}, f32[4,80,128]{2,1,0:T(8,128)S(1)}, f32[16,128]{1,0:T(8,128)S(1)}, bf16[528,128]{1,0:T(8,128)(2,1)S(1)}, bf16[5...) custom-call(bf16[832,128]{1,0:T(8,128)(2,1)S(1)} %get-tuple-element.25.refs_0_, ...), custom_call_target="tpu_custom_call" | custom-call | flops 1048576 | bytes 1048576 | tf_op jit(solution)/shard_map/prepare/pallas_call | solution.py:477
  21.9 3.1 %collective-permute-start.8 = (bf16[528,128]{1,0:T(8,128)(2,1)S(1)}, bf16[528,128]{1,0:T(8,128)(2,1)S(1)}, u32[]{:S(2)}, u32[]{:S(2)}) collective-permute-start(bf16[528,128]{1,0:T(8,128)(2,1)S(1)} %get-tuple-element.32), channel_id=1, source_target_pairs={{4,8},{8,4},{12,16},{16,12},{20,24},{24,20},{5,9},{9,5},{13,17},{1... | collective-permute-start | bytes 405512 | tf_op jit(solution)/shard_map/ppermute | solution.py:490
  25.0 0.1 collective-permute-start.9
  25.1 0.0 collective-permute-done.1.far_ref
  25.1 0.0 collective-permute-done.2.near_ref
  25.1 2.1 %advance.1 = f32[3,4,256,128]{3,2,1,0:T(8,128)} custom-call(f32[3,4,256,128]{3,2,1,0:T(8,128)S(1)} %copy-done, bf16[3,256,128]{2,1,0:T(8,128)(2,1)S(1)} %collective-permute-done.1.far_ref, bf16[3,256,128]{2,1,0:T(8,128)(2,1)S(1)} %collective-permute-done.2.near_ref, bf16[96,128]{1,0:T(8,128)(2,1)S(1)} %collective-permute-done.3.first_ref.refs_9_, ...), custom_call_target="tpu_custom_call" | custom-call | flops 1048576 | bytes 1048576 | tf_op jit(solution)/shard_map/advance/pallas_call | solution.py:467
  27.2 2.8 %collective-permute-done.8.far_ref = bf16[528,128]{1,0:T(8,128)(2,1)S(1)} collective-permute-done((bf16[528,128]{1,0:T(8,128)(2,1)S(1)}, bf16[528,128]{1,0:T(8,128)(2,1)S(1)}, u32[]{:S(2)}, u32[]{:S(2)}) %collective-permute-start.8) | collective-permute-done | bytes 135200 | tf_op jit(solution)/shard_map/ppermute | solution.py:490
  30.1 0.0 collective-permute-done.9.near_ref
  30.1 1.5 %transport.1 = f32[4,64,128]{2,1,0:T(8,128)} custom-call(f32[12,80,128]{2,1,0:T(8,128)S(1)} %get-tuple-element.28.wind_ref, bf16[6,80,128]{2,1,0:T(8,128)(2,1)S(1)} %get-tuple-element.29.edge_ref, f32[4,80,128]{2,1,0:T(8,128)S(1)} %get-tuple-element.30.conc_ref, f32[16,128]{1,0:T(8,128)S(1)} %get-tuple-element.31.cols_ref, ...), custom_call_target="tpu_custom_call" | custom-call | flops 1048576 | bytes 1048576 | tf_op jit(solution)/shard_map/transport/pallas_call | solution.py:492
Async XLA Ops:
  0.6 3.7 %copy-start = (f32[3,4,256,128]{3,2,1,0:T(8,128)S(1)}, f32[3,4,256,128]{3,2,1,0:T(8,128)}, u32[]{:S(2)}) copy-start(f32[3,4,256,128]{3,2,1,0:T(8,128)} %v_ref.7) | copy-start | bytes 4718596
  1.5 19.9 %collective-permute-start.5 = (bf16[928,128]{1,0:T(8,128)(2,1)S(1)}, bf16[928,128]{1,0:T(8,128)(2,1)S(1)}, u32[]{:S(2)}, u32[]{:S(2)}) collective-permute-start(bf16[928,128]{1,0:T(8,128)(2,1)S(1)} %get-tuple-element.24), channel_id=1, source_target_pairs={{0,1},{4,5},{8,9},{12,13},{16,17},{20,21},{24,25},{28,29}} | collective-permute-start | bytes 712712 | tf_op jit(solution)/shard_map/ppermute | solution.py:446
  2.2 19.2 %collective-permute-start.6 = (bf16[832,128]{1,0:T(8,128)(2,1)S(1)}, bf16[832,128]{1,0:T(8,128)(2,1)S(1)}, u32[]{:S(2)}, u32[]{:S(2)}) collective-permute-start(bf16[832,128]{1,0:T(8,128)(2,1)S(1)} %get-tuple-element.18.after_ref), channel_id=1, source_target_pairs={{0,3},{4,7},{8,11},{12,15},{16,19},{20,23},{24,27},{28,31}} | collective-permute-start | bytes 638984 | tf_op jit(solution)/shard_map/ppermute | solution.py:446
  2.8 18.4 %copy-start.3 = (s32[4,2]{0,1:T(2,128)S(1)}, s32[4,2]{0,1:T(2,128)}, u32[]{:S(2)}) copy-start(s32[4,2]{0,1:T(2,128)} %param.6) | copy-start | bytes 100
  2.8 18.5 %copy-start.1 = (f32[4,64,128]{2,1,0:T(8,128)S(1)}, f32[4,64,128]{2,1,0:T(8,128)}, u32[]{:S(2)}) copy-start(f32[4,64,128]{2,1,0:T(8,128)} %refs_6_.1) | copy-start | bytes 393220
  2.9 18.5 %copy-start.2 = (s32[4,64]{1,0:T(4,128)S(1)}, s32[4,64]{1,0:T(4,128)}, u32[]{:S(2)}) copy-start(s32[4,64]{1,0:T(4,128)} %refs_7_.1) | copy-start | bytes 3076
  2.9 18.5 %collective-permute-start.7 = (bf16[832,128]{1,0:T(8,128)(2,1)}, bf16[832,128]{1,0:T(8,128)(2,1)S(1)}, u32[]{:S(2)}, u32[]{:S(2)}) collective-permute-start(bf16[832,128]{1,0:T(8,128)(2,1)} %get-tuple-element.26), channel_id=1, source_target_pairs={{0,2},{4,6},{8,10},{12,14},{16,18},{20,22},{24,26},{28,30}} | collective-permute-start | bytes 638984 | tf_op jit(solution)/shard_map/ppermute | solution.py:446
  5.4 4.5 %collective-permute-start = (bf16[16,128]{1,0:T(8,128)(2,1)S(1)}, bf16[16,128]{1,0:T(8,128)(2,1)S(1)}, u32[]{:S(2)}, u32[]{:S(2)}) collective-permute-start(bf16[16,128]{1,0:T(8,128)(2,1)S(1)} %get-tuple-element.19), channel_id=1, source_target_pairs={{1,3},{5,7},{9,11},{13,15},{17,19},{21,23},{25,27},{29,31}} | collective-permute-start | bytes 12296 | tf_op jit(solution)/shard_map/ppermute | solution.py:459
  6.1 9.6 %collective-permute-start.3 = (bf16[96,128]{1,0:T(8,128)(2,1)S(1)}, bf16[96,128]{1,0:T(8,128)(2,1)S(1)}, u32[]{:S(2)}, u32[]{:S(2)}) collective-permute-start(bf16[96,128]{1,0:T(8,128)(2,1)S(1)} %get-tuple-element.22), channel_id=1, source_target_pairs={{1,0},{2,3},{3,2},{5,4},{6,7},{7,6},{9,8},{10,11},{11,10},{13,12},... | collective-permute-start | bytes 73736 | tf_op jit(solution)/shard_map/ppermute | solution.py:457
  9.9 10.9 %collective-permute-start.4 = (bf16[96,128]{1,0:T(8,128)(2,1)S(1)}, bf16[96,128]{1,0:T(8,128)(2,1)S(1)}, u32[]{:S(2)}, u32[]{:S(2)}) collective-permute-start(bf16[96,128]{1,0:T(8,128)(2,1)S(1)} %get-tuple-element.23), channel_id=1, source_target_pairs={{1,2},{2,1},{5,6},{6,5},{9,10},{10,9},{13,14},{14,13},{17,18},{18,... | collective-permute-start | bytes 73736 | tf_op jit(solution)/shard_map/ppermute | solution.py:458
  15.7 9.4 %collective-permute-start.1 = (bf16[3,256,128]{2,1,0:T(8,128)(2,1)}, bf16[3,256,128]{2,1,0:T(8,128)(2,1)S(1)}, u32[]{:S(2)}, u32[]{:S(2)}) collective-permute-start(bf16[3,256,128]{2,1,0:T(8,128)(2,1)} %get-tuple-element.20), channel_id=1, source_target_pairs={{4,8},{8,4},{12,16},{16,12},{20,24},{24,20},{5,9},{9,5},{13,17},{1... | collective-permute-start | bytes 589832 | tf_op jit(solution)/shard_map/ppermute | solution.py:464
  20.8 4.3 %collective-permute-start.2 = (bf16[3,256,128]{2,1,0:T(8,128)(2,1)}, bf16[3,256,128]{2,1,0:T(8,128)(2,1)S(1)}, u32[]{:S(2)}, u32[]{:S(2)}) collective-permute-start(bf16[3,256,128]{2,1,0:T(8,128)(2,1)} %get-tuple-element.21), channel_id=1, source_target_pairs={{0,4},{4,0},{8,12},{12,8},{16,20},{20,16},{24,28},{28,24},{1,5},{5... | collective-permute-start | bytes 589832 | tf_op jit(solution)/shard_map/ppermute | solution.py:465
  21.9 8.1 %collective-permute-start.8 = (bf16[528,128]{1,0:T(8,128)(2,1)S(1)}, bf16[528,128]{1,0:T(8,128)(2,1)S(1)}, u32[]{:S(2)}, u32[]{:S(2)}) collective-permute-start(bf16[528,128]{1,0:T(8,128)(2,1)S(1)} %get-tuple-element.32), channel_id=1, source_target_pairs={{4,8},{8,4},{12,16},{16,12},{20,24},{24,20},{5,9},{9,5},{13,17},{1... | collective-permute-start | bytes 405512 | tf_op jit(solution)/shard_map/ppermute | solution.py:490
  25.0 5.0 %collective-permute-start.9 = (bf16[528,128]{1,0:T(8,128)(2,1)S(1)}, bf16[528,128]{1,0:T(8,128)(2,1)S(1)}, u32[]{:S(2)}, u32[]{:S(2)}) collective-permute-start(bf16[528,128]{1,0:T(8,128)(2,1)S(1)} %get-tuple-element.33), channel_id=1, source_target_pairs={{0,4},{4,0},{8,12},{12,8},{16,20},{20,16},{24,28},{28,24},{1,5},{5... | collective-permute-start | bytes 405512 | tf_op jit(solution)/shard_map/ppermute | solution.py:491

commit v5 on v4

--- a/solution.py
+++ b/solution.py
@@ -58,20 +58,52 @@
     return (start - 2, start - 1, start + size, start + size + 1)
 
 
-def pack_sides(v_ref, after_ref, far_ref, near_ref):
+def columns(place, terrain_ref, eligible_ref):
+    nx, size = terrain_ref.shape
+    own = jnp.concatenate([terrain_ref[...].astype(F32), jnp.zeros((nx, LANES - size), F32)], 1)
+    ground = pltpu.roll(own, EDGE, 1)
+    return ground, lifted_layer(place, ground, eligible_ref, size)
+
+
+def lifted_layer(place, ground, eligible_ref, size):
+    y = iota(ground.shape, 1) + (place * size - EDGE)
+    flags = jnp.zeros(ground.shape, jnp.int32)
+    for b in range(eligible_ref.shape[1]):
+        inside = (y >= b * 128) & (y < (b + 1) * 128)
+        flags = jnp.where(inside, jnp.broadcast_to(eligible_ref[:, b : b + 1], ground.shape), flags)
+    return jnp.where(flags == 1, ground, -1.0)
+
+
+def pack_sides(v_ref, dust_ref, terrain_ref, eligible_ref, after_ref, far_ref, near_ref):
     del after_ref
-    nx = v_ref.shape[1]
+    ncomp, nx, ny, _ = v_ref.shape
+    size = dust_ref.shape[1]
     odd = lax.rem(lax.axis_index("horiz"), 2) == 1
-
+    ground, lifted = columns(lax.axis_index("vert"), terrain_ref, eligible_ref)
+    fill = jnp.zeros((14, LANES), F32)
+
+    def send(ref, x, inner):
+        for comp in range(ncomp):
+            ref[comp * ny : (comp + 1) * ny] = v_ref[comp, x].astype(BF)
+        at = ncomp * ny
+        ref[at : at + size] = dust_ref[x].astype(BF)
+        ref[at + size : at + 2 * size] = dust_ref[inner].astype(BF)
+        at = at + 2 * size
+        ref[at : at + 16] = jnp.concatenate([ground[x : x + 1], lifted[x : x + 1], fill], 0).astype(BF)
+
+    send_both(odd, send, near_ref, far_ref, nx)
+
+
+def send_both(odd, send, near_ref, far_ref, nx):
     @pl.when(odd)
     def _():
-        near_ref[...] = v_ref[:, 0].astype(BF)
-        far_ref[...] = v_ref[:, nx - 1].astype(BF)
+        send(near_ref, 0, 1)
+        send(far_ref, nx - 1, nx - 2)
 
     @pl.when(jnp.logical_not(odd))
     def _():
-        near_ref[...] = v_ref[:, nx - 1].astype(BF)
-        far_ref[...] = v_ref[:, 0].astype(BF)
+        send(near_ref, nx - 1, nx - 2)
+        send(far_ref, 0, 1)
 
 
 def start_all(copies):
@@ -127,11 +159,11 @@
                     out[j * size : (j + 1) * size] = buf[comp, x, t * size : (t + 1) * size, :].astype(BF)
                     for i, y in enumerate(halo_rows(t * size, size)):
                         if 0 <= y < ny:
-                            side[t, i * 16 + j : i * 16 + j + 1] = buf[comp, x, y : y + 1, :]
+                            side[t, i * nplane + j : i * nplane + j + 1] = buf[comp, x, y : y + 1, :]
         for t, out in enumerate(outs):
-            out[nplane * size : nplane * size + 64] = side[t].astype(BF)
+            out[nplane * size : nplane * (size + 4)] = side[t].astype(BF)
         wait_all(small)
-        write_ends(outs[1], nplane * size + 64, high, dusts[...], land[...], jnp.zeros((16, LANES), BF))
+        write_ends(outs[1], nplane * (size + 4), high, dusts[...], land[...], jnp.zeros((16, LANES), BF))
 
 
 def pack_ends(size, nstrips, v_ref, dust_ref, terrain_ref, after_ref, first_ref, second_ref, mine_ref, *refs):
@@ -199,7 +231,8 @@
         for half in range(nb):
             a = half * LANES
             span = slice(a, a + LANES)
-            near, far = (near_ref[comp, span, :].astype(F32), far_ref[comp, span, :].astype(F32))
+            rows = slice(comp * ny + a, comp * ny + a + LANES)
+            near, far = (near_ref[rows].astype(F32), far_ref[rows].astype(F32))
             below = jnp.where(odd, near, far)
             above = jnp.where(odd, far, near)
             for x in range(nx):
@@ -224,7 +257,7 @@
 
 
 def prepare(nstrips, *refs):
-    strips = refs[:1] + refs[nstrips - 1 : 0 : -1]
+    strips = refs[:nstrips]
     nlay = 1 + max(nstrips - 3, 0)
     lays = refs[nstrips : nstrips + nlay]
     dust_ref, terrain_ref, eligible_ref, first_ref, second_ref = refs[nstrips + nlay : nstrips + nlay + 5]
@@ -240,11 +273,11 @@
     for t in range(nstrips):
         @pl.when(place == t)
         def _(t=t):
-            beside = strips[t][nplane * size : nplane * size + 64].astype(F32)
+            beside = strips[t][nplane * size : nplane * (size + 4)].astype(F32)
             for j in range(nplane):
                 frame[j, EDGE : EDGE + size] = strips[t][j * size : (j + 1) * size].astype(F32)
                 for i, y in enumerate(halo_rows(EDGE, size)):
-                    frame[j, y : y + 1] = beside[i * 16 + j : i * 16 + j + 1]
+                    frame[j, y : y + 1] = beside[i * nplane + j : i * nplane + j + 1]
 
     face = first_ref.shape[0] - 32 - nx * EDGE
     over, under = sorted_ends(first_ref, second_ref, strips[1], face, nx * EDGE + 32)
@@ -288,71 +321,66 @@
     before = pltpu.roll(under[land], (EDGE - size) % LANES, 1)[:nx]
     after = pltpu.roll(over[land], (EDGE + size) % LANES, 1)[:nx]
     ground = jnp.where(lane < EDGE, before, jnp.where(lane < EDGE + size, pltpu.roll(own, EDGE, 1), after))
-    y = lane + (place * size - EDGE)
-    flags = jnp.zeros((nx, LANES), jnp.int32)
-    for b in range(eligible_ref.shape[1]):
-        inside = (y >= b * 128) & (y < (b + 1) * 128)
-        flags = jnp.where(inside, jnp.broadcast_to(eligible_ref[:, b : b + 1], (nx, LANES)), flags)
-    lifted = jnp.where(flags == 1, ground, -1.0)
+    lifted = lifted_layer(place, ground, eligible_ref, size)
     cols_ref[...] = jnp.zeros_like(cols_ref)
     cols_ref[:nx] = ground
     cols_ref[EDGE : EDGE + nx] = lifted
-    fill = jnp.zeros((16 - 2 * ncomp - 4, LANES), F32)
+    fill = jnp.zeros((16 - 2 * ncomp - 2, LANES), F32)
     strip, first, last = (slice(EDGE, EDGE + size), slice(EDGE - 1, EDGE), slice(EDGE + size, EDGE + size + 1))
 
     def send(ref, x, inner):
+        del inner
         for comp in range(ncomp):
             j = comp * nx + x
             ref[comp * size : (comp + 1) * size] = frame[j, strip].astype(BF)
             ref[(ncomp + comp) * size : (ncomp + comp + 1) * size] = wind_ref[j, strip].astype(BF)
         at = 2 * ncomp * size
-        ref[at : at + size] = conc_ref[x, strip].astype(BF)
-        ref[at + size : at + 2 * size] = conc_ref[inner, strip].astype(BF)
-        at = at + 2 * size
         rows = [frame[comp * nx + x, first] for comp in range(ncomp)] + [conc_ref[x, first]]
         rows += [frame[comp * nx + x, last] for comp in range(ncomp)] + [conc_ref[x, last]]
-        ref[at : at + 16] = jnp.concatenate(rows + [ground[x : x + 1], lifted[x : x + 1], fill], 0).astype(BF)
-
-    @pl.when(odd)
-    def _():
-        send(near_ref, 0, 1)
-        send(far_ref, nx - 1, nx - 2)
-
-    @pl.when(jnp.logical_not(odd))
-    def _():
-        send(near_ref, nx - 1, nx - 2)
-        send(far_ref, 0, 1)
-
-
-def transport(ny, nhoriz, wind_ref, edge_ref, conc_ref, cols_ref, far_ref, near_ref, out_ref):
+        ref[at : at + 16] = jnp.concatenate(rows + [fill], 0).astype(BF)
+
+    send_both(odd, send, near_ref, far_ref, nx)
+
+
+def transport(ny, nhoriz, wind_ref, edge_ref, conc_ref, cols_ref, face_far, face_near, far_ref, near_ref, out_ref):
     nx, size, nz = out_ref.shape
     ncomp = edge_ref.shape[0] // 2
     rows = size + 2 * EDGE
     column, place = (lax.axis_index("horiz"), lax.axis_index("vert"))
     odd = lax.rem(column, 2) == 1
-    here = 2 * (ncomp + 1) * size
     low = iota((EDGE, nz), 0)
 
-    def below(start, n):
-        return jnp.where(odd, near_ref[start : start + n].astype(F32), far_ref[start : start + n].astype(F32))
-
-    def above(start, n):
-        return jnp.where(odd, far_ref[start : start + n].astype(F32), near_ref[start : start + n].astype(F32))
+    def either(one, other, start, n):
+        return jnp.where(odd, one[start : start + n].astype(F32), other[start : start + n].astype(F32))
+
+    def framed(rows, ends=None, halo=0):
+        head, tail = (jnp.zeros((EDGE, nz), F32),) * 2
+        if ends is not None:
+            head = jnp.where(low == EDGE - 1, ends[halo : halo + 1], head)
+            tail = jnp.where(low == 0, ends[ncomp + 1 + halo : ncomp + 2 + halo], tail)
+        return jnp.concatenate([head, rows, tail], 0)
+
+    pairs_of = {"below": (near_ref, far_ref, face_near, face_far), "above": (far_ref, near_ref, face_far, face_near)}
+    ends, dusts, marks = ({}, {}, {})
+    for side, (one, other, face_one, face_other) in pairs_of.items():
+        ends[side] = either(one, other, 2 * ncomp * size, 16)
+        at = ncomp * ny
+        dusts[side] = (
+            framed(either(face_one, face_other, at, size), ends[side], ncomp),
+            framed(either(face_one, face_other, at + size, size)),
+        )
+        marks[side] = either(face_one, face_other, at + 2 * size, 16)
 
     def part(side, i, halo=None):
-        head, tail = (jnp.zeros((EDGE, nz), F32),) * 2
-        if halo is not None:
-            rest = ends[side]
-            head = jnp.where(low == EDGE - 1, rest[halo : halo + 1], head)
-            tail = jnp.where(low == 0, rest[ncomp + 1 + halo : ncomp + 2 + halo], tail)
-        return jnp.concatenate([head, side(i * size, size), tail], 0)
-
-    ends = {below: below(here, 16), above: above(here, 16)}
-    conc = [part(below, 2 * ncomp + 1), part(below, 2 * ncomp, ncomp)]
+        rows = either(*pairs_of[side][:2], i * size, size)
+        return framed(rows) if halo is None else framed(rows, ends[side], halo)
+
+    below, above = ("below", "above")
+    conc = [dusts[below][1], dusts[below][0]]
     conc += [conc_ref[x] for x in range(nx)]
-    conc += [part(above, 2 * ncomp, ncomp), part(above, 2 * ncomp + 1)]
-    table = jnp.concatenate([ends[below], cols_ref[...], ends[above], jnp.zeros((LANES - 48, LANES), F32)], 0).T[:rows]
-    mark = 2 * (ncomp + 1)
+    conc += [dusts[above][0], dusts[above][1]]
+    table = jnp.concatenate([marks[below], cols_ref[...], marks[above], jnp.zeros((LANES - 48, LANES), F32)], 0).T[:rows]
+    mark = 0
     ground = [mark] + [16 + x for x in range(nx)] + [32 + mark]
     lifted = [mark + 1] + [16 + EDGE + x for x in range(nx)] + [33 + mark]
     layer = iota((rows, nz), 1).astype(F32)
@@ -426,16 +454,16 @@
     anywhere = pl.BlockSpec(memory_space=pl.ANY)
 
     ends = ny // LANES * 16 + nx * EDGE + 32
-    strip = nplane * size + 64
+    strip = nplane * (size + 4)
     held = [pltpu.with_memory_space_constraint(array, pltpu.HBM) for array in (velocity, dust, terrain)]
     strips = call(
         functools.partial(pack_low, size),
-        [shaped(strip + (ends if t == 1 else 0), LANES) for t in range(nv)],
+        [shaped(strip + {1: ends, 2: 16}.get(t, 0), LANES) for t in range(nv)],
         "pack_low",
         [
             pltpu.VMEM((ncomp, nx, ny, nz), F32),
             pltpu.VMEM((16, ny), F32),
-            pltpu.VMEM((nv, 64, LANES), F32),
+            pltpu.VMEM((nv, 4 * nplane, LANES), F32),
             pltpu.VMEM((nx, EDGE, nz), F32),
             pltpu.VMEM((nx, size), jnp.int32),
             pltpu.SemaphoreType.DMA((nplane + 2,)),
@@ -443,8 +471,7 @@
         in_specs=[anywhere] * 3,
         out_specs=[VMEM] * nv,
     )(*held)
-    got = [lax.ppermute(strips[t], "vert", [(0, t)]) for t in range(nv - 1, 0, -1)]
-    got = [strips[0]] + got
+    got = [strips[0]] + [lax.ppermute(strips[t], "vert", [(0, t)]) for t in range(1, nv)]
 
     first, second, mine, *lays = call(
         functools.partial(pack_ends, size, nv),
@@ -459,8 +486,8 @@
     lays = [mine] + [lax.ppermute(lay, "vert", [(1, t + 3)]) for t, lay in enumerate(lays)]
 
     far, near = call(
-        pack_sides, [shaped(ncomp, ny, nz)] * 2, "pack_sides", cost=1 << 26, in_specs=[VMEM, anywhere]
-    )(velocity, lays[-1])
+        pack_sides, [shaped(ncomp * ny + 2 * size + 16, LANES)] * 2, "pack_sides", in_specs=[VMEM] * 4 + [anywhere]
+    )(velocity, dust, terrain, eligible, lays[-1])
     far = lax.ppermute(far, "horiz", far_pairs)
     near = lax.ppermute(near, "horiz", near_pairs)
 
@@ -471,9 +498,9 @@
         [pltpu.VMEM((ncomp, nx, ny, nz), F32), pltpu.SemaphoreType.DMA((ncomp,))],
         in_specs=[VMEM] * 6,
         out_specs=anywhere,
-    )(velocity, far, near, first, second, got[-1])
-
-    wire = (2 * ncomp + 2) * size + 16
+    )(velocity, far, near, first, second, got[1])
+
+    wire = 2 * ncomp * size + 16
     wind, conc, cols, mf, mn, edge = call(
         functools.partial(prepare, nv),
         [
@@ -493,7 +520,7 @@
         functools.partial(transport, ny, nh),
         jax.ShapeDtypeStruct(dust.shape, F32),
         "transport",
-    )(wind, edge, conc, cols, mf, mn)
+    )(wind, edge, conc, cols, far, near, mf, mn)
     return (velocity_next, dust_next)
 
 

time: 31.8 us -> 30.1 us (0.947)
  Pallas kernels: 6.86 us -> 5.48 us
  starting transfers between devices: 20.3 us -> 19.7 us
    pallas_call x2, Pallas kernels: 1.63 us -> 0.24 us  [the longest x1 0.14 us: local(): call(functools.partial(pack_low, size), [shaped(strip + {1: ends, 2: 16}....]
    ppermute x1, waiting for transfers between devices: 0.62 us -> 1.61 us  [local(): second = lax.ppermute(second, 'vert', pairs(nv, 1))]
    ppermute x1, waiting for transfers between devices: 2.82 us -> 2.12 us  [local(): mf = lax.ppermute(mf, 'horiz', far_pairs)]
    ppermute x1, starting transfers between devices: 4.89 us -> 4.26 us  [local(): second = lax.ppermute(second, 'vert', pairs(nv, 1))]
  transfers between devices with their start and end apart: 10 -> 10, of which waited for: 2 -> 2; matrix products, arithmetic and copies ran while one was open for 0% -> 0% of each run, Pallas kernels for 15% -> 13%
where the time goes in v5:
time: 30.1 us; the launch traced here: 29.8 us
  starting transfers between devices  19.7 us (65%)
  Pallas kernels  5.48 us (18%)
  waiting for transfers between devices  3.76 us (12%)
  between operations  0.83 us (3%)
    ppermute x1, starting transfers between devices, local(): far = lax.ppermute(far, 'horiz', far_pairs)  4.53 us
    ppermute x1, starting transfers between devices, local(): second = lax.ppermute(second, 'vert', pairs(nv, 1))  4.26 us
    ppermute x1, starting transfers between devices, local(): first = lax.ppermute(first, 'vert', pairs(nv, 0)[1:])  3.84 us
    ppermute x1, starting transfers between devices, local(): mf = lax.ppermute(mf, 'horiz', far_pairs)  3.03 us
    ppermute x3, starting transfers between devices, local(): lax.ppermute(strips[t], 'vert', [(0, t)])  2.77 us
    ppermute x1, waiting for transfers between devices, local(): mf = lax.ppermute(mf, 'horiz', far_pairs)  2.12 us
    pallas_call x1, Pallas kernels, local(): call(advance, jax.ShapeDtypeStruct(velocity.shape, F32), 'advance', [pltp...  2.1 us
    ppermute x1, waiting for transfers between devices, local(): second = lax.ppermute(second, 'vert', pairs(nv, 1))  1.61 us
  transfers between devices with their start and end apart: 10, of which 2 were waited for; matrix products, arithmetic and copies ran while one was open for 0% of the time, Pallas kernels for 13%

profile of v5, /device:TPU:19, one launch (start us, length us, event | category | flops | bytes accessed | tf_op | source)
XLA Modules:
  0.0 29.8 jit_solution(16845154270425283396)
XLA Ops:
  0.6 0.0 copy-start.2
  0.6 0.0 copy-start.1
  0.7 0.0 copy-start
  0.7 0.0 copy-start.3
  0.7 0.1 pack_low.1
  0.8 0.8 %collective-permute-start.5 = (bf16[912,128]{1,0:T(8,128)(2,1)S(1)}, bf16[912,128]{1,0:T(8,128)(2,1)S(1)}, u32[]{:S(2)}, u32[]{:S(2)}) collective-permute-start(bf16[912,128]{1,0:T(8,128)(2,1)S(1)} %get-tuple-element.24), channel_id=1, source_target_pairs={{0,1},{4,5},{8,9},{12,13},{16,17},{20,21},{24,25},{28,29}} | collective-permute-start | bytes 700424 | tf_op jit(solution)/shard_map/ppermute | solution.py:474
  1.6 1.3 %collective-permute-start.6 = (bf16[832,128]{1,0:T(8,128)(2,1)S(1)}, bf16[832,128]{1,0:T(8,128)(2,1)S(1)}, u32[]{:S(2)}, u32[]{:S(2)}) collective-permute-start(bf16[832,128]{1,0:T(8,128)(2,1)S(1)} %get-tuple-element.26), channel_id=1, source_target_pairs={{0,2},{4,6},{8,10},{12,14},{16,18},{20,22},{24,26},{28,30}} | collective-permute-start | bytes 638984 | tf_op jit(solution)/shard_map/ppermute | solution.py:474
  2.9 0.7 %collective-permute-start.7 = (bf16[816,128]{1,0:T(8,128)(2,1)S(1)}, bf16[816,128]{1,0:T(8,128)(2,1)S(1)}, u32[]{:S(2)}, u32[]{:S(2)}) collective-permute-start(bf16[816,128]{1,0:T(8,128)(2,1)S(1)} %get-tuple-element.18.after_ref), channel_id=1, source_target_pairs={{0,3},{4,7},{8,11},{12,15},{16,19},{20,23},{24,27},{28,31}} | collective-permute-start | bytes 626696 | tf_op jit(solution)/shard_map/ppermute | solution.py:474
  3.6 0.0 copy-done
  3.6 1.1 %pack_ends.1 = (bf16[96,128]{1,0:T(8,128)(2,1)S(1)}, bf16[96,128]{1,0:T(8,128)(2,1)S(1)}, bf16[3,16,128]{2,1,0:T(8,128)(2,1)S(1)}, bf16[16,128]{1,0:T(8,128)(2,1)S(1)}) custom-call(f32[3,4,256,128]{3,2,1,0:T(8,128)S(1)} %copy-done, f32[4,64,128]{2,1,0:T(8,128)} %refs_6_.1, s32[4,64]{1,0:T(4,128)} %refs_7_.1, bf16[816,128]{1,0:T(8,128)(2,1)S(1)} %get-tuple-element.18.after_ref), custom_call_target="tpu_custom_call" | custom-call | flops 1048576 | bytes 1048576 | tf_op jit(solution)/shard_map/pack_ends/pallas_call | solution.py:476
  4.7 0.7 %collective-permute-start = (bf16[16,128]{1,0:T(8,128)(2,1)S(1)}, bf16[16,128]{1,0:T(8,128)(2,1)S(1)}, u32[]{:S(2)}, u32[]{:S(2)}) collective-permute-start(bf16[16,128]{1,0:T(8,128)(2,1)S(1)} %get-tuple-element.19), channel_id=1, source_target_pairs={{1,3},{5,7},{9,11},{13,15},{17,19},{21,23},{25,27},{29,31}} | collective-permute-start | bytes 12296 | tf_op jit(solution)/shard_map/ppermute | solution.py:486
  5.4 3.8 %collective-permute-start.3 = (bf16[96,128]{1,0:T(8,128)(2,1)S(1)}, bf16[96,128]{1,0:T(8,128)(2,1)S(1)}, u32[]{:S(2)}, u32[]{:S(2)}) collective-permute-start(bf16[96,128]{1,0:T(8,128)(2,1)S(1)} %get-tuple-element.22), channel_id=1, source_target_pairs={{1,0},{2,3},{3,2},{5,4},{6,7},{7,6},{9,8},{10,11},{11,10},{13,12},... | collective-permute-start | bytes 73736 | tf_op jit(solution)/shard_map/ppermute | solution.py:484
  9.2 0.0 collective-permute-done.after_ref.refs_5_
  9.3 4.3 %collective-permute-start.4 = (bf16[96,128]{1,0:T(8,128)(2,1)S(1)}, bf16[96,128]{1,0:T(8,128)(2,1)S(1)}, u32[]{:S(2)}, u32[]{:S(2)}) collective-permute-start(bf16[96,128]{1,0:T(8,128)(2,1)S(1)} %get-tuple-element.23), channel_id=1, source_target_pairs={{1,2},{2,1},{5,6},{6,5},{9,10},{10,9},{13,14},{14,13},{17,18},{18,... | collective-permute-start | bytes 73736 | tf_op jit(solution)/shard_map/ppermute | solution.py:485
  13.5 0.0 copy-done.3
  13.5 0.1 copy.6.eligible_ref.refs_8_
  13.6 0.0 copy-done.2
  13.6 0.0 copy-done.1
  13.6 0.1 pack_sides.1
  13.7 0.0 collective-permute-done.3.first_ref.refs_9_
  13.8 4.5 %collective-permute-start.1 = (bf16[912,128]{1,0:T(8,128)(2,1)S(1)}, bf16[912,128]{1,0:T(8,128)(2,1)S(1)}, u32[]{:S(2)}, u32[]{:S(2)}) collective-permute-start(bf16[912,128]{1,0:T(8,128)(2,1)S(1)} %get-tuple-element.20), channel_id=1, source_target_pairs={{4,8},{8,4},{12,16},{16,12},{20,24},{24,20},{5,9},{9,5},{13,17},{1... | collective-permute-start | bytes 700424 | tf_op jit(solution)/shard_map/ppermute | solution.py:491
  18.3 1.6 %collective-permute-done.4.second_ref.refs_10_ = bf16[96,128]{1,0:T(8,128)(2,1)S(1)} collective-permute-done((bf16[96,128]{1,0:T(8,128)(2,1)S(1)}, bf16[96,128]{1,0:T(8,128)(2,1)S(1)}, u32[]{:S(2)}, u32[]{:S(2)}) %collective-permute-start.4) | collective-permute-done | bytes 24608 | tf_op jit(solution)/shard_map/ppermute | solution.py:485
  19.9 0.5 %collective-permute-start.2 = (bf16[912,128]{1,0:T(8,128)(2,1)S(1)}, bf16[912,128]{1,0:T(8,128)(2,1)S(1)}, u32[]{:S(2)}, u32[]{:S(2)}) collective-permute-start(bf16[912,128]{1,0:T(8,128)(2,1)S(1)} %get-tuple-element.21), channel_id=1, source_target_pairs={{0,4},{4,0},{8,12},{12,8},{16,20},{20,16},{24,28},{28,24},{1,5},{5... | collective-permute-start | bytes 700424 | tf_op jit(solution)/shard_map/ppermute | solution.py:492
  20.4 0.0 collective-permute-done.7.refs_3_
  20.4 0.0 collective-permute-done.6.refs_2_
  20.4 0.0 collective-permute-done.5.strip_ref.refs_1_
  20.4 0.6 %prepare.1 = (f32[12,80,128]{2,1,0:T(8,128)S(1)}, f32[4,80,128]{2,1,0:T(8,128)S(1)}, f32[16,128]{1,0:T(8,128)S(1)}, bf16[400,128]{1,0:T(8,128)(2,1)S(1)}, bf16[4...) custom-call(bf16[816,128]{1,0:T(8,128)(2,1)S(1)} %get-tuple-element.25.refs_0_, ...), custom_call_target="tpu_custom_call" | custom-call | flops 1048576 | bytes 1048576 | tf_op jit(solution)/shard_map/prepare/pallas_call | solution.py:504
  21.0 3.0 %collective-permute-start.8 = (bf16[400,128]{1,0:T(8,128)(2,1)S(1)}, bf16[400,128]{1,0:T(8,128)(2,1)S(1)}, u32[]{:S(2)}, u32[]{:S(2)}) collective-permute-start(bf16[400,128]{1,0:T(8,128)(2,1)S(1)} %get-tuple-element.32), channel_id=1, source_target_pairs={{4,8},{8,4},{12,16},{16,12},{20,24},{24,20},{5,9},{9,5},{13,17},{1... | collective-permute-start | bytes 307208 | tf_op jit(solution)/shard_map/ppermute | solution.py:517
  24.0 0.1 collective-permute-start.9
  24.1 0.0 collective-permute-done.1.far_ref.face_far
  24.1 0.0 collective-permute-done.2.near_ref.face_near
  24.1 2.1 %advance.1 = f32[3,4,256,128]{3,2,1,0:T(8,128)} custom-call(f32[3,4,256,128]{3,2,1,0:T(8,128)S(1)} %copy-done, bf16[912,128]{1,0:T(8,128)(2,1)S(1)} %collective-permute-done.1.far_ref.face_far, bf16[912,128]{1,0:T(8,128)(2,1)S(1)} %collective-permute-done.2.near_ref.face_near, bf16[96,128]{1,0:T(8,128)(2,1)S(1)} %collective-permute-done.3.first_ref.refs_9_, ...), custom_call_target="tpu_custom_call" | custom-call | flops 1048576 | bytes 1048576 | tf_op jit(solution)/shard_map/advance/pallas_call | solution.py:494
  26.2 2.1 %collective-permute-done.8.far_ref = bf16[400,128]{1,0:T(8,128)(2,1)S(1)} collective-permute-done((bf16[400,128]{1,0:T(8,128)(2,1)S(1)}, bf16[400,128]{1,0:T(8,128)(2,1)S(1)}, u32[]{:S(2)}, u32[]{:S(2)}) %collective-permute-start.8) | collective-permute-done | bytes 102432 | tf_op jit(solution)/shard_map/ppermute | solution.py:517
  28.3 0.0 collective-permute-done.9.near_ref
  28.4 1.5 %transport.1 = f32[4,64,128]{2,1,0:T(8,128)} custom-call(f32[12,80,128]{2,1,0:T(8,128)S(1)} %get-tuple-element.28.wind_ref, bf16[6,80,128]{2,1,0:T(8,128)(2,1)S(1)} %get-tuple-element.29.edge_ref, f32[4,80,128]{2,1,0:T(8,128)S(1)} %get-tuple-element.30.conc_ref, f32[16,128]{1,0:T(8,128)S(1)} %get-tuple-element.31.cols_ref, ...), custom_call_target="tpu_custom_call" | custom-call | flops 1048576 | bytes 1048576 | tf_op jit(solution)/shard_map/transport/pallas_call | solution.py:519
Async XLA Ops:
  0.6 13.0 %copy-start.2 = (s32[4,64]{1,0:T(4,128)S(1)}, s32[4,64]{1,0:T(4,128)}, u32[]{:S(2)}) copy-start(s32[4,64]{1,0:T(4,128)} %refs_7_.1) | copy-start | bytes 3076
  0.6 13.0 %copy-start.1 = (f32[4,64,128]{2,1,0:T(8,128)S(1)}, f32[4,64,128]{2,1,0:T(8,128)}, u32[]{:S(2)}) copy-start(f32[4,64,128]{2,1,0:T(8,128)} %refs_6_.1) | copy-start | bytes 393220
  0.7 3.0 %copy-start = (f32[3,4,256,128]{3,2,1,0:T(8,128)S(1)}, f32[3,4,256,128]{3,2,1,0:T(8,128)}, u32[]{:S(2)}) copy-start(f32[3,4,256,128]{3,2,1,0:T(8,128)} %v_ref.7) | copy-start | bytes 4718596
  0.7 12.9 %copy-start.3 = (s32[4,2]{0,1:T(2,128)S(1)}, s32[4,2]{0,1:T(2,128)}, u32[]{:S(2)}) copy-start(s32[4,2]{0,1:T(2,128)} %param.6) | copy-start | bytes 100
  0.8 19.6 %collective-permute-start.5 = (bf16[912,128]{1,0:T(8,128)(2,1)S(1)}, bf16[912,128]{1,0:T(8,128)(2,1)S(1)}, u32[]{:S(2)}, u32[]{:S(2)}) collective-permute-start(bf16[912,128]{1,0:T(8,128)(2,1)S(1)} %get-tuple-element.24), channel_id=1, source_target_pairs={{0,1},{4,5},{8,9},{12,13},{16,17},{20,21},{24,25},{28,29}} | collective-permute-start | bytes 700424 | tf_op jit(solution)/shard_map/ppermute | solution.py:474
  1.6 18.8 %collective-permute-start.6 = (bf16[832,128]{1,0:T(8,128)(2,1)S(1)}, bf16[832,128]{1,0:T(8,128)(2,1)S(1)}, u32[]{:S(2)}, u32[]{:S(2)}) collective-permute-start(bf16[832,128]{1,0:T(8,128)(2,1)S(1)} %get-tuple-element.26), channel_id=1, source_target_pairs={{0,2},{4,6},{8,10},{12,14},{16,18},{20,22},{24,26},{28,30}} | collective-permute-start | bytes 638984 | tf_op jit(solution)/shard_map/ppermute | solution.py:474
  2.9 17.5 %collective-permute-start.7 = (bf16[816,128]{1,0:T(8,128)(2,1)S(1)}, bf16[816,128]{1,0:T(8,128)(2,1)S(1)}, u32[]{:S(2)}, u32[]{:S(2)}) collective-permute-start(bf16[816,128]{1,0:T(8,128)(2,1)S(1)} %get-tuple-element.18.after_ref), channel_id=1, source_target_pairs={{0,3},{4,7},{8,11},{12,15},{16,19},{20,23},{24,27},{28,31}} | collective-permute-start | bytes 626696 | tf_op jit(solution)/shard_map/ppermute | solution.py:474
  4.7 4.5 %collective-permute-start = (bf16[16,128]{1,0:T(8,128)(2,1)S(1)}, bf16[16,128]{1,0:T(8,128)(2,1)S(1)}, u32[]{:S(2)}, u32[]{:S(2)}) collective-permute-start(bf16[16,128]{1,0:T(8,128)(2,1)S(1)} %get-tuple-element.19), channel_id=1, source_target_pairs={{1,3},{5,7},{9,11},{13,15},{17,19},{21,23},{25,27},{29,31}} | collective-permute-start | bytes 12296 | tf_op jit(solution)/shard_map/ppermute | solution.py:486
  5.4 8.3 %collective-permute-start.3 = (bf16[96,128]{1,0:T(8,128)(2,1)S(1)}, bf16[96,128]{1,0:T(8,128)(2,1)S(1)}, u32[]{:S(2)}, u32[]{:S(2)}) collective-permute-start(bf16[96,128]{1,0:T(8,128)(2,1)S(1)} %get-tuple-element.22), channel_id=1, source_target_pairs={{1,0},{2,3},{3,2},{5,4},{6,7},{7,6},{9,8},{10,11},{11,10},{13,12},... | collective-permute-start | bytes 73736 | tf_op jit(solution)/shard_map/ppermute | solution.py:484
  9.3 10.7 %collective-permute-start.4 = (bf16[96,128]{1,0:T(8,128)(2,1)S(1)}, bf16[96,128]{1,0:T(8,128)(2,1)S(1)}, u32[]{:S(2)}, u32[]{:S(2)}) collective-permute-start(bf16[96,128]{1,0:T(8,128)(2,1)S(1)} %get-tuple-element.23), channel_id=1, source_target_pairs={{1,2},{2,1},{5,6},{6,5},{9,10},{10,9},{13,14},{14,13},{17,18},{18,... | collective-permute-start | bytes 73736 | tf_op jit(solution)/shard_map/ppermute | solution.py:485
  13.8 10.3 %collective-permute-start.1 = (bf16[912,128]{1,0:T(8,128)(2,1)S(1)}, bf16[912,128]{1,0:T(8,128)(2,1)S(1)}, u32[]{:S(2)}, u32[]{:S(2)}) collective-permute-start(bf16[912,128]{1,0:T(8,128)(2,1)S(1)} %get-tuple-element.20), channel_id=1, source_target_pairs={{4,8},{8,4},{12,16},{16,12},{20,24},{24,20},{5,9},{9,5},{13,17},{1... | collective-permute-start | bytes 700424 | tf_op jit(solution)/shard_map/ppermute | solution.py:491
  19.9 4.2 %collective-permute-start.2 = (bf16[912,128]{1,0:T(8,128)(2,1)S(1)}, bf16[912,128]{1,0:T(8,128)(2,1)S(1)}, u32[]{:S(2)}, u32[]{:S(2)}) collective-permute-start(bf16[912,128]{1,0:T(8,128)(2,1)S(1)} %get-tuple-element.21), channel_id=1, source_target_pairs={{0,4},{4,0},{8,12},{12,8},{16,20},{20,16},{24,28},{28,24},{1,5},{5... | collective-permute-start | bytes 700424 | tf_op jit(solution)/shard_map/ppermute | solution.py:492
  21.0 7.4 %collective-permute-start.8 = (bf16[400,128]{1,0:T(8,128)(2,1)S(1)}, bf16[400,128]{1,0:T(8,128)(2,1)S(1)}, u32[]{:S(2)}, u32[]{:S(2)}) collective-permute-start(bf16[400,128]{1,0:T(8,128)(2,1)S(1)} %get-tuple-element.32), channel_id=1, source_target_pairs={{4,8},{8,4},{12,16},{16,12},{20,24},{24,20},{5,9},{9,5},{13,17},{1... | collective-permute-start | bytes 307208 | tf_op jit(solution)/shard_map/ppermute | solution.py:517
  24.0 4.3 %collective-permute-start.9 = (bf16[400,128]{1,0:T(8,128)(2,1)S(1)}, bf16[400,128]{1,0:T(8,128)(2,1)S(1)}, u32[]{:S(2)}, u32[]{:S(2)}) collective-permute-start(bf16[400,128]{1,0:T(8,128)(2,1)S(1)} %get-tuple-element.33), channel_id=1, source_target_pairs={{0,4},{4,0},{8,12},{12,8},{16,20},{20,16},{24,28},{28,24},{1,5},{5... | collective-permute-start | bytes 307208 | tf_op jit(solution)/shard_map/ppermute | solution.py:518

commit v6 on v5

--- a/solution.py
+++ b/solution.py
@@ -54,6 +54,10 @@
                 out[j : j + 1, span] = rows[i : i + 1]
 
 
+def beside_rows(nplane, t, nstrips):
+    return -(-2 * nplane // 16) * 16 if t == nstrips - 1 else 4 * nplane
+
+
 def halo_rows(start, size):
     return (start - 2, start - 1, start + size, start + size + 1)
 
@@ -117,18 +121,16 @@
         copy.wait()
 
 
-def write_ends(ref, at, face, dust, land, layer):
+def write_ends(ref, at, face, dust, land, layer=None):
     nx, size = land.shape
-    ny = face.shape[1]
     terrain = jnp.concatenate([land.astype(F32), jnp.zeros((nx, LANES - size), F32)], 1)
-    terrain = jnp.concatenate([terrain, jnp.zeros((16 - nx, LANES), F32)], 0)
-    for half in range(ny // LANES):
-        ref[at + half * 16 : at + half * 16 + 16] = face[:, half * LANES : (half + 1) * LANES].astype(BF)
-    at = at + ny // LANES * 16
-    ref[at : at + nx * EDGE] = dust.reshape(nx * EDGE, LANES).astype(BF)
-    at = at + nx * EDGE
-    ref[at : at + 16] = terrain.astype(BF)
-    ref[at + 16 : at + 32] = layer
+    fill = jnp.zeros((16 - 3 * nx, LANES), F32)
+    for half in range(face.shape[1] // LANES):
+        ref[at : at + 16] = face[:, half * LANES : (half + 1) * LANES].astype(BF)
+        at = at + 16
+    ref[at : at + 16] = jnp.concatenate([dust[x] for x in range(nx)] + [terrain, fill], 0).astype(BF)
+    if layer is not None:
+        ref[at + 16 : at + 32] = layer
 
 
 def pack_low(size, v_ref, dust_ref, terrain_ref, *refs):
@@ -161,9 +163,10 @@
                         if 0 <= y < ny:
                             side[t, i * nplane + j : i * nplane + j + 1] = buf[comp, x, y : y + 1, :]
         for t, out in enumerate(outs):
-            out[nplane * size : nplane * (size + 4)] = side[t].astype(BF)
+            count = beside_rows(nplane, t, len(outs))
+            out[nplane * size : nplane * size + count] = side[t, :count].astype(BF)
         wait_all(small)
-        write_ends(outs[1], nplane * (size + 4), high, dusts[...], land[...], jnp.zeros((16, LANES), BF))
+        write_ends(outs[1], nplane * (size + 4), high, dusts[:, EDGE - 2 :], land[...])
 
 
 def pack_ends(size, nstrips, v_ref, dust_ref, terrain_ref, after_ref, first_ref, second_ref, mine_ref, *refs):
@@ -192,25 +195,35 @@
         part = jnp.where((row >= 0) & (row < ny), moved[:, :LANES], 0.0).astype(BF)
         if t < 3:
             mine_ref[t] = part
+        elif t == 3:
+            second_ref[second_ref.shape[0] - 16 :] = part
         else:
-            lays[t - 3][...] = part
+            lays[t - 4][...] = part
     wait_all(small)
 
     @pl.when(odd)
     def _():
-        write_ends(first_ref, 0, low, dusts[0], land[...], mine_ref[0])
-        write_ends(second_ref, 0, high, dusts[1], land[...], mine_ref[2])
+        write_ends(first_ref, 0, low, dusts[0, :, :2], land[...], mine_ref[0])
+        write_ends(second_ref, 0, high, dusts[1, :, EDGE - 2 :], land[...], mine_ref[2])
 
     @pl.when(jnp.logical_not(odd))
     def _():
-        write_ends(first_ref, 0, high, dusts[1], land[...], mine_ref[2])
-        write_ends(second_ref, 0, low, dusts[0], land[...], mine_ref[0])
+        write_ends(first_ref, 0, high, dusts[1, :, EDGE - 2 :], land[...], mine_ref[2])
+        write_ends(second_ref, 0, low, dusts[0, :, :2], land[...], mine_ref[0])
+
+
+def relay(base_ref, second_ref, first_ref):
+    first_ref[...] = base_ref[...]
+
+    @pl.when(lax.axis_index("vert") == 2)
+    def _():
+        first_ref[first_ref.shape[0] - 16 :] = second_ref[second_ref.shape[0] - 16 :]
 
 
 def sorted_ends(first_ref, second_ref, strip_ref, start, n):
     place = lax.axis_index("vert")
     odd = lax.rem(place, 2) == 1
-    base = strip_ref.shape[0] - first_ref.shape[0] + start
+    base = strip_ref.shape[0] - first_ref.shape[0] + 16 + start
     first, second = (first_ref[start : start + n].astype(F32), second_ref[start : start + n].astype(F32))
     below = jnp.where(place == 1, strip_ref[base : base + n].astype(F32), jnp.where(odd, first, second))
     return (jnp.where(odd, second, first), below)
@@ -258,7 +271,7 @@
 
 def prepare(nstrips, *refs):
     strips = refs[:nstrips]
-    nlay = 1 + max(nstrips - 3, 0)
+    nlay = 1 + max(nstrips - 4, 0)
     lays = refs[nstrips : nstrips + nlay]
     dust_ref, terrain_ref, eligible_ref, first_ref, second_ref = refs[nstrips + nlay : nstrips + nlay + 5]
     wind_ref, conc_ref, cols_ref, far_ref, near_ref, edge_ref, frame = refs[nstrips + nlay + 5 :]
@@ -273,18 +286,20 @@
     for t in range(nstrips):
         @pl.when(place == t)
         def _(t=t):
-            beside = strips[t][nplane * size : nplane * (size + 4)].astype(F32)
+            count = beside_rows(nplane, t, nstrips)
+            beside = strips[t][nplane * size : nplane * size + count].astype(F32)
             for j in range(nplane):
                 frame[j, EDGE : EDGE + size] = strips[t][j * size : (j + 1) * size].astype(F32)
-                for i, y in enumerate(halo_rows(EDGE, size)):
+                for i, y in enumerate(halo_rows(EDGE, size)[: count // nplane]):
                     frame[j, y : y + 1] = beside[i * nplane + j : i * nplane + j + 1]
 
-    face = first_ref.shape[0] - 32 - nx * EDGE
-    over, under = sorted_ends(first_ref, second_ref, strips[1], face, nx * EDGE + 32)
+    face = first_ref.shape[0] - 32
+    over, under = sorted_ends(first_ref, second_ref, strips[1], face, 16)
     zero = jnp.zeros((16, LANES), F32)
-    layer = jnp.where(place == 0, over[nx * EDGE + 16 :], zero)
+    layer = jnp.where(place == 0, first_ref[face + 16 : face + 32].astype(F32), zero)
     layer = layer + jnp.where(place == 1, lays[0][min(1, nstrips - 1)].astype(F32), zero)
-    layer = layer + jnp.where(place == 2, under[nx * EDGE + 16 :], zero)
+    layer = layer + jnp.where(place == 2, second_ref[face + 16 : face + 32].astype(F32), zero)
+    layer = layer + jnp.where(place == 3, first_ref[face + 16 : face + 32].astype(F32), zero)
     for got in lays[1:]:
         layer = layer + got[...].astype(F32)
     layer = jnp.concatenate([layer, jnp.zeros((LANES - 16, LANES), F32)], 0)
@@ -311,15 +326,18 @@
                 edge_ref[comp] = raw
             if x == nx - 1:
                 edge_ref[ncomp + comp] = raw
+    row = iota((EDGE, nz), 0)
     for x in range(nx):
-        before, after = (under[x * EDGE : (x + 1) * EDGE], over[x * EDGE : (x + 1) * EDGE])
+        one, two = (slice(2 * x, 2 * x + 1), slice(2 * x + 1, 2 * x + 2))
+        before = jnp.where(row == EDGE - 2, under[one], jnp.where(row == EDGE - 1, under[two], 0.0))
+        after = jnp.where(row == 0, over[one], jnp.where(row == 1, over[two], 0.0))
         conc_ref[x] = jnp.concatenate([before, dust_ref[x], after], 0)
     lane = iota((nx, LANES), 1)
     own = terrain_ref[...].astype(F32)
     own = jnp.concatenate([own, jnp.zeros((nx, LANES - size), F32)], 1)
-    land = slice(nx * EDGE, nx * EDGE + 16)
-    before = pltpu.roll(under[land], (EDGE - size) % LANES, 1)[:nx]
-    after = pltpu.roll(over[land], (EDGE + size) % LANES, 1)[:nx]
+    land = slice(2 * nx, 3 * nx)
+    before = pltpu.roll(under, (EDGE - size) % LANES, 1)[land]
+    after = pltpu.roll(over, (EDGE + size) % LANES, 1)[land]
     ground = jnp.where(lane < EDGE, before, jnp.where(lane < EDGE + size, pltpu.roll(own, EDGE, 1), after))
     lifted = lifted_layer(place, ground, eligible_ref, size)
     cols_ref[...] = jnp.zeros_like(cols_ref)
@@ -453,12 +471,11 @@
     nplane = ncomp * nx
     anywhere = pl.BlockSpec(memory_space=pl.ANY)
 
-    ends = ny // LANES * 16 + nx * EDGE + 32
-    strip = nplane * (size + 4)
+    ends = ny // LANES * 16 + 32
     held = [pltpu.with_memory_space_constraint(array, pltpu.HBM) for array in (velocity, dust, terrain)]
     strips = call(
         functools.partial(pack_low, size),
-        [shaped(strip + {1: ends, 2: 16}.get(t, 0), LANES) for t in range(nv)],
+        [shaped(nplane * size + beside_rows(nplane, t, nv) + (ends - 16 if t == 1 else 0), LANES) for t in range(nv)],
         "pack_low",
         [
             pltpu.VMEM((ncomp, nx, ny, nz), F32),
@@ -475,19 +492,20 @@
 
     first, second, mine, *lays = call(
         functools.partial(pack_ends, size, nv),
-        [shaped(ends, LANES)] * 2 + [shaped(3, 16, LANES)] + [shaped(16, LANES)] * (nv - 3),
+        [shaped(ends, LANES), shaped(ends + 16, LANES), shaped(3, 16, LANES)] + [shaped(16, LANES)] * (nv - 4),
         "pack_ends",
         [pltpu.VMEM((16, ny), F32)] * 2
         + [pltpu.VMEM((2, nx, EDGE, nz), F32), pltpu.VMEM((nx, size), jnp.int32), pltpu.SemaphoreType.DMA((3,))],
         in_specs=[VMEM] + [anywhere] * 3,
     )(velocity, *held[1:], strips[-1])
+    second = lax.ppermute(second, "vert", pairs(nv, 1))
+    first = call(relay, shaped(ends, LANES), "relay")(first, second)
     first = lax.ppermute(first, "vert", pairs(nv, 0)[1:])
-    second = lax.ppermute(second, "vert", pairs(nv, 1))
-    lays = [mine] + [lax.ppermute(lay, "vert", [(1, t + 3)]) for t, lay in enumerate(lays)]
+    lays = [mine] + [lax.ppermute(lay, "vert", [(1, t + 4)]) for t, lay in enumerate(lays)]
 
     far, near = call(
         pack_sides, [shaped(ncomp * ny + 2 * size + 16, LANES)] * 2, "pack_sides", in_specs=[VMEM] * 4 + [anywhere]
-    )(velocity, dust, terrain, eligible, lays[-1])
+    )(velocity, dust, terrain, eligible, second)
     far = lax.ppermute(far, "horiz", far_pairs)
     near = lax.ppermute(near, "horiz", near_pairs)
 

time: 30.1 us -> 28.1 us (0.934)
  the two profiles are of different devices: /device:TPU:19 before, /device:TPU:28 now
where the time goes in v6:
time: 28.1 us; the launch traced here: 27.8 us
  starting transfers between devices  18.1 us (64%)
  Pallas kernels  5.51 us (20%)
  waiting for transfers between devices  3.22 us (11%)
  between operations  0.8 us (3%)
    ppermute x1, starting transfers between devices, local(): first = lax.ppermute(first, 'vert', pairs(nv, 0)[1:])  7.54 us
    ppermute x3, starting transfers between devices, local(): lax.ppermute(strips[t], 'vert', [(0, t)])  2.77 us
    pallas_call x1, Pallas kernels, local(): call(advance, jax.ShapeDtypeStruct(velocity.shape, F32), 'advance', [pltp...  2.11 us
    ppermute x1, starting transfers between devices, local(): far = lax.ppermute(far, 'horiz', far_pairs)  1.92 us
    ppermute x1, starting transfers between devices, local(): mf = lax.ppermute(mf, 'horiz', far_pairs)  1.92 us
    ppermute x3, waiting for transfers between devices, local(): lax.ppermute(strips[t], 'vert', [(0, t)])  1.84 us
    ppermute x1, starting transfers between devices, local(): near = lax.ppermute(near, 'horiz', near_pairs)  1.66 us
    ppermute x1, starting transfers between devices, local(): mn = lax.ppermute(mn, 'horiz', near_pairs)  1.66 us
  transfers between devices with their start and end apart: 9, of which 3 were waited for; matrix products, arithmetic and copies ran while one was open for 0% of the time, Pallas kernels for 14%

profile of v6, /device:TPU:28, one launch (start us, length us, event | category | flops | bytes accessed | tf_op | source)
XLA Modules:
  0.0 27.8 jit_solution(7351358849536868010)
XLA Ops:
  0.6 0.0 copy-start.2
  0.6 0.0 copy-start.1
  0.7 0.0 copy-start
  0.7 0.0 copy-start.3
  0.7 0.1 pack_low.1
  0.8 0.8 %collective-permute-start.4 = (bf16[864,128]{1,0:T(8,128)(2,1)S(1)}, bf16[864,128]{1,0:T(8,128)(2,1)S(1)}, u32[]{:S(2)}, u32[]{:S(2)}) collective-permute-start(bf16[864,128]{1,0:T(8,128)(2,1)S(1)} %get-tuple-element.22), channel_id=1, source_target_pairs={{0,1},{4,5},{8,9},{12,13},{16,17},{20,21},{24,25},{28,29}} | collective-permute-start | bytes 663560 | tf_op jit(solution)/shard_map/ppermute | solution.py:491
  1.6 0.7 %collective-permute-start.5 = (bf16[816,128]{1,0:T(8,128)(2,1)S(1)}, bf16[816,128]{1,0:T(8,128)(2,1)S(1)}, u32[]{:S(2)}, u32[]{:S(2)}) collective-permute-start(bf16[816,128]{1,0:T(8,128)(2,1)S(1)} %get-tuple-element.24), channel_id=1, source_target_pairs={{0,2},{4,6},{8,10},{12,14},{16,18},{20,22},{24,26},{28,30}} | collective-permute-start | bytes 626696 | tf_op jit(solution)/shard_map/ppermute | solution.py:491
  2.3 1.3 %collective-permute-start.6 = (bf16[800,128]{1,0:T(8,128)(2,1)S(1)}, bf16[800,128]{1,0:T(8,128)(2,1)S(1)}, u32[]{:S(2)}, u32[]{:S(2)}) collective-permute-start(bf16[800,128]{1,0:T(8,128)(2,1)S(1)} %get-tuple-element.17.after_ref), channel_id=1, source_target_pairs={{0,3},{4,7},{8,11},{12,15},{16,19},{20,23},{24,27},{28,31}} | collective-permute-start | bytes 614408 | tf_op jit(solution)/shard_map/ppermute | solution.py:491
  3.6 0.0 copy-done
  3.6 1.1 %pack_ends.1 = (bf16[64,128]{1,0:T(8,128)(2,1)S(1)}, bf16[80,128]{1,0:T(8,128)(2,1)S(1)}, bf16[3,16,128]{2,1,0:T(8,128)(2,1)S(1)}) custom-call(f32[3,4,256,128]{3,2,1,0:T(8,128)S(1)} %copy-done, f32[4,64,128]{2,1,0:T(8,128)} %refs_5_.1, s32[4,64]{1,0:T(4,128)} %refs_6_.1, bf16[800,128]{1,0:T(8,128)(2,1)S(1)} %get-tuple-element.17.after_ref), custom_call_target="tpu_custom_call" | custom-call | flops 1048576 | bytes 1048576 | tf_op jit(solution)/shard_map/pack_ends/pallas_call | solution.py:493
  4.7 0.7 %collective-permute-start = (bf16[80,128]{1,0:T(8,128)(2,1)S(1)}, bf16[80,128]{1,0:T(8,128)(2,1)S(1)}, u32[]{:S(2)}, u32[]{:S(2)}) collective-permute-start(bf16[80,128]{1,0:T(8,128)(2,1)S(1)} %get-tuple-element.18), channel_id=1, source_target_pairs={{1,2},{2,1},{5,6},{6,5},{9,10},{10,9},{13,14},{14,13},{17,18},{18,... | collective-permute-start | bytes 61448 | tf_op jit(solution)/shard_map/ppermute | solution.py:501
  5.4 0.0 collective-permute-done.after_ref.second_ref.refs_9_
  5.4 7.5 %collective-permute-start.3 = (bf16[64,128]{1,0:T(8,128)(2,1)S(1)}, bf16[64,128]{1,0:T(8,128)(2,1)S(1)}, u32[]{:S(2)}, u32[]{:S(2)}) collective-permute-start(bf16[64,128]{1,0:T(8,128)(2,1)S(1)} %relay.1), channel_id=1, source_target_pairs={{1,0},{2,3},{3,2},{5,4},{6,7},{7,6},{9,8},{10,11},{11,10},{13,12},... | collective-permute-start | bytes 49160 | tf_op jit(solution)/shard_map/ppermute | solution.py:503
  13.0 0.0 copy-done.3
  13.0 0.1 copy.6.eligible_ref.refs_7_
  13.1 0.0 copy-done.2
  13.1 0.0 copy-done.1
  13.1 0.1 pack_sides.1
  13.2 1.9 %collective-permute-start.1 = (bf16[912,128]{1,0:T(8,128)(2,1)S(1)}, bf16[912,128]{1,0:T(8,128)(2,1)S(1)}, u32[]{:S(2)}, u32[]{:S(2)}) collective-permute-start(bf16[912,128]{1,0:T(8,128)(2,1)S(1)} %get-tuple-element.19), channel_id=1, source_target_pairs={{4,8},{8,4},{12,16},{16,12},{20,24},{24,20},{5,9},{9,5},{13,17},{1... | collective-permute-start | bytes 700424 | tf_op jit(solution)/shard_map/ppermute | solution.py:509
  15.1 0.0 collective-permute-done.3.first_ref.refs_8_
  15.2 1.7 %collective-permute-start.2 = (bf16[912,128]{1,0:T(8,128)(2,1)S(1)}, bf16[912,128]{1,0:T(8,128)(2,1)S(1)}, u32[]{:S(2)}, u32[]{:S(2)}) collective-permute-start(bf16[912,128]{1,0:T(8,128)(2,1)S(1)} %get-tuple-element.20), channel_id=1, source_target_pairs={{0,4},{4,0},{8,12},{12,8},{16,20},{20,16},{24,28},{28,24},{1,5},{5... | collective-permute-start | bytes 700424 | tf_op jit(solution)/shard_map/ppermute | solution.py:510
  16.8 1.8 %collective-permute-done.6.refs_3_ = bf16[800,128]{1,0:T(8,128)(2,1)S(1)} collective-permute-done((bf16[800,128]{1,0:T(8,128)(2,1)S(1)}, bf16[800,128]{1,0:T(8,128)(2,1)S(1)}, u32[]{:S(2)}, u32[]{:S(2)}) %collective-permute-start.6) | collective-permute-done | bytes 204832 | tf_op jit(solution)/shard_map/ppermute | solution.py:491
  18.7 0.0 collective-permute-done.5.refs_2_
  18.7 0.0 collective-permute-done.4.strip_ref.refs_1_
  18.7 0.5 %prepare.1 = (f32[12,80,128]{2,1,0:T(8,128)S(1)}, f32[4,80,128]{2,1,0:T(8,128)S(1)}, f32[16,128]{1,0:T(8,128)S(1)}, bf16[400,128]{1,0:T(8,128)(2,1)S(1)}, bf16[4...) custom-call(bf16[816,128]{1,0:T(8,128)(2,1)S(1)} %get-tuple-element.23.refs_0_, ...), custom_call_target="tpu_custom_call" | custom-call | flops 1048576 | bytes 1048576 | tf_op jit(solution)/shard_map/prepare/pallas_call | solution.py:522
  19.2 1.9 %collective-permute-start.7 = (bf16[400,128]{1,0:T(8,128)(2,1)S(1)}, bf16[400,128]{1,0:T(8,128)(2,1)S(1)}, u32[]{:S(2)}, u32[]{:S(2)}) collective-permute-start(bf16[400,128]{1,0:T(8,128)(2,1)S(1)} %get-tuple-element.30), channel_id=1, source_target_pairs={{4,8},{8,4},{12,16},{16,12},{20,24},{24,20},{5,9},{9,5},{13,17},{1... | collective-permute-start | bytes 307208 | tf_op jit(solution)/shard_map/ppermute | solution.py:535
  21.1 1.7 %collective-permute-start.8 = (bf16[400,128]{1,0:T(8,128)(2,1)S(1)}, bf16[400,128]{1,0:T(8,128)(2,1)S(1)}, u32[]{:S(2)}, u32[]{:S(2)}) collective-permute-start(bf16[400,128]{1,0:T(8,128)(2,1)S(1)} %get-tuple-element.31), channel_id=1, source_target_pairs={{0,4},{4,0},{8,12},{12,8},{16,20},{20,16},{24,28},{28,24},{1,5},{5... | collective-permute-start | bytes 307208 | tf_op jit(solution)/shard_map/ppermute | solution.py:536
  22.8 0.3 %collective-permute-done.1.far_ref.face_far = bf16[912,128]{1,0:T(8,128)(2,1)S(1)} collective-permute-done((bf16[912,128]{1,0:T(8,128)(2,1)S(1)}, bf16[912,128]{1,0:T(8,128)(2,1)S(1)}, u32[]{:S(2)}, u32[]{:S(2)}) %collective-permute-start.1) | collective-permute-done | bytes 233504 | tf_op jit(solution)/shard_map/ppermute | solution.py:509
  23.1 0.0 collective-permute-done.2.near_ref.face_near
  23.1 2.1 %advance.1 = f32[3,4,256,128]{3,2,1,0:T(8,128)} custom-call(f32[3,4,256,128]{3,2,1,0:T(8,128)S(1)} %copy-done, bf16[912,128]{1,0:T(8,128)(2,1)S(1)} %collective-permute-done.1.far_ref.face_far, bf16[912,128]{1,0:T(8,128)(2,1)S(1)} %collective-permute-done.2.near_ref.face_near, bf16[64,128]{1,0:T(8,128)(2,1)S(1)} %collective-permute-done.3.first_ref.refs_8_, ...), custom_call_target="tpu_custom_call" | custom-call | flops 1048576 | bytes 1048576 | tf_op jit(solution)/shard_map/advance/pallas_call | solution.py:512
  25.2 1.1 %collective-permute-done.7.far_ref = bf16[400,128]{1,0:T(8,128)(2,1)S(1)} collective-permute-done((bf16[400,128]{1,0:T(8,128)(2,1)S(1)}, bf16[400,128]{1,0:T(8,128)(2,1)S(1)}, u32[]{:S(2)}, u32[]{:S(2)}) %collective-permute-start.7) | collective-permute-done | bytes 102432 | tf_op jit(solution)/shard_map/ppermute | solution.py:535
  26.3 0.0 collective-permute-done.8.near_ref
  26.3 1.5 %transport.1 = f32[4,64,128]{2,1,0:T(8,128)} custom-call(f32[12,80,128]{2,1,0:T(8,128)S(1)} %get-tuple-element.26.wind_ref, bf16[6,80,128]{2,1,0:T(8,128)(2,1)S(1)} %get-tuple-element.27.edge_ref, f32[4,80,128]{2,1,0:T(8,128)S(1)} %get-tuple-element.28.conc_ref, f32[16,128]{1,0:T(8,128)S(1)} %get-tuple-element.29.cols_ref, ...), custom_call_target="tpu_custom_call" | custom-call | flops 1048576 | bytes 1048576 | tf_op jit(solution)/shard_map/transport/pallas_call | solution.py:537
  (1 shorter events, 0.0 us)
Async XLA Ops:
  0.6 12.5 %copy-start.2 = (s32[4,64]{1,0:T(4,128)S(1)}, s32[4,64]{1,0:T(4,128)}, u32[]{:S(2)}) copy-start(s32[4,64]{1,0:T(4,128)} %refs_6_.1) | copy-start | bytes 3076
  0.6 12.4 %copy-start.1 = (f32[4,64,128]{2,1,0:T(8,128)S(1)}, f32[4,64,128]{2,1,0:T(8,128)}, u32[]{:S(2)}) copy-start(f32[4,64,128]{2,1,0:T(8,128)} %refs_5_.1) | copy-start | bytes 393220
  0.7 3.0 %copy-start = (f32[3,4,256,128]{3,2,1,0:T(8,128)S(1)}, f32[3,4,256,128]{3,2,1,0:T(8,128)}, u32[]{:S(2)}) copy-start(f32[3,4,256,128]{3,2,1,0:T(8,128)} %v_ref.7) | copy-start | bytes 4718596
  0.7 12.3 %copy-start.3 = (s32[4,2]{0,1:T(2,128)S(1)}, s32[4,2]{0,1:T(2,128)}, u32[]{:S(2)}) copy-start(s32[4,2]{0,1:T(2,128)} %param.6) | copy-start | bytes 100
  0.8 17.8 %collective-permute-start.4 = (bf16[864,128]{1,0:T(8,128)(2,1)S(1)}, bf16[864,128]{1,0:T(8,128)(2,1)S(1)}, u32[]{:S(2)}, u32[]{:S(2)}) collective-permute-start(bf16[864,128]{1,0:T(8,128)(2,1)S(1)} %get-tuple-element.22), channel_id=1, source_target_pairs={{0,1},{4,5},{8,9},{12,13},{16,17},{20,21},{24,25},{28,29}} | collective-permute-start | bytes 663560 | tf_op jit(solution)/shard_map/ppermute | solution.py:491
  1.6 17.0 %collective-permute-start.5 = (bf16[816,128]{1,0:T(8,128)(2,1)S(1)}, bf16[816,128]{1,0:T(8,128)(2,1)S(1)}, u32[]{:S(2)}, u32[]{:S(2)}) collective-permute-start(bf16[816,128]{1,0:T(8,128)(2,1)S(1)} %get-tuple-element.24), channel_id=1, source_target_pairs={{0,2},{4,6},{8,10},{12,14},{16,18},{20,22},{24,26},{28,30}} | collective-permute-start | bytes 626696 | tf_op jit(solution)/shard_map/ppermute | solution.py:491
  2.3 16.3 %collective-permute-start.6 = (bf16[800,128]{1,0:T(8,128)(2,1)S(1)}, bf16[800,128]{1,0:T(8,128)(2,1)S(1)}, u32[]{:S(2)}, u32[]{:S(2)}) collective-permute-start(bf16[800,128]{1,0:T(8,128)(2,1)S(1)} %get-tuple-element.17.after_ref), channel_id=1, source_target_pairs={{0,3},{4,7},{8,11},{12,15},{16,19},{20,23},{24,27},{28,31}} | collective-permute-start | bytes 614408 | tf_op jit(solution)/shard_map/ppermute | solution.py:491
  4.7 0.7 %collective-permute-start = (bf16[80,128]{1,0:T(8,128)(2,1)S(1)}, bf16[80,128]{1,0:T(8,128)(2,1)S(1)}, u32[]{:S(2)}, u32[]{:S(2)}) collective-permute-start(bf16[80,128]{1,0:T(8,128)(2,1)S(1)} %get-tuple-element.18), channel_id=1, source_target_pairs={{1,2},{2,1},{5,6},{6,5},{9,10},{10,9},{13,14},{14,13},{17,18},{18,... | collective-permute-start | bytes 61448 | tf_op jit(solution)/shard_map/ppermute | solution.py:501
  5.4 9.7 %collective-permute-start.3 = (bf16[64,128]{1,0:T(8,128)(2,1)S(1)}, bf16[64,128]{1,0:T(8,128)(2,1)S(1)}, u32[]{:S(2)}, u32[]{:S(2)}) collective-permute-start(bf16[64,128]{1,0:T(8,128)(2,1)S(1)} %relay.1), channel_id=1, source_target_pairs={{1,0},{2,3},{3,2},{5,4},{6,7},{7,6},{9,8},{10,11},{11,10},{13,12},... | collective-permute-start | bytes 49160 | tf_op jit(solution)/shard_map/ppermute | solution.py:503
  13.2 9.9 %collective-permute-start.1 = (bf16[912,128]{1,0:T(8,128)(2,1)S(1)}, bf16[912,128]{1,0:T(8,128)(2,1)S(1)}, u32[]{:S(2)}, u32[]{:S(2)}) collective-permute-start(bf16[912,128]{1,0:T(8,128)(2,1)S(1)} %get-tuple-element.19), channel_id=1, source_target_pairs={{4,8},{8,4},{12,16},{16,12},{20,24},{24,20},{5,9},{9,5},{13,17},{1... | collective-permute-start | bytes 700424 | tf_op jit(solution)/shard_map/ppermute | solution.py:509
  15.2 7.9 %collective-permute-start.2 = (bf16[912,128]{1,0:T(8,128)(2,1)S(1)}, bf16[912,128]{1,0:T(8,128)(2,1)S(1)}, u32[]{:S(2)}, u32[]{:S(2)}) collective-permute-start(bf16[912,128]{1,0:T(8,128)(2,1)S(1)} %get-tuple-element.20), channel_id=1, source_target_pairs={{0,4},{4,0},{8,12},{12,8},{16,20},{20,16},{24,28},{28,24},{1,5},{5... | collective-permute-start | bytes 700424 | tf_op jit(solution)/shard_map/ppermute | solution.py:510
  19.2 7.1 %collective-permute-start.7 = (bf16[400,128]{1,0:T(8,128)(2,1)S(1)}, bf16[400,128]{1,0:T(8,128)(2,1)S(1)}, u32[]{:S(2)}, u32[]{:S(2)}) collective-permute-start(bf16[400,128]{1,0:T(8,128)(2,1)S(1)} %get-tuple-element.30), channel_id=1, source_target_pairs={{4,8},{8,4},{12,16},{16,12},{20,24},{24,20},{5,9},{9,5},{13,17},{1... | collective-permute-start | bytes 307208 | tf_op jit(solution)/shard_map/ppermute | solution.py:535
  21.1 5.1 %collective-permute-start.8 = (bf16[400,128]{1,0:T(8,128)(2,1)S(1)}, bf16[400,128]{1,0:T(8,128)(2,1)S(1)}, u32[]{:S(2)}, u32[]{:S(2)}) collective-permute-start(bf16[400,128]{1,0:T(8,128)(2,1)S(1)} %get-tuple-element.31), channel_id=1, source_target_pairs={{0,4},{4,0},{8,12},{12,8},{16,20},{20,16},{24,28},{28,24},{1,5},{5... | collective-permute-start | bytes 307208 | tf_op jit(solution)/shard_map/ppermute | solution.py:536

commit v7 on v6

--- a/solution.py
+++ b/solution.py
@@ -269,12 +269,34 @@
         copy.wait()
 
 
+def strip_winds(frame, layer, nx, planes):
+    nplane, rows, nz = frame.shape
+    turned = jnp.concatenate([layer, jnp.zeros((LANES - 16, LANES), F32)], 0).T.astype(BF)[:rows]
+    brow, blane = iota((LANES, nz), 0), iota((LANES, nz), 1)
+    beside = jnp.where((brow == blane + 1) | (brow == blane - 1), 1.0, 0.0).astype(BF)
+    winds = {}
+    for comp in range(nplane // nx):
+        for x in planes:
+            j = comp * nx + x
+            f = frame[j]
+            near = jnp.dot(f.astype(BF), beside, preferred_element_type=F32)
+            top = jnp.where((brow == j) & (blane == nz - 1), 1.0, 0.0).astype(BF)
+            near = near + jnp.dot(turned, top, preferred_element_type=F32)
+            near = near + pltpu.roll(f, 1, 0) + pltpu.roll(f, rows - 1, 0)
+            if x:
+                near = near + frame[j - 1]
+            if x < nx - 1:
+                near = near + frame[j + 1]
+            winds[comp, x] = 0.28 * f + 0.12 * near
+    return winds
+
+
 def prepare(nstrips, *refs):
     strips = refs[:nstrips]
     nlay = 1 + max(nstrips - 4, 0)
     lays = refs[nstrips : nstrips + nlay]
     dust_ref, terrain_ref, eligible_ref, first_ref, second_ref = refs[nstrips + nlay : nstrips + nlay + 5]
-    wind_ref, conc_ref, cols_ref, far_ref, near_ref, edge_ref, frame = refs[nstrips + nlay + 5 :]
+    wind_ref, conc_ref, cols_ref, far_ref, near_ref, layer_ref, frame = refs[nstrips + nlay + 5 :]
     nx, size, nz = dust_ref.shape
     nplane = frame.shape[0]
     ncomp = nplane // nx
@@ -302,30 +324,11 @@
     layer = layer + jnp.where(place == 3, first_ref[face + 16 : face + 32].astype(F32), zero)
     for got in lays[1:]:
         layer = layer + got[...].astype(F32)
-    layer = jnp.concatenate([layer, jnp.zeros((LANES - 16, LANES), F32)], 0)
-    turned = layer.T.astype(BF)[:rows]
-    brow, blane = iota((LANES, nz), 0), iota((LANES, nz), 1)
-    beside = jnp.where((brow == blane + 1) | (brow == blane - 1), 1.0, 0.0).astype(BF)
-    edges = {}
+    layer_ref[...] = layer
+    winds = strip_winds(frame, layer, nx, (0, nx - 1))
     for comp in range(ncomp):
-        f = [frame[comp * nx + x] for x in range(nx)]
-        for x in range(nx):
-            j = comp * nx + x
-            raw = f[x].astype(BF)
-            near = jnp.dot(raw, beside, preferred_element_type=F32)
-            top = jnp.where((brow == j) & (blane == nz - 1), 1.0, 0.0).astype(BF)
-            near = near + jnp.dot(turned, top, preferred_element_type=F32)
-            near = near + pltpu.roll(f[x], 1, 0) + pltpu.roll(f[x], rows - 1, 0)
-            if x:
-                near = near + f[x - 1]
-            if x < nx - 1:
-                near = near + f[x + 1]
-            wind = 0.28 * f[x] + 0.12 * near
-            wind_ref[j] = wind
-            if x == 0:
-                edge_ref[comp] = raw
-            if x == nx - 1:
-                edge_ref[ncomp + comp] = raw
+        wind_ref[comp] = winds[comp, 0]
+        wind_ref[ncomp + comp] = winds[comp, nx - 1]
     row = iota((EDGE, nz), 0)
     for x in range(nx):
         one, two = (slice(2 * x, 2 * x + 1), slice(2 * x + 1, 2 * x + 2))
@@ -351,7 +354,7 @@
         for comp in range(ncomp):
             j = comp * nx + x
             ref[comp * size : (comp + 1) * size] = frame[j, strip].astype(BF)
-            ref[(ncomp + comp) * size : (ncomp + comp + 1) * size] = wind_ref[j, strip].astype(BF)
+            ref[(ncomp + comp) * size : (ncomp + comp + 1) * size] = wind_ref[(ncomp if x else 0) + comp, strip].astype(BF)
         at = 2 * ncomp * size
         rows = [frame[comp * nx + x, first] for comp in range(ncomp)] + [conc_ref[x, first]]
         rows += [frame[comp * nx + x, last] for comp in range(ncomp)] + [conc_ref[x, last]]
@@ -360,11 +363,74 @@
     send_both(odd, send, near_ref, far_ref, nx)
 
 
-def transport(ny, nhoriz, wind_ref, edge_ref, conc_ref, cols_ref, face_far, face_near, far_ref, near_ref, out_ref):
+def plane_state(comps, rise, base, inside):
+    gu, gv, gw = comps
+    shape = gu.shape
+    layer = iota(shape, 1).astype(F32)
+    speed = jnp.sqrt(gu * gu + gv * gv)
+    lift = jnp.where(layer == jnp.broadcast_to(rise, shape), 0.5 * jnp.maximum(speed - 1.0, 0.0), 0.0)
+    keep = (layer >= jnp.broadcast_to(base, shape)) & inside
+    coef = [
+        (0.15 * (0.1 - jnp.minimum(a, 0.0)), 0.15 * (0.1 + jnp.maximum(a, 0.0)))
+        for a in (gu, gv, gw - 0.5)
+    ]
+    return coef, lift, keep
+
+
+def step(state, c, behind, ahead, span=slice(None)):
+    coef, lift, keep = state
+    rows, nz = c.shape
+    layer = iota(lift.shape, 1)
+    here = c[span]
+    total = here + lift
+    pairs = (
+        (ahead, behind),
+        (pltpu.roll(c, rows - 1, 0)[span], pltpu.roll(c, 1, 0)[span]),
+        (
+            jnp.where(layer == nz - 1, 0.0, pltpu.roll(here, nz - 1, 1)),
+            jnp.where(layer == 0, 0.0, pltpu.roll(here, 1, 1)),
+        ),
+    )
+    for (forward, back), (post, prev) in zip(coef, pairs):
+        total = total + forward * (post - here) - back * (here - prev)
+    return jnp.where(keep, total, 0.0)
+
+
+def rows_of(state, span):
+    coef, lift, keep = state
+    return [(forward[span], back[span]) for forward, back in coef], lift[span], keep[span]
+
+
+def domain_rows(shape, ny, size):
+    y = iota(shape, 0) + (lax.axis_index("vert") * size - EDGE)
+    return (y >= 0) & (y < ny)
+
+
+def interior(ny, size, frame, layer_ref, conc_ref, cols_ref, after_ref, coef_ref, lift_ref, keep_ref, once_ref):
+    del after_ref
+    nx, rows, nz = conc_ref.shape
+    ncomp = frame.shape[0] // nx
+    winds = strip_winds(frame, layer_ref[...], nx, range(1, nx - 1))
+    table = jnp.concatenate([cols_ref[...], jnp.zeros((LANES - 16, LANES), F32)], 0).T[:rows]
+    inside = domain_rows((rows, nz), ny, size)
+    for x in range(1, nx - 1):
+        comps = [winds[comp, x] for comp in range(ncomp)]
+        state = plane_state(comps, table[:, EDGE + x : EDGE + x + 1], table[:, x : x + 1], inside)
+        coef, lift, keep = state
+        for i, pair in enumerate(coef):
+            coef_ref[x - 1, 2 * i], coef_ref[x - 1, 2 * i + 1] = pair
+        lift_ref[x - 1] = lift
+        keep_ref[x - 1] = jnp.where(keep, 1.0, 0.0)
+        once_ref[x - 1] = step(state, conc_ref[x], conc_ref[x - 1], conc_ref[x + 1])
+
+
+def transport(ny, nhoriz, *refs):
+    wind_ref, frame, conc_ref, cols_ref, face_far, face_near, far_ref, near_ref = refs[:8]
+    coef_ref, lift_ref, keep_ref, once_ref, out_ref = refs[8:]
     nx, size, nz = out_ref.shape
-    ncomp = edge_ref.shape[0] // 2
+    ncomp = frame.shape[0] // nx
     rows = size + 2 * EDGE
-    column, place = (lax.axis_index("horiz"), lax.axis_index("vert"))
+    column = lax.axis_index("horiz")
     odd = lax.rem(column, 2) == 1
     low = iota((EDGE, nz), 0)
 
@@ -385,13 +451,13 @@
         at = ncomp * ny
         dusts[side] = (
             framed(either(face_one, face_other, at, size), ends[side], ncomp),
-            framed(either(face_one, face_other, at + size, size)),
+            either(face_one, face_other, at + size, size),
         )
         marks[side] = either(face_one, face_other, at + 2 * size, 16)
 
     def part(side, i, halo=None):
         rows = either(*pairs_of[side][:2], i * size, size)
-        return framed(rows) if halo is None else framed(rows, ends[side], halo)
+        return rows if halo is None else framed(rows, ends[side], halo)
 
     below, above = ("below", "above")
     conc = [dusts[below][1], dusts[below][0]]
@@ -401,61 +467,48 @@
     mark = 0
     ground = [mark] + [16 + x for x in range(nx)] + [32 + mark]
     lifted = [mark + 1] + [16 + EDGE + x for x in range(nx)] + [33 + mark]
-    layer = iota((rows, nz), 1).astype(F32)
-    y = iota((rows, nz), 0) + (place * size - EDGE)
-    inside = (y >= 0) & (y < ny)
-    first, last = layer == 0.0, layer == nz - 1.0
-    zero = jnp.zeros((rows, nz), F32)
+    inside = domain_rows((rows, nz), ny, size)
+    strip = slice(EDGE, EDGE + size)
     state = [None] * (nx + 2)
     for p in range(nx + 2):
+        if 1 < p < nx:
+            coef = [(coef_ref[p - 2, 2 * i], coef_ref[p - 2, 2 * i + 1]) for i in range(3)]
+            state[p] = (coef, lift_ref[p - 2], keep_ref[p - 2] > 0.5)
+            continue
         comps = []
         for comp in range(ncomp):
             if p == 0:
-                w = part(below, ncomp + comp) + 0.12 * edge_ref[comp].astype(F32)
+                w = part(below, ncomp + comp) + 0.12 * frame[comp * nx, strip]
             elif p == nx + 1:
-                w = part(above, ncomp + comp) + 0.12 * edge_ref[ncomp + comp].astype(F32)
+                w = part(above, ncomp + comp) + 0.12 * frame[comp * nx + nx - 1, strip]
+            elif p == 1:
+                w = wind_ref[comp] + 0.12 * part(below, comp, comp)
             else:
-                w = wind_ref[comp * nx + p - 1]
-                if p == 1:
-                    w = w + 0.12 * part(below, comp, comp)
-                if p == nx:
-                    w = w + 0.12 * part(above, comp, comp)
+                w = wind_ref[ncomp + comp] + 0.12 * part(above, comp, comp)
             comps.append(w)
-        gu, gv, gw = comps
-        speed = jnp.sqrt(gu * gu + gv * gv)
-        rise = jnp.broadcast_to(table[:, lifted[p] : lifted[p] + 1], (rows, nz))
-        base = jnp.broadcast_to(table[:, ground[p] : ground[p] + 1], (rows, nz))
-        lift = jnp.where(layer == rise, 0.5 * jnp.maximum(speed - 1.0, 0.0), 0.0)
-        keep = (layer >= base) & inside
+        rise, base = (table[:, lifted[p] : lifted[p] + 1], table[:, ground[p] : ground[p] + 1])
         if p == 0:
-            keep = keep & (column > 0)
-        if p == nx + 1:
-            keep = keep & (column < nhoriz - 1)
-        coef = [
-            (0.15 * (0.1 - jnp.minimum(a, 0.0)), 0.15 * (0.1 + jnp.maximum(a, 0.0)))
-            for a in (gu, gv, gw - 0.5)
-        ]
-        state[p] = (coef, lift, keep)
-
-    def step(p, c, behind, ahead):
-        coef, lift, keep = state[p]
-        total = c + lift
-        pairs = (
-            (ahead, behind),
-            (pltpu.roll(c, rows - 1, 0), pltpu.roll(c, 1, 0)),
-            (
-                jnp.where(last, zero, pltpu.roll(c, nz - 1, 1)),
-                jnp.where(first, zero, pltpu.roll(c, 1, 1)),
-            ),
-        )
-        for (forward, back), (post, prev) in zip(coef, pairs):
-            total = total + forward * (post - c) - back * (c - prev)
-        return jnp.where(keep, total, 0.0)
-
-    once = [step(p, conc[p + 1], conc[p], conc[p + 2]) for p in range(nx + 2)]
+            state[p] = plane_state(comps, rise[strip], base[strip], inside[strip] & (column > 0))
+        elif p == nx + 1:
+            state[p] = plane_state(comps, rise[strip], base[strip], inside[strip] & (column < nhoriz - 1))
+        else:
+            state[p] = plane_state(comps, rise, base, inside)
+
+    once = []
+    for p in range(nx + 2):
+        c, behind, ahead = (conc[p + 1], conc[p], conc[p + 2])
+        if 1 < p < nx:
+            once.append(once_ref[p - 2])
+        elif p in (0, nx + 1):
+            behind = behind if p == 0 else behind[strip]
+            ahead = ahead[strip] if p == 0 else ahead
+            once.append(step(state[p], c, behind, ahead, strip))
+        else:
+            once.append(step(state[p], c, behind, ahead))
     for x in range(nx):
-        twice = step(x + 1, once[x + 1], once[x], once[x + 2])
-        out_ref[x] = twice[EDGE : EDGE + size]
+        behind = once[x] if x == 0 else once[x][strip]
+        ahead = once[x + 2] if x == nx - 1 else once[x + 2][strip]
+        out_ref[x] = step(rows_of(state[x + 1], strip), once[x + 1], behind, ahead, strip)
 
 
 def pairs(size, start):
@@ -519,26 +572,30 @@
     )(velocity, far, near, first, second, got[1])
 
     wire = 2 * ncomp * size + 16
-    wind, conc, cols, mf, mn, edge = call(
+    wind, conc, cols, mf, mn, layer, frame = call(
         functools.partial(prepare, nv),
         [
-            shaped(nplane, rows, LANES, dtype=F32),
+            shaped(2 * ncomp, rows, LANES, dtype=F32),
             shaped(nx, rows, LANES, dtype=F32),
             shaped(16, LANES, dtype=F32),
             shaped(wire, LANES),
             shaped(wire, LANES),
-            shaped(2 * ncomp, rows, LANES),
+            shaped(16, LANES, dtype=F32),
+            shaped(nplane, rows, LANES, dtype=F32),
         ],
         "prepare",
-        [pltpu.VMEM((nplane, rows, LANES), F32)],
     )(*got, *lays, dust, terrain, eligible, first, second)
     mf = lax.ppermute(mf, "horiz", far_pairs)
     mn = lax.ppermute(mn, "horiz", near_pairs)
+    inner = [shaped(nx - 2, *dims, rows, LANES, dtype=F32) for dims in ((6,), (), (), ())]
+    inner = call(
+        functools.partial(interior, ny, size), inner, "interior", in_specs=[VMEM] * 4 + [anywhere]
+    )(frame, layer, conc, cols, far)
     dust_next = call(
         functools.partial(transport, ny, nh),
         jax.ShapeDtypeStruct(dust.shape, F32),
         "transport",
-    )(wind, edge, conc, cols, far, near, mf, mn)
+    )(wind, frame, conc, cols, far, near, mf, mn, *inner)
     return (velocity_next, dust_next)
 
 

time: 28.1 us -> 27.7 us (0.986)
  waiting for transfers between devices: 3.22 us -> 2.69 us
    ppermute x1, waiting for transfers between devices: 1.07 us -> 0.41 us  [local(): mf = lax.ppermute(mf, 'horiz', far_pairs)]
    pallas_call x1 -> x2, Pallas kernels: 0.54 us -> 0.94 us  [the longest x1 0.52 us: local(): call(functools.partial(interior, ny, size), inner, 'interior', in_specs=[...]
  transfers between devices with their start and end apart: 9 -> 9, of which waited for: 3 -> 3; matrix products, arithmetic and copies ran while one was open for 0% -> 0% of each run, Pallas kernels for 14% -> 16%
where the time goes in v7:
time: 27.7 us; the launch traced here: 27.4 us
  starting transfers between devices  18.1 us (65%)
  Pallas kernels  5.69 us (21%)
  waiting for transfers between devices  2.69 us (10%)
  between operations  0.8 us (3%)
    ppermute x1, starting transfers between devices, local(): first = lax.ppermute(first, 'vert', pairs(nv, 0)[1:])  7.54 us
    ppermute x3, starting transfers between devices, local(): lax.ppermute(strips[t], 'vert', [(0, t)])  2.77 us
    pallas_call x1, Pallas kernels, local(): call(advance, jax.ShapeDtypeStruct(velocity.shape, F32), 'advance', [pltp...  2.11 us
    ppermute x1, starting transfers between devices, local(): far = lax.ppermute(far, 'horiz', far_pairs)  1.92 us
    ppermute x1, starting transfers between devices, local(): mf = lax.ppermute(mf, 'horiz', far_pairs)  1.92 us
    ppermute x3, waiting for transfers between devices, local(): lax.ppermute(strips[t], 'vert', [(0, t)])  1.84 us
    ppermute x1, starting transfers between devices, local(): mn = lax.ppermute(mn, 'horiz', near_pairs)  1.66 us
    ppermute x1, starting transfers between devices, local(): near = lax.ppermute(near, 'horiz', near_pairs)  1.66 us
  transfers between devices with their start and end apart: 9, of which 3 were waited for; matrix products, arithmetic and copies ran while one was open for 0% of the time, Pallas kernels for 16%

profile of v7, /device:TPU:28, one launch (start us, length us, event | category | flops | bytes accessed | tf_op | source)
XLA Modules:
  0.0 27.4 jit_solution(8385973041082617668)
XLA Ops:
  0.6 0.0 copy-start.2
  0.6 0.0 copy-start.1
  0.7 0.0 copy-start
  0.7 0.0 copy-start.3
  0.7 0.1 pack_low.1
  0.8 0.8 %collective-permute-start.4 = (bf16[864,128]{1,0:T(8,128)(2,1)S(1)}, bf16[864,128]{1,0:T(8,128)(2,1)S(1)}, u32[]{:S(2)}, u32[]{:S(2)}) collective-permute-start(bf16[864,128]{1,0:T(8,128)(2,1)S(1)} %get-tuple-element.27), channel_id=1, source_target_pairs={{0,1},{4,5},{8,9},{12,13},{16,17},{20,21},{24,25},{28,29}} | collective-permute-start | bytes 663560 | tf_op jit(solution)/shard_map/ppermute | solution.py:544
  1.6 0.7 %collective-permute-start.5 = (bf16[816,128]{1,0:T(8,128)(2,1)S(1)}, bf16[816,128]{1,0:T(8,128)(2,1)S(1)}, u32[]{:S(2)}, u32[]{:S(2)}) collective-permute-start(bf16[816,128]{1,0:T(8,128)(2,1)S(1)} %get-tuple-element.29), channel_id=1, source_target_pairs={{0,2},{4,6},{8,10},{12,14},{16,18},{20,22},{24,26},{28,30}} | collective-permute-start | bytes 626696 | tf_op jit(solution)/shard_map/ppermute | solution.py:544
  2.3 1.3 %collective-permute-start.6 = (bf16[800,128]{1,0:T(8,128)(2,1)S(1)}, bf16[800,128]{1,0:T(8,128)(2,1)S(1)}, u32[]{:S(2)}, u32[]{:S(2)}) collective-permute-start(bf16[800,128]{1,0:T(8,128)(2,1)S(1)} %get-tuple-element.22.after_ref), channel_id=1, source_target_pairs={{0,3},{4,7},{8,11},{12,15},{16,19},{20,23},{24,27},{28,31}} | collective-permute-start | bytes 614408 | tf_op jit(solution)/shard_map/ppermute | solution.py:544
  3.6 0.0 copy-done
  3.6 1.1 %pack_ends.1 = (bf16[64,128]{1,0:T(8,128)(2,1)S(1)}, bf16[80,128]{1,0:T(8,128)(2,1)S(1)}, bf16[3,16,128]{2,1,0:T(8,128)(2,1)S(1)}) custom-call(f32[3,4,256,128]{3,2,1,0:T(8,128)S(1)} %copy-done, f32[4,64,128]{2,1,0:T(8,128)} %refs_5_.1, s32[4,64]{1,0:T(4,128)} %refs_6_.1, bf16[800,128]{1,0:T(8,128)(2,1)S(1)} %get-tuple-element.22.after_ref), custom_call_target="tpu_custom_call" | custom-call | flops 1048576 | bytes 1048576 | tf_op jit(solution)/shard_map/pack_ends/pallas_call | solution.py:546
  4.7 0.7 %collective-permute-start = (bf16[80,128]{1,0:T(8,128)(2,1)S(1)}, bf16[80,128]{1,0:T(8,128)(2,1)S(1)}, u32[]{:S(2)}, u32[]{:S(2)}) collective-permute-start(bf16[80,128]{1,0:T(8,128)(2,1)S(1)} %get-tuple-element.23), channel_id=1, source_target_pairs={{1,2},{2,1},{5,6},{6,5},{9,10},{10,9},{13,14},{14,13},{17,18},{18,... | collective-permute-start | bytes 61448 | tf_op jit(solution)/shard_map/ppermute | solution.py:554
  5.4 0.0 collective-permute-done.after_ref.second_ref.refs_9_
  5.4 7.5 %collective-permute-start.3 = (bf16[64,128]{1,0:T(8,128)(2,1)S(1)}, bf16[64,128]{1,0:T(8,128)(2,1)S(1)}, u32[]{:S(2)}, u32[]{:S(2)}) collective-permute-start(bf16[64,128]{1,0:T(8,128)(2,1)S(1)} %relay.1), channel_id=1, source_target_pairs={{1,0},{2,3},{3,2},{5,4},{6,7},{7,6},{9,8},{10,11},{11,10},{13,12},... | collective-permute-start | bytes 49160 | tf_op jit(solution)/shard_map/ppermute | solution.py:556
  13.0 0.0 copy-done.3
  13.0 0.1 copy.6.eligible_ref.refs_7_
  13.1 0.0 copy-done.2
  13.1 0.0 copy-done.1
  13.1 0.1 pack_sides.1
  13.2 1.9 %collective-permute-start.1 = (bf16[912,128]{1,0:T(8,128)(2,1)S(1)}, bf16[912,128]{1,0:T(8,128)(2,1)S(1)}, u32[]{:S(2)}, u32[]{:S(2)}) collective-permute-start(bf16[912,128]{1,0:T(8,128)(2,1)S(1)} %get-tuple-element.24), channel_id=1, source_target_pairs={{4,8},{8,4},{12,16},{16,12},{20,24},{24,20},{5,9},{9,5},{13,17},{1... | collective-permute-start | bytes 700424 | tf_op jit(solution)/shard_map/ppermute | solution.py:562
  15.1 0.0 collective-permute-done.3.first_ref.refs_8_
  15.2 1.7 %collective-permute-start.2 = (bf16[912,128]{1,0:T(8,128)(2,1)S(1)}, bf16[912,128]{1,0:T(8,128)(2,1)S(1)}, u32[]{:S(2)}, u32[]{:S(2)}) collective-permute-start(bf16[912,128]{1,0:T(8,128)(2,1)S(1)} %get-tuple-element.25), channel_id=1, source_target_pairs={{0,4},{4,0},{8,12},{12,8},{16,20},{20,16},{24,28},{28,24},{1,5},{5... | collective-permute-start | bytes 700424 | tf_op jit(solution)/shard_map/ppermute | solution.py:563
  16.8 1.8 %collective-permute-done.6.refs_3_ = bf16[800,128]{1,0:T(8,128)(2,1)S(1)} collective-permute-done((bf16[800,128]{1,0:T(8,128)(2,1)S(1)}, bf16[800,128]{1,0:T(8,128)(2,1)S(1)}, u32[]{:S(2)}, u32[]{:S(2)}) %collective-permute-start.6) | collective-permute-done | bytes 204832 | tf_op jit(solution)/shard_map/ppermute | solution.py:544
  18.7 0.0 collective-permute-done.5.refs_2_
  18.7 0.0 collective-permute-done.4.strip_ref.refs_1_
  18.7 0.4 %prepare.1 = (f32[6,80,128]{2,1,0:T(8,128)S(1)}, f32[4,80,128]{2,1,0:T(8,128)S(1)}, f32[16,128]{1,0:T(8,128)S(1)}, bf16[400,128]{1,0:T(8,128)(2,1)S(1)}, bf16[40...) custom-call(bf16[816,128]{1,0:T(8,128)(2,1)S(1)} %get-tuple-element.28.refs_0_, ...), custom_call_target="tpu_custom_call" | custom-call | flops 1048576 | bytes 1048576 | tf_op jit(solution)/shard_map/prepare/pallas_call | solution.py:575
  19.1 1.9 %collective-permute-start.7 = (bf16[400,128]{1,0:T(8,128)(2,1)S(1)}, bf16[400,128]{1,0:T(8,128)(2,1)S(1)}, u32[]{:S(2)}, u32[]{:S(2)}) collective-permute-start(bf16[400,128]{1,0:T(8,128)(2,1)S(1)} %get-tuple-element.35), channel_id=1, source_target_pairs={{4,8},{8,4},{12,16},{16,12},{20,24},{24,20},{5,9},{9,5},{13,17},{1... | collective-permute-start | bytes 307208 | tf_op jit(solution)/shard_map/ppermute | solution.py:588
  21.0 1.7 %collective-permute-start.8 = (bf16[400,128]{1,0:T(8,128)(2,1)S(1)}, bf16[400,128]{1,0:T(8,128)(2,1)S(1)}, u32[]{:S(2)}, u32[]{:S(2)}) collective-permute-start(bf16[400,128]{1,0:T(8,128)(2,1)S(1)} %get-tuple-element.36), channel_id=1, source_target_pairs={{0,4},{4,0},{8,12},{12,8},{16,20},{20,16},{24,28},{28,24},{1,5},{5... | collective-permute-start | bytes 307208 | tf_op jit(solution)/shard_map/ppermute | solution.py:589
  22.7 0.4 %collective-permute-done.1.far_ref.after_ref.refs_4_ = bf16[912,128]{1,0:T(8,128)(2,1)S(1)} collective-permute-done((bf16[912,128]{1,0:T(8,128)(2,1)S(1)}, bf16[912,128]{1,0:T(8,128)(2,1)S(1)}, u32[]{:S(2)}, u32[]{:S(2)}) %collective-permute-start.1) | collective-permute-done | bytes 233504 | tf_op jit(solution)/shard_map/ppermute | solution.py:562
  23.1 0.0 collective-permute-done.2.near_ref.refs_5_
  23.1 2.1 %advance.1 = f32[3,4,256,128]{3,2,1,0:T(8,128)} custom-call(f32[3,4,256,128]{3,2,1,0:T(8,128)S(1)} %copy-done, bf16[912,128]{1,0:T(8,128)(2,1)S(1)} %collective-permute-done.1.far_ref.after_ref.refs_4_, bf16[912,128]{1,0:T(8,128)(2,1)S(1)} %collective-permute-done.2.near_ref.refs_5_, bf16[64,128]{1,0:T(8,128)(2,1)S(1)} %collective-permute-done.3.first_ref.refs_8_, ...), custom_call_target="tpu_custom_call" | custom-call | flops 1048576 | bytes 1048576 | tf_op jit(solution)/shard_map/advance/pallas_call | solution.py:565
  25.2 0.5 %interior.1 = (f32[2,6,80,128]{3,2,1,0:T(8,128)S(1)}, f32[2,80,128]{2,1,0:T(8,128)S(1)}, f32[2,80,128]{2,1,0:T(8,128)S(1)}, f32[2,80,128]{2,1,0:T(8,128)S(1)}) custom-call(f32[12,80,128]{2,1,0:T(8,128)S(1)} %get-tuple-element.32.frame.refs_1_, f32[16,128]{1,0:T(8,128)S(1)} %get-tuple-element.37.layer_ref, ...), custom_call_target="tpu_custom_call" | custom-call | flops 1048576 | bytes 1048576 | tf_op jit(solution)/shard_map/interior/pallas_call | solution.py:591
  25.7 0.4 %collective-permute-done.7.refs_6_ = bf16[400,128]{1,0:T(8,128)(2,1)S(1)} collective-permute-done((bf16[400,128]{1,0:T(8,128)(2,1)S(1)}, bf16[400,128]{1,0:T(8,128)(2,1)S(1)}, u32[]{:S(2)}, u32[]{:S(2)}) %collective-permute-start.7) | collective-permute-done | bytes 102432 | tf_op jit(solution)/shard_map/ppermute | solution.py:588
  26.2 0.0 collective-permute-done.8.refs_7_
  26.2 1.3 %transport.1 = f32[4,64,128]{2,1,0:T(8,128)} custom-call(f32[6,80,128]{2,1,0:T(8,128)S(1)} %get-tuple-element.31.refs_0_, f32[12,80,128]{2,1,0:T(8,128)S(1)} %get-tuple-element.32.frame.refs_1_, f32[4,80,128]{2,1,0:T(8,128)S(1)} %get-tuple-element.33.conc_ref.refs_2_, f32[16,128]{1,0:T(8,128)S(1)} %get-tuple-element.34.cols_ref.refs_3_, ...), custom_call_target="tpu_custom_call" | custom-call | flops 1048576 | bytes 1048576 | tf_op jit(solution)/shard_map/transport/pallas_call | solution.py:594
  (1 shorter events, 0.0 us)
Async XLA Ops:
  0.6 12.5 %copy-start.2 = (s32[4,64]{1,0:T(4,128)S(1)}, s32[4,64]{1,0:T(4,128)}, u32[]{:S(2)}) copy-start(s32[4,64]{1,0:T(4,128)} %refs_6_.1) | copy-start | bytes 3076
  0.6 12.4 %copy-start.1 = (f32[4,64,128]{2,1,0:T(8,128)S(1)}, f32[4,64,128]{2,1,0:T(8,128)}, u32[]{:S(2)}) copy-start(f32[4,64,128]{2,1,0:T(8,128)} %refs_5_.1) | copy-start | bytes 393220
  0.7 3.0 %copy-start = (f32[3,4,256,128]{3,2,1,0:T(8,128)S(1)}, f32[3,4,256,128]{3,2,1,0:T(8,128)}, u32[]{:S(2)}) copy-start(f32[3,4,256,128]{3,2,1,0:T(8,128)} %v_ref.7) | copy-start | bytes 4718596
  0.7 12.3 %copy-start.3 = (s32[4,2]{0,1:T(2,128)S(1)}, s32[4,2]{0,1:T(2,128)}, u32[]{:S(2)}) copy-start(s32[4,2]{0,1:T(2,128)} %param.6) | copy-start | bytes 100
  0.8 17.8 %collective-permute-start.4 = (bf16[864,128]{1,0:T(8,128)(2,1)S(1)}, bf16[864,128]{1,0:T(8,128)(2,1)S(1)}, u32[]{:S(2)}, u32[]{:S(2)}) collective-permute-start(bf16[864,128]{1,0:T(8,128)(2,1)S(1)} %get-tuple-element.27), channel_id=1, source_target_pairs={{0,1},{4,5},{8,9},{12,13},{16,17},{20,21},{24,25},{28,29}} | collective-permute-start | bytes 663560 | tf_op jit(solution)/shard_map/ppermute | solution.py:544
  1.6 17.0 %collective-permute-start.5 = (bf16[816,128]{1,0:T(8,128)(2,1)S(1)}, bf16[816,128]{1,0:T(8,128)(2,1)S(1)}, u32[]{:S(2)}, u32[]{:S(2)}) collective-permute-start(bf16[816,128]{1,0:T(8,128)(2,1)S(1)} %get-tuple-element.29), channel_id=1, source_target_pairs={{0,2},{4,6},{8,10},{12,14},{16,18},{20,22},{24,26},{28,30}} | collective-permute-start | bytes 626696 | tf_op jit(solution)/shard_map/ppermute | solution.py:544
  2.3 16.3 %collective-permute-start.6 = (bf16[800,128]{1,0:T(8,128)(2,1)S(1)}, bf16[800,128]{1,0:T(8,128)(2,1)S(1)}, u32[]{:S(2)}, u32[]{:S(2)}) collective-permute-start(bf16[800,128]{1,0:T(8,128)(2,1)S(1)} %get-tuple-element.22.after_ref), channel_id=1, source_target_pairs={{0,3},{4,7},{8,11},{12,15},{16,19},{20,23},{24,27},{28,31}} | collective-permute-start | bytes 614408 | tf_op jit(solution)/shard_map/ppermute | solution.py:544
  4.7 0.7 %collective-permute-start = (bf16[80,128]{1,0:T(8,128)(2,1)S(1)}, bf16[80,128]{1,0:T(8,128)(2,1)S(1)}, u32[]{:S(2)}, u32[]{:S(2)}) collective-permute-start(bf16[80,128]{1,0:T(8,128)(2,1)S(1)} %get-tuple-element.23), channel_id=1, source_target_pairs={{1,2},{2,1},{5,6},{6,5},{9,10},{10,9},{13,14},{14,13},{17,18},{18,... | collective-permute-start | bytes 61448 | tf_op jit(solution)/shard_map/ppermute | solution.py:554
  5.4 9.7 %collective-permute-start.3 = (bf16[64,128]{1,0:T(8,128)(2,1)S(1)}, bf16[64,128]{1,0:T(8,128)(2,1)S(1)}, u32[]{:S(2)}, u32[]{:S(2)}) collective-permute-start(bf16[64,128]{1,0:T(8,128)(2,1)S(1)} %relay.1), channel_id=1, source_target_pairs={{1,0},{2,3},{3,2},{5,4},{6,7},{7,6},{9,8},{10,11},{11,10},{13,12},... | collective-permute-start | bytes 49160 | tf_op jit(solution)/shard_map/ppermute | solution.py:556
  13.2 9.9 %collective-permute-start.1 = (bf16[912,128]{1,0:T(8,128)(2,1)S(1)}, bf16[912,128]{1,0:T(8,128)(2,1)S(1)}, u32[]{:S(2)}, u32[]{:S(2)}) collective-permute-start(bf16[912,128]{1,0:T(8,128)(2,1)S(1)} %get-tuple-element.24), channel_id=1, source_target_pairs={{4,8},{8,4},{12,16},{16,12},{20,24},{24,20},{5,9},{9,5},{13,17},{1... | collective-permute-start | bytes 700424 | tf_op jit(solution)/shard_map/ppermute | solution.py:562
  15.2 7.9 %collective-permute-start.2 = (bf16[912,128]{1,0:T(8,128)(2,1)S(1)}, bf16[912,128]{1,0:T(8,128)(2,1)S(1)}, u32[]{:S(2)}, u32[]{:S(2)}) collective-permute-start(bf16[912,128]{1,0:T(8,128)(2,1)S(1)} %get-tuple-element.25), channel_id=1, source_target_pairs={{0,4},{4,0},{8,12},{12,8},{16,20},{20,16},{24,28},{28,24},{1,5},{5... | collective-permute-start | bytes 700424 | tf_op jit(solution)/shard_map/ppermute | solution.py:563
  19.1 7.1 %collective-permute-start.7 = (bf16[400,128]{1,0:T(8,128)(2,1)S(1)}, bf16[400,128]{1,0:T(8,128)(2,1)S(1)}, u32[]{:S(2)}, u32[]{:S(2)}) collective-permute-start(bf16[400,128]{1,0:T(8,128)(2,1)S(1)} %get-tuple-element.35), channel_id=1, source_target_pairs={{4,8},{8,4},{12,16},{16,12},{20,24},{24,20},{5,9},{9,5},{13,17},{1... | collective-permute-start | bytes 307208 | tf_op jit(solution)/shard_map/ppermute | solution.py:588
  21.0 5.1 %collective-permute-start.8 = (bf16[400,128]{1,0:T(8,128)(2,1)S(1)}, bf16[400,128]{1,0:T(8,128)(2,1)S(1)}, u32[]{:S(2)}, u32[]{:S(2)}) collective-permute-start(bf16[400,128]{1,0:T(8,128)(2,1)S(1)} %get-tuple-element.36), channel_id=1, source_target_pairs={{0,4},{4,0},{8,12},{12,8},{16,20},{20,16},{24,28},{28,24},{1,5},{5... | collective-permute-start | bytes 307208 | tf_op jit(solution)/shard_map/ppermute | solution.py:589

commit v8 on v7

--- a/solution.py
+++ b/solution.py
@@ -229,7 +229,25 @@
     return (jnp.where(odd, second, first), below)
 
 
-def advance(v_ref, far_ref, near_ref, first_ref, second_ref, strip_ref, out_ref, buf, sems):
+def rows_before(v_ref, comp, x, a):
+    if a:
+        return v_ref[comp, x, a - 1 : a + LANES - 1, :]
+    edge = pltpu.roll(v_ref[comp, x, :8, :], 1, 0)
+    edge = jnp.where(iota(edge.shape, 0) == 0, 0.0, edge)
+    return jnp.concatenate([edge, v_ref[comp, x, 7 : LANES - 1, :]], 0)
+
+
+def rows_after(v_ref, comp, x, a):
+    ny = v_ref.shape[2]
+    if a + LANES < ny:
+        return v_ref[comp, x, a + 1 : a + LANES + 1, :]
+    edge = pltpu.roll(v_ref[comp, x, ny - 8 :, :], 7, 0)
+    edge = jnp.where(iota(edge.shape, 0) == 7, 0.0, edge)
+    return jnp.concatenate([v_ref[comp, x, a + 1 : ny - 7, :], edge], 0)
+
+
+def advance(v_ref, far_ref, near_ref, first_ref, second_ref, strip_ref, mark_ref, out_ref, buf, sems):
+    del mark_ref
     ncomp, nx, ny, nz = v_ref.shape
     odd = lax.rem(lax.axis_index("horiz"), 2) == 1
     row, lane = iota((LANES, nz), 0), iota((LANES, nz), 1)
@@ -256,10 +274,7 @@
                 f = v_ref[comp, x, span, :]
                 sums = sums + jnp.where(lane == 0, 0.0, pltpu.roll(f, 1, 1))
                 sums = sums + jnp.where(lane == nz - 1, 0.0, pltpu.roll(f, nz - 1, 1))
-                prev = v_ref[comp, x, a - 1 : a, :] if a else jnp.zeros((1, nz), F32)
-                post = v_ref[comp, x, a + LANES : a + LANES + 1, :] if half < nb - 1 else jnp.zeros((1, nz), F32)
-                sums = sums + jnp.where(row == 0, prev, pltpu.roll(f, 1, 0))
-                sums = sums + jnp.where(row == LANES - 1, post, pltpu.roll(f, LANES - 1, 0))
+                sums = sums + rows_before(v_ref, comp, x, a) + rows_after(v_ref, comp, x, a)
                 sums = sums + (v_ref[comp, x - 1, span, :] if x else below)
                 sums = sums + (v_ref[comp, x + 1, span, :] if x < nx - 1 else above)
                 buf[comp, x, span, :] = f + 0.12 * (sums - 6.0 * f)
@@ -370,29 +385,30 @@
     speed = jnp.sqrt(gu * gu + gv * gv)
     lift = jnp.where(layer == jnp.broadcast_to(rise, shape), 0.5 * jnp.maximum(speed - 1.0, 0.0), 0.0)
     keep = (layer >= jnp.broadcast_to(base, shape)) & inside
-    coef = [
-        (0.15 * (0.1 - jnp.minimum(a, 0.0)), 0.15 * (0.1 + jnp.maximum(a, 0.0)))
-        for a in (gu, gv, gw - 0.5)
-    ]
-    return coef, lift, keep
+    coef, own = ([], 1.0)
+    for a in (gu, gv, gw - 0.5):
+        scaled = 0.15 * a
+        forward, back = (0.015 - jnp.minimum(scaled, 0.0), 0.015 + jnp.maximum(scaled, 0.0))
+        own = own - (forward + back)
+        coef.append((forward, back))
+    forward, back = coef[2]
+    coef[2] = (jnp.where(layer == shape[1] - 1.0, 0.0, forward), jnp.where(layer == 0.0, 0.0, back))
+    return coef + [(own, lift)], lift, keep
 
 
 def step(state, c, behind, ahead, span=slice(None)):
-    coef, lift, keep = state
+    coef, _, keep = state
     rows, nz = c.shape
-    layer = iota(lift.shape, 1)
     here = c[span]
-    total = here + lift
     pairs = (
         (ahead, behind),
         (pltpu.roll(c, rows - 1, 0)[span], pltpu.roll(c, 1, 0)[span]),
-        (
-            jnp.where(layer == nz - 1, 0.0, pltpu.roll(here, nz - 1, 1)),
-            jnp.where(layer == 0, 0.0, pltpu.roll(here, 1, 1)),
-        ),
+        (pltpu.roll(here, nz - 1, 1), pltpu.roll(here, 1, 1)),
     )
-    for (forward, back), (post, prev) in zip(coef, pairs):
-        total = total + forward * (post - here) - back * (here - prev)
+    own, lift = coef[3]
+    total = own * here + lift
+    for (forward, back), (post, prev) in zip(coef[:3], pairs):
+        total = total + (forward * post + back * prev)
     return jnp.where(keep, total, 0.0)
 
 
@@ -406,8 +422,8 @@
     return (y >= 0) & (y < ny)
 
 
-def interior(ny, size, frame, layer_ref, conc_ref, cols_ref, after_ref, coef_ref, lift_ref, keep_ref, once_ref):
-    del after_ref
+def interior(ny, size, frame, layer_ref, conc_ref, cols_ref, coef_ref, lift_ref, keep_ref, once_ref, mark_ref):
+    mark_ref[...] = jnp.zeros_like(mark_ref)
     nx, rows, nz = conc_ref.shape
     ncomp = frame.shape[0] // nx
     winds = strip_winds(frame, layer_ref[...], nx, range(1, nx - 1))
@@ -426,7 +442,7 @@
 
 def transport(ny, nhoriz, *refs):
     wind_ref, frame, conc_ref, cols_ref, face_far, face_near, far_ref, near_ref = refs[:8]
-    coef_ref, lift_ref, keep_ref, once_ref, out_ref = refs[8:]
+    coef_ref, lift_ref, keep_ref, once_ref, out_ref, buf, sems = refs[8:]
     nx, size, nz = out_ref.shape
     ncomp = frame.shape[0] // nx
     rows = size + 2 * EDGE
@@ -472,7 +488,7 @@
     state = [None] * (nx + 2)
     for p in range(nx + 2):
         if 1 < p < nx:
-            coef = [(coef_ref[p - 2, 2 * i], coef_ref[p - 2, 2 * i + 1]) for i in range(3)]
+            coef = [(coef_ref[p - 2, 2 * i], coef_ref[p - 2, 2 * i + 1]) for i in range(4)]
             state[p] = (coef, lift_ref[p - 2], keep_ref[p - 2] > 0.5)
             continue
         comps = []
@@ -505,10 +521,14 @@
             once.append(step(state[p], c, behind, ahead, strip))
         else:
             once.append(step(state[p], c, behind, ahead))
+    copies = []
     for x in range(nx):
         behind = once[x] if x == 0 else once[x][strip]
         ahead = once[x + 2] if x == nx - 1 else once[x + 2][strip]
-        out_ref[x] = step(rows_of(state[x + 1], strip), once[x + 1], behind, ahead, strip)
+        buf[x] = step(rows_of(state[x + 1], strip), once[x + 1], behind, ahead, strip)
+        copies.append(pltpu.make_async_copy(buf.at[x], out_ref.at[x], sems.at[x]))
+        copies[-1].start()
+    wait_all(copies)
 
 
 def pairs(size, start):
@@ -562,15 +582,6 @@
     far = lax.ppermute(far, "horiz", far_pairs)
     near = lax.ppermute(near, "horiz", near_pairs)
 
-    velocity_next = call(
-        advance,
-        jax.ShapeDtypeStruct(velocity.shape, F32),
-        "advance",
-        [pltpu.VMEM((ncomp, nx, ny, nz), F32), pltpu.SemaphoreType.DMA((ncomp,))],
-        in_specs=[VMEM] * 6,
-        out_specs=anywhere,
-    )(velocity, far, near, first, second, got[1])
-
     wire = 2 * ncomp * size + 16
     wind, conc, cols, mf, mn, layer, frame = call(
         functools.partial(prepare, nv),
@@ -587,14 +598,26 @@
     )(*got, *lays, dust, terrain, eligible, first, second)
     mf = lax.ppermute(mf, "horiz", far_pairs)
     mn = lax.ppermute(mn, "horiz", near_pairs)
-    inner = [shaped(nx - 2, *dims, rows, LANES, dtype=F32) for dims in ((6,), (), (), ())]
-    inner = call(
-        functools.partial(interior, ny, size), inner, "interior", in_specs=[VMEM] * 4 + [anywhere]
-    )(frame, layer, conc, cols, far)
+    inner = [shaped(nx - 2, *dims, rows, LANES, dtype=F32) for dims in ((8,), (), (), ())]
+    *inner, mark = call(
+        functools.partial(interior, ny, size), inner + [shaped(8, LANES, dtype=F32)], "interior"
+    )(frame, layer, conc, cols)
+    velocity_next = call(
+        advance,
+        jax.ShapeDtypeStruct(velocity.shape, F32),
+        "advance",
+        [pltpu.VMEM((ncomp, nx, ny, nz), F32), pltpu.SemaphoreType.DMA((ncomp,))],
+        in_specs=[VMEM] * 7,
+        out_specs=anywhere,
+    )(velocity, far, near, first, second, got[1], mark)
+
     dust_next = call(
         functools.partial(transport, ny, nh),
         jax.ShapeDtypeStruct(dust.shape, F32),
         "transport",
+        [pltpu.VMEM(dust.shape, F32), pltpu.SemaphoreType.DMA((nx,))],
+        in_specs=[VMEM] * 12,
+        out_specs=anywhere,
     )(wind, frame, conc, cols, far, near, mf, mn, *inner)
     return (velocity_next, dust_next)
 

time: 27.7 us -> 27.7 us (level)
    ppermute x1, waiting for transfers between devices: 0.41 us -> 0.99 us  [local(): mf = lax.ppermute(mf, 'horiz', far_pairs)]
    ppermute x1, waiting for transfers between devices: 0.43 us -> 0.01 us  [local(): far = lax.ppermute(far, 'horiz', far_pairs)]
  transfers between devices with their start and end apart: 9 -> 9, of which waited for: 3 -> 2; matrix products, arithmetic and copies ran while one was open for 0% -> 0% of each run, Pallas kernels for 16% -> 15%
where the time goes in v8:
time: 27.7 us; the launch traced here: 27.4 us
  starting transfers between devices  18.1 us (65%)
  Pallas kernels  5.53 us (20%)
  waiting for transfers between devices  2.85 us (10%)
  between operations  0.82 us (3%)
    ppermute x1, starting transfers between devices, local(): first = lax.ppermute(first, 'vert', pairs(nv, 0)[1:])  7.54 us
    ppermute x3, starting transfers between devices, local(): lax.ppermute(strips[t], 'vert', [(0, t)])  2.77 us
    pallas_call x1, Pallas kernels, local(): call(advance, jax.ShapeDtypeStruct(velocity.shape, F32), 'advance', [pltp...  1.97 us
    ppermute x1, starting transfers between devices, local(): far = lax.ppermute(far, 'horiz', far_pairs)  1.92 us
    ppermute x1, starting transfers between devices, local(): mf = lax.ppermute(mf, 'horiz', far_pairs)  1.92 us
    ppermute x3, waiting for transfers between devices, local(): lax.ppermute(strips[t], 'vert', [(0, t)])  1.84 us
    ppermute x1, starting transfers between devices, local(): near = lax.ppermute(near, 'horiz', near_pairs)  1.66 us
    ppermute x1, starting transfers between devices, local(): mn = lax.ppermute(mn, 'horiz', near_pairs)  1.66 us
  transfers between devices with their start and end apart: 9, of which 2 were waited for; matrix products, arithmetic and copies ran while one was open for 0% of the time, Pallas kernels for 15%

profile of v8, /device:TPU:28, one launch (start us, length us, event | category | flops | bytes accessed | tf_op | source)
XLA Modules:
  0.0 27.4 jit_solution(15514480583387853528)
XLA Ops:
  0.6 0.0 copy-start.2
  0.6 0.0 copy-start.1
  0.7 0.0 copy-start
  0.7 0.0 copy-start.3
  0.7 0.1 pack_low.1
  0.8 0.8 %collective-permute-start.4 = (bf16[864,128]{1,0:T(8,128)(2,1)S(1)}, bf16[864,128]{1,0:T(8,128)(2,1)S(1)}, u32[]{:S(2)}, u32[]{:S(2)}) collective-permute-start(bf16[864,128]{1,0:T(8,128)(2,1)S(1)} %get-tuple-element.28), channel_id=1, source_target_pairs={{0,1},{4,5},{8,9},{12,13},{16,17},{20,21},{24,25},{28,29}} | collective-permute-start | bytes 663560 | tf_op jit(solution)/shard_map/ppermute | solution.py:564
  1.6 0.7 %collective-permute-start.5 = (bf16[816,128]{1,0:T(8,128)(2,1)S(1)}, bf16[816,128]{1,0:T(8,128)(2,1)S(1)}, u32[]{:S(2)}, u32[]{:S(2)}) collective-permute-start(bf16[816,128]{1,0:T(8,128)(2,1)S(1)} %get-tuple-element.30), channel_id=1, source_target_pairs={{0,2},{4,6},{8,10},{12,14},{16,18},{20,22},{24,26},{28,30}} | collective-permute-start | bytes 626696 | tf_op jit(solution)/shard_map/ppermute | solution.py:564
  2.3 1.3 %collective-permute-start.6 = (bf16[800,128]{1,0:T(8,128)(2,1)S(1)}, bf16[800,128]{1,0:T(8,128)(2,1)S(1)}, u32[]{:S(2)}, u32[]{:S(2)}) collective-permute-start(bf16[800,128]{1,0:T(8,128)(2,1)S(1)} %get-tuple-element.23.after_ref), channel_id=1, source_target_pairs={{0,3},{4,7},{8,11},{12,15},{16,19},{20,23},{24,27},{28,31}} | collective-permute-start | bytes 614408 | tf_op jit(solution)/shard_map/ppermute | solution.py:564
  3.6 0.0 copy-done
  3.6 1.1 %pack_ends.1 = (bf16[64,128]{1,0:T(8,128)(2,1)S(1)}, bf16[80,128]{1,0:T(8,128)(2,1)S(1)}, bf16[3,16,128]{2,1,0:T(8,128)(2,1)S(1)}) custom-call(f32[3,4,256,128]{3,2,1,0:T(8,128)S(1)} %copy-done, f32[4,64,128]{2,1,0:T(8,128)} %refs_5_.1, s32[4,64]{1,0:T(4,128)} %refs_6_.1, bf16[800,128]{1,0:T(8,128)(2,1)S(1)} %get-tuple-element.23.after_ref), custom_call_target="tpu_custom_call" | custom-call | flops 1048576 | bytes 1048576 | tf_op jit(solution)/shard_map/pack_ends/pallas_call | solution.py:566
  4.7 0.7 %collective-permute-start = (bf16[80,128]{1,0:T(8,128)(2,1)S(1)}, bf16[80,128]{1,0:T(8,128)(2,1)S(1)}, u32[]{:S(2)}, u32[]{:S(2)}) collective-permute-start(bf16[80,128]{1,0:T(8,128)(2,1)S(1)} %get-tuple-element.24), channel_id=1, source_target_pairs={{1,2},{2,1},{5,6},{6,5},{9,10},{10,9},{13,14},{14,13},{17,18},{18,... | collective-permute-start | bytes 61448 | tf_op jit(solution)/shard_map/ppermute | solution.py:574
  5.4 0.0 collective-permute-done.after_ref.second_ref.refs_9_
  5.4 7.5 %collective-permute-start.3 = (bf16[64,128]{1,0:T(8,128)(2,1)S(1)}, bf16[64,128]{1,0:T(8,128)(2,1)S(1)}, u32[]{:S(2)}, u32[]{:S(2)}) collective-permute-start(bf16[64,128]{1,0:T(8,128)(2,1)S(1)} %relay.1), channel_id=1, source_target_pairs={{1,0},{2,3},{3,2},{5,4},{6,7},{7,6},{9,8},{10,11},{11,10},{13,12},... | collective-permute-start | bytes 49160 | tf_op jit(solution)/shard_map/ppermute | solution.py:576
  13.0 0.0 copy-done.3
  13.0 0.1 copy.6.eligible_ref.refs_7_
  13.1 0.0 copy-done.2
  13.1 0.0 copy-done.1
  13.1 0.1 pack_sides.1
  13.2 1.9 %collective-permute-start.1 = (bf16[912,128]{1,0:T(8,128)(2,1)S(1)}, bf16[912,128]{1,0:T(8,128)(2,1)S(1)}, u32[]{:S(2)}, u32[]{:S(2)}) collective-permute-start(bf16[912,128]{1,0:T(8,128)(2,1)S(1)} %get-tuple-element.25), channel_id=1, source_target_pairs={{4,8},{8,4},{12,16},{16,12},{20,24},{24,20},{5,9},{9,5},{13,17},{1... | collective-permute-start | bytes 700424 | tf_op jit(solution)/shard_map/ppermute | solution.py:582
  15.1 0.0 collective-permute-done.3.refs_8_.first_ref
  15.2 1.7 %collective-permute-start.2 = (bf16[912,128]{1,0:T(8,128)(2,1)S(1)}, bf16[912,128]{1,0:T(8,128)(2,1)S(1)}, u32[]{:S(2)}, u32[]{:S(2)}) collective-permute-start(bf16[912,128]{1,0:T(8,128)(2,1)S(1)} %get-tuple-element.26), channel_id=1, source_target_pairs={{0,4},{4,0},{8,12},{12,8},{16,20},{20,16},{24,28},{28,24},{1,5},{5... | collective-permute-start | bytes 700424 | tf_op jit(solution)/shard_map/ppermute | solution.py:583
  16.8 1.8 %collective-permute-done.6.refs_3_ = bf16[800,128]{1,0:T(8,128)(2,1)S(1)} collective-permute-done((bf16[800,128]{1,0:T(8,128)(2,1)S(1)}, bf16[800,128]{1,0:T(8,128)(2,1)S(1)}, u32[]{:S(2)}, u32[]{:S(2)}) %collective-permute-start.6) | collective-permute-done | bytes 204832 | tf_op jit(solution)/shard_map/ppermute | solution.py:564
  18.7 0.0 collective-permute-done.5.refs_2_
  18.7 0.0 collective-permute-done.4.refs_1_.strip_ref
  18.7 0.4 %prepare.1 = (f32[6,80,128]{2,1,0:T(8,128)S(1)}, f32[4,80,128]{2,1,0:T(8,128)S(1)}, f32[16,128]{1,0:T(8,128)S(1)}, bf16[400,128]{1,0:T(8,128)(2,1)S(1)}, bf16[40...) custom-call(bf16[816,128]{1,0:T(8,128)(2,1)S(1)} %get-tuple-element.29.refs_0_, ...), custom_call_target="tpu_custom_call" | custom-call | flops 1048576 | bytes 1048576 | tf_op jit(solution)/shard_map/prepare/pallas_call | solution.py:586
  19.1 1.9 %collective-permute-start.7 = (bf16[400,128]{1,0:T(8,128)(2,1)S(1)}, bf16[400,128]{1,0:T(8,128)(2,1)S(1)}, u32[]{:S(2)}, u32[]{:S(2)}) collective-permute-start(bf16[400,128]{1,0:T(8,128)(2,1)S(1)} %get-tuple-element.38), channel_id=1, source_target_pairs={{4,8},{8,4},{12,16},{16,12},{20,24},{24,20},{5,9},{9,5},{13,17},{1... | collective-permute-start | bytes 307208 | tf_op jit(solution)/shard_map/ppermute | solution.py:599
  21.0 1.7 %collective-permute-start.8 = (bf16[400,128]{1,0:T(8,128)(2,1)S(1)}, bf16[400,128]{1,0:T(8,128)(2,1)S(1)}, u32[]{:S(2)}, u32[]{:S(2)}) collective-permute-start(bf16[400,128]{1,0:T(8,128)(2,1)S(1)} %get-tuple-element.39), channel_id=1, source_target_pairs={{0,4},{4,0},{8,12},{12,8},{16,20},{20,16},{24,28},{28,24},{1,5},{5... | collective-permute-start | bytes 307208 | tf_op jit(solution)/shard_map/ppermute | solution.py:600
  22.7 0.5 %interior.1 = (f32[2,8,80,128]{3,2,1,0:T(8,128)S(1)}, f32[2,80,128]{2,1,0:T(8,128)S(1)}, f32[2,80,128]{2,1,0:T(8,128)S(1)}, f32[2,80,128]{2,1,0:T(8,128)S(1)}, f32[8,128]{1,0:T(8,128)S(1)}) custom-call(f32[12,80,128]{2,1,0:T(8,128)S(1)} %get-tuple-element.32.frame.refs_1_, f32[16,128]{1,0:T(8,128)S(1)} %get-tuple-element.33.layer_ref, ...), custom_call_target="tpu_custom_call" | custom-call | flops 1048576 | bytes 1048576 | tf_op jit(solution)/shard_map/interior/pallas_call | solution.py:602
  23.2 0.0 collective-permute-done.1.far_ref.refs_4_
  23.2 0.0 collective-permute-done.2.near_ref.refs_5_
  23.2 2.0 %advance.1 = f32[3,4,256,128]{3,2,1,0:T(8,128)} custom-call(f32[3,4,256,128]{3,2,1,0:T(8,128)S(1)} %copy-done, bf16[912,128]{1,0:T(8,128)(2,1)S(1)} %collective-permute-done.1.far_ref.refs_4_, bf16[912,128]{1,0:T(8,128)(2,1)S(1)} %collective-permute-done.2.near_ref.refs_5_, bf16[64,128]{1,0:T(8,128)(2,1)S(1)} %collective-permute-done.3.refs_8_.first_ref, ...), custom_call_target="tpu_custom_call" | custom-call | flops 1048576 | bytes 1048576 | tf_op jit(solution)/shard_map/advance/pallas_call | solution.py:605
  25.2 1.0 %collective-permute-done.7.refs_6_ = bf16[400,128]{1,0:T(8,128)(2,1)S(1)} collective-permute-done((bf16[400,128]{1,0:T(8,128)(2,1)S(1)}, bf16[400,128]{1,0:T(8,128)(2,1)S(1)}, u32[]{:S(2)}, u32[]{:S(2)}) %collective-permute-start.7) | collective-permute-done | bytes 102432 | tf_op jit(solution)/shard_map/ppermute | solution.py:599
  26.2 0.0 collective-permute-done.8.refs_7_
  26.2 1.3 %transport.1 = f32[4,64,128]{2,1,0:T(8,128)} custom-call(f32[6,80,128]{2,1,0:T(8,128)S(1)} %get-tuple-element.37.refs_0_, f32[12,80,128]{2,1,0:T(8,128)S(1)} %get-tuple-element.32.frame.refs_1_, f32[4,80,128]{2,1,0:T(8,128)S(1)} %get-tuple-element.34.conc_ref.refs_2_, f32[16,128]{1,0:T(8,128)S(1)} %get-tuple-element.35.cols_ref.refs_3_, ...), custom_call_target="tpu_custom_call" | custom-call | flops 1048576 | bytes 1048576 | tf_op jit(solution)/shard_map/transport/pallas_call | solution.py:614
  (1 shorter events, 0.0 us)
Async XLA Ops:
  0.6 12.5 %copy-start.2 = (s32[4,64]{1,0:T(4,128)S(1)}, s32[4,64]{1,0:T(4,128)}, u32[]{:S(2)}) copy-start(s32[4,64]{1,0:T(4,128)} %refs_6_.1) | copy-start | bytes 3076
  0.6 12.4 %copy-start.1 = (f32[4,64,128]{2,1,0:T(8,128)S(1)}, f32[4,64,128]{2,1,0:T(8,128)}, u32[]{:S(2)}) copy-start(f32[4,64,128]{2,1,0:T(8,128)} %refs_5_.1) | copy-start | bytes 393220
  0.7 3.0 %copy-start = (f32[3,4,256,128]{3,2,1,0:T(8,128)S(1)}, f32[3,4,256,128]{3,2,1,0:T(8,128)}, u32[]{:S(2)}) copy-start(f32[3,4,256,128]{3,2,1,0:T(8,128)} %v_ref.7) | copy-start | bytes 4718596
  0.7 12.3 %copy-start.3 = (s32[4,2]{0,1:T(2,128)S(1)}, s32[4,2]{0,1:T(2,128)}, u32[]{:S(2)}) copy-start(s32[4,2]{0,1:T(2,128)} %param.6) | copy-start | bytes 100
  0.8 17.8 %collective-permute-start.4 = (bf16[864,128]{1,0:T(8,128)(2,1)S(1)}, bf16[864,128]{1,0:T(8,128)(2,1)S(1)}, u32[]{:S(2)}, u32[]{:S(2)}) collective-permute-start(bf16[864,128]{1,0:T(8,128)(2,1)S(1)} %get-tuple-element.28), channel_id=1, source_target_pairs={{0,1},{4,5},{8,9},{12,13},{16,17},{20,21},{24,25},{28,29}} | collective-permute-start | bytes 663560 | tf_op jit(solution)/shard_map/ppermute | solution.py:564
  1.6 17.0 %collective-permute-start.5 = (bf16[816,128]{1,0:T(8,128)(2,1)S(1)}, bf16[816,128]{1,0:T(8,128)(2,1)S(1)}, u32[]{:S(2)}, u32[]{:S(2)}) collective-permute-start(bf16[816,128]{1,0:T(8,128)(2,1)S(1)} %get-tuple-element.30), channel_id=1, source_target_pairs={{0,2},{4,6},{8,10},{12,14},{16,18},{20,22},{24,26},{28,30}} | collective-permute-start | bytes 626696 | tf_op jit(solution)/shard_map/ppermute | solution.py:564
  2.3 16.3 %collective-permute-start.6 = (bf16[800,128]{1,0:T(8,128)(2,1)S(1)}, bf16[800,128]{1,0:T(8,128)(2,1)S(1)}, u32[]{:S(2)}, u32[]{:S(2)}) collective-permute-start(bf16[800,128]{1,0:T(8,128)(2,1)S(1)} %get-tuple-element.23.after_ref), channel_id=1, source_target_pairs={{0,3},{4,7},{8,11},{12,15},{16,19},{20,23},{24,27},{28,31}} | collective-permute-start | bytes 614408 | tf_op jit(solution)/shard_map/ppermute | solution.py:564
  4.7 0.7 %collective-permute-start = (bf16[80,128]{1,0:T(8,128)(2,1)S(1)}, bf16[80,128]{1,0:T(8,128)(2,1)S(1)}, u32[]{:S(2)}, u32[]{:S(2)}) collective-permute-start(bf16[80,128]{1,0:T(8,128)(2,1)S(1)} %get-tuple-element.24), channel_id=1, source_target_pairs={{1,2},{2,1},{5,6},{6,5},{9,10},{10,9},{13,14},{14,13},{17,18},{18,... | collective-permute-start | bytes 61448 | tf_op jit(solution)/shard_map/ppermute | solution.py:574
  5.4 9.7 %collective-permute-start.3 = (bf16[64,128]{1,0:T(8,128)(2,1)S(1)}, bf16[64,128]{1,0:T(8,128)(2,1)S(1)}, u32[]{:S(2)}, u32[]{:S(2)}) collective-permute-start(bf16[64,128]{1,0:T(8,128)(2,1)S(1)} %relay.1), channel_id=1, source_target_pairs={{1,0},{2,3},{3,2},{5,4},{6,7},{7,6},{9,8},{10,11},{11,10},{13,12},... | collective-permute-start | bytes 49160 | tf_op jit(solution)/shard_map/ppermute | solution.py:576
  13.2 9.9 %collective-permute-start.1 = (bf16[912,128]{1,0:T(8,128)(2,1)S(1)}, bf16[912,128]{1,0:T(8,128)(2,1)S(1)}, u32[]{:S(2)}, u32[]{:S(2)}) collective-permute-start(bf16[912,128]{1,0:T(8,128)(2,1)S(1)} %get-tuple-element.25), channel_id=1, source_target_pairs={{4,8},{8,4},{12,16},{16,12},{20,24},{24,20},{5,9},{9,5},{13,17},{1... | collective-permute-start | bytes 700424 | tf_op jit(solution)/shard_map/ppermute | solution.py:582
  15.2 8.0 %collective-permute-start.2 = (bf16[912,128]{1,0:T(8,128)(2,1)S(1)}, bf16[912,128]{1,0:T(8,128)(2,1)S(1)}, u32[]{:S(2)}, u32[]{:S(2)}) collective-permute-start(bf16[912,128]{1,0:T(8,128)(2,1)S(1)} %get-tuple-element.26), channel_id=1, source_target_pairs={{0,4},{4,0},{8,12},{12,8},{16,20},{20,16},{24,28},{28,24},{1,5},{5... | collective-permute-start | bytes 700424 | tf_op jit(solution)/shard_map/ppermute | solution.py:583
  19.1 7.1 %collective-permute-start.7 = (bf16[400,128]{1,0:T(8,128)(2,1)S(1)}, bf16[400,128]{1,0:T(8,128)(2,1)S(1)}, u32[]{:S(2)}, u32[]{:S(2)}) collective-permute-start(bf16[400,128]{1,0:T(8,128)(2,1)S(1)} %get-tuple-element.38), channel_id=1, source_target_pairs={{4,8},{8,4},{12,16},{16,12},{20,24},{24,20},{5,9},{9,5},{13,17},{1... | collective-permute-start | bytes 307208 | tf_op jit(solution)/shard_map/ppermute | solution.py:599
  21.0 5.1 %collective-permute-start.8 = (bf16[400,128]{1,0:T(8,128)(2,1)S(1)}, bf16[400,128]{1,0:T(8,128)(2,1)S(1)}, u32[]{:S(2)}, u32[]{:S(2)}) collective-permute-start(bf16[400,128]{1,0:T(8,128)(2,1)S(1)} %get-tuple-element.39), channel_id=1, source_target_pairs={{0,4},{4,0},{8,12},{12,8},{16,20},{20,16},{24,28},{28,24},{1,5},{5... | collective-permute-start | bytes 307208 | tf_op jit(solution)/shard_map/ppermute | solution.py:600

commit v9 on v8

--- a/solution.py
+++ b/solution.py
@@ -448,87 +448,92 @@
     rows = size + 2 * EDGE
     column = lax.axis_index("horiz")
     odd = lax.rem(column, 2) == 1
-    low = iota((EDGE, nz), 0)
-
-    def either(one, other, start, n):
-        return jnp.where(odd, one[start : start + n].astype(F32), other[start : start + n].astype(F32))
-
-    def framed(rows, ends=None, halo=0):
-        head, tail = (jnp.zeros((EDGE, nz), F32),) * 2
-        if ends is not None:
-            head = jnp.where(low == EDGE - 1, ends[halo : halo + 1], head)
-            tail = jnp.where(low == 0, ends[ncomp + 1 + halo : ncomp + 2 + halo], tail)
-        return jnp.concatenate([head, rows, tail], 0)
-
-    pairs_of = {"below": (near_ref, far_ref, face_near, face_far), "above": (far_ref, near_ref, face_far, face_near)}
-    ends, dusts, marks = ({}, {}, {})
-    for side, (one, other, face_one, face_other) in pairs_of.items():
-        ends[side] = either(one, other, 2 * ncomp * size, 16)
-        at = ncomp * ny
-        dusts[side] = (
-            framed(either(face_one, face_other, at, size), ends[side], ncomp),
-            either(face_one, face_other, at + size, size),
-        )
-        marks[side] = either(face_one, face_other, at + 2 * size, 16)
-
-    def part(side, i, halo=None):
-        rows = either(*pairs_of[side][:2], i * size, size)
-        return rows if halo is None else framed(rows, ends[side], halo)
-
-    below, above = ("below", "above")
-    conc = [dusts[below][1], dusts[below][0]]
-    conc += [conc_ref[x] for x in range(nx)]
-    conc += [dusts[above][0], dusts[above][1]]
-    table = jnp.concatenate([marks[below], cols_ref[...], marks[above], jnp.zeros((LANES - 48, LANES), F32)], 0).T[:rows]
-    mark = 0
-    ground = [mark] + [16 + x for x in range(nx)] + [32 + mark]
-    lifted = [mark + 1] + [16 + EDGE + x for x in range(nx)] + [33 + mark]
-    inside = domain_rows((rows, nz), ny, size)
-    strip = slice(EDGE, EDGE + size)
-    state = [None] * (nx + 2)
-    for p in range(nx + 2):
-        if 1 < p < nx:
-            coef = [(coef_ref[p - 2, 2 * i], coef_ref[p - 2, 2 * i + 1]) for i in range(4)]
-            state[p] = (coef, lift_ref[p - 2], keep_ref[p - 2] > 0.5)
-            continue
-        comps = []
-        for comp in range(ncomp):
+
+    def run(upper):
+        low = iota((EDGE, nz), 0)
+
+        def either(one, other, start, n):
+            return (one if upper else other)[start : start + n].astype(F32)
+
+        def framed(rows, ends=None, halo=0):
+            head, tail = (jnp.zeros((EDGE, nz), F32),) * 2
+            if ends is not None:
+                head = jnp.where(low == EDGE - 1, ends[halo : halo + 1], head)
+                tail = jnp.where(low == 0, ends[ncomp + 1 + halo : ncomp + 2 + halo], tail)
+            return jnp.concatenate([head, rows, tail], 0)
+
+        pairs_of = {"below": (near_ref, far_ref, face_near, face_far), "above": (far_ref, near_ref, face_far, face_near)}
+        ends, dusts, marks = ({}, {}, {})
+        for side, (one, other, face_one, face_other) in pairs_of.items():
+            ends[side] = either(one, other, 2 * ncomp * size, 16)
+            at = ncomp * ny
+            dusts[side] = (
+                framed(either(face_one, face_other, at, size), ends[side], ncomp),
+                either(face_one, face_other, at + size, size),
+            )
+            marks[side] = either(face_one, face_other, at + 2 * size, 16)
+
+        def part(side, i, halo=None):
+            rows = either(*pairs_of[side][:2], i * size, size)
+            return rows if halo is None else framed(rows, ends[side], halo)
+
+        below, above = ("below", "above")
+        conc = [dusts[below][1], dusts[below][0]]
+        conc += [conc_ref[x] for x in range(nx)]
+        conc += [dusts[above][0], dusts[above][1]]
+        table = jnp.concatenate([marks[below], cols_ref[...], marks[above], jnp.zeros((LANES - 48, LANES), F32)], 0).T[:rows]
+        mark = 0
+        ground = [mark] + [16 + x for x in range(nx)] + [32 + mark]
+        lifted = [mark + 1] + [16 + EDGE + x for x in range(nx)] + [33 + mark]
+        inside = domain_rows((rows, nz), ny, size)
+        strip = slice(EDGE, EDGE + size)
+        state = [None] * (nx + 2)
+        for p in range(nx + 2):
+            if 1 < p < nx:
+                coef = [(coef_ref[p - 2, 2 * i], coef_ref[p - 2, 2 * i + 1]) for i in range(4)]
+                state[p] = (coef, lift_ref[p - 2], keep_ref[p - 2] > 0.5)
+                continue
+            comps = []
+            for comp in range(ncomp):
+                if p == 0:
+                    w = part(below, ncomp + comp) + 0.12 * frame[comp * nx, strip]
+                elif p == nx + 1:
+                    w = part(above, ncomp + comp) + 0.12 * frame[comp * nx + nx - 1, strip]
+                elif p == 1:
+                    w = wind_ref[comp] + 0.12 * part(below, comp, comp)
+                else:
+                    w = wind_ref[ncomp + comp] + 0.12 * part(above, comp, comp)
+                comps.append(w)
+            rise, base = (table[:, lifted[p] : lifted[p] + 1], table[:, ground[p] : ground[p] + 1])
             if p == 0:
-                w = part(below, ncomp + comp) + 0.12 * frame[comp * nx, strip]
+                state[p] = plane_state(comps, rise[strip], base[strip], inside[strip] & (column > 0))
             elif p == nx + 1:
-                w = part(above, ncomp + comp) + 0.12 * frame[comp * nx + nx - 1, strip]
-            elif p == 1:
-                w = wind_ref[comp] + 0.12 * part(below, comp, comp)
+                state[p] = plane_state(comps, rise[strip], base[strip], inside[strip] & (column < nhoriz - 1))
             else:
-                w = wind_ref[ncomp + comp] + 0.12 * part(above, comp, comp)
-            comps.append(w)
-        rise, base = (table[:, lifted[p] : lifted[p] + 1], table[:, ground[p] : ground[p] + 1])
-        if p == 0:
-            state[p] = plane_state(comps, rise[strip], base[strip], inside[strip] & (column > 0))
-        elif p == nx + 1:
-            state[p] = plane_state(comps, rise[strip], base[strip], inside[strip] & (column < nhoriz - 1))
-        else:
-            state[p] = plane_state(comps, rise, base, inside)
-
-    once = []
-    for p in range(nx + 2):
-        c, behind, ahead = (conc[p + 1], conc[p], conc[p + 2])
-        if 1 < p < nx:
-            once.append(once_ref[p - 2])
-        elif p in (0, nx + 1):
-            behind = behind if p == 0 else behind[strip]
-            ahead = ahead[strip] if p == 0 else ahead
-            once.append(step(state[p], c, behind, ahead, strip))
-        else:
-            once.append(step(state[p], c, behind, ahead))
-    copies = []
-    for x in range(nx):
-        behind = once[x] if x == 0 else once[x][strip]
-        ahead = once[x + 2] if x == nx - 1 else once[x + 2][strip]
-        buf[x] = step(rows_of(state[x + 1], strip), once[x + 1], behind, ahead, strip)
-        copies.append(pltpu.make_async_copy(buf.at[x], out_ref.at[x], sems.at[x]))
-        copies[-1].start()
-    wait_all(copies)
+                state[p] = plane_state(comps, rise, base, inside)
+
+        once = []
+        for p in range(nx + 2):
+            c, behind, ahead = (conc[p + 1], conc[p], conc[p + 2])
+            if 1 < p < nx:
+                once.append(once_ref[p - 2])
+            elif p in (0, nx + 1):
+                behind = behind if p == 0 else behind[strip]
+                ahead = ahead[strip] if p == 0 else ahead
+                once.append(step(state[p], c, behind, ahead, strip))
+            else:
+                once.append(step(state[p], c, behind, ahead))
+        copies = []
+        for x in range(nx):
+            behind = once[x] if x == 0 else once[x][strip]
+            ahead = once[x + 2] if x == nx - 1 else once[x + 2][strip]
+            buf[x] = step(rows_of(state[x + 1], strip), once[x + 1], behind, ahead, strip)
+            copies.append(pltpu.make_async_copy(buf.at[x], out_ref.at[x], sems.at[x]))
+            copies[-1].start()
+        wait_all(copies)
+
+    pl.when(odd)(functools.partial(run, True))
+    pl.when(jnp.logical_not(odd))(functools.partial(run, False))
 
 
 def pairs(size, start):

time: 27.7 us -> 27.7 us (level)
  no operation moved by 1% of the time
where the time goes in v9:
time: 27.7 us; the launch traced here: 27.4 us
  starting transfers between devices  18.1 us (65%)
  Pallas kernels  5.48 us (20%)
  waiting for transfers between devices  2.85 us (10%)
  between operations  0.82 us (3%)
    ppermute x1, starting transfers between devices, local(): first = lax.ppermute(first, 'vert', pairs(nv, 0)[1:])  7.54 us
    ppermute x3, starting transfers between devices, local(): lax.ppermute(strips[t], 'vert', [(0, t)])  2.77 us
    pallas_call x1, Pallas kernels, local(): call(advance, jax.ShapeDtypeStruct(velocity.shape, F32), 'advance', [pltp...  1.97 us
    ppermute x1, starting transfers between devices, local(): far = lax.ppermute(far, 'horiz', far_pairs)  1.92 us
    ppermute x1, starting transfers between devices, local(): mf = lax.ppermute(mf, 'horiz', far_pairs)  1.92 us
    ppermute x3, waiting for transfers between devices, local(): lax.ppermute(strips[t], 'vert', [(0, t)])  1.84 us
    ppermute x1, starting transfers between devices, local(): near = lax.ppermute(near, 'horiz', near_pairs)  1.66 us
    ppermute x1, starting transfers between devices, local(): mn = lax.ppermute(mn, 'horiz', near_pairs)  1.66 us
  transfers between devices with their start and end apart: 9, of which 2 were waited for; matrix products, arithmetic and copies ran while one was open for 0% of the time, Pallas kernels for 15%

profile of v9, /device:TPU:28, one launch (start us, length us, event | category | flops | bytes accessed | tf_op | source)
XLA Modules:
  0.0 27.4 jit_solution(10071749433700704903)
XLA Ops:
  0.6 0.0 copy-start.2
  0.6 0.0 copy-start.1
  0.7 0.0 copy-start
  0.7 0.0 copy-start.3
  0.7 0.1 pack_low.1
  0.8 0.8 %collective-permute-start.4 = (bf16[864,128]{1,0:T(8,128)(2,1)S(1)}, bf16[864,128]{1,0:T(8,128)(2,1)S(1)}, u32[]{:S(2)}, u32[]{:S(2)}) collective-permute-start(bf16[864,128]{1,0:T(8,128)(2,1)S(1)} %get-tuple-element.28), channel_id=1, source_target_pairs={{0,1},{4,5},{8,9},{12,13},{16,17},{20,21},{24,25},{28,29}} | collective-permute-start | bytes 663560 | tf_op jit(solution)/shard_map/ppermute | solution.py:569
  1.6 0.7 %collective-permute-start.5 = (bf16[816,128]{1,0:T(8,128)(2,1)S(1)}, bf16[816,128]{1,0:T(8,128)(2,1)S(1)}, u32[]{:S(2)}, u32[]{:S(2)}) collective-permute-start(bf16[816,128]{1,0:T(8,128)(2,1)S(1)} %get-tuple-element.30), channel_id=1, source_target_pairs={{0,2},{4,6},{8,10},{12,14},{16,18},{20,22},{24,26},{28,30}} | collective-permute-start | bytes 626696 | tf_op jit(solution)/shard_map/ppermute | solution.py:569
  2.3 1.3 %collective-permute-start.6 = (bf16[800,128]{1,0:T(8,128)(2,1)S(1)}, bf16[800,128]{1,0:T(8,128)(2,1)S(1)}, u32[]{:S(2)}, u32[]{:S(2)}) collective-permute-start(bf16[800,128]{1,0:T(8,128)(2,1)S(1)} %get-tuple-element.23.after_ref), channel_id=1, source_target_pairs={{0,3},{4,7},{8,11},{12,15},{16,19},{20,23},{24,27},{28,31}} | collective-permute-start | bytes 614408 | tf_op jit(solution)/shard_map/ppermute | solution.py:569
  3.6 0.0 copy-done
  3.6 1.1 %pack_ends.1 = (bf16[64,128]{1,0:T(8,128)(2,1)S(1)}, bf16[80,128]{1,0:T(8,128)(2,1)S(1)}, bf16[3,16,128]{2,1,0:T(8,128)(2,1)S(1)}) custom-call(f32[3,4,256,128]{3,2,1,0:T(8,128)S(1)} %copy-done, f32[4,64,128]{2,1,0:T(8,128)} %refs_5_.1, s32[4,64]{1,0:T(4,128)} %refs_6_.1, bf16[800,128]{1,0:T(8,128)(2,1)S(1)} %get-tuple-element.23.after_ref), custom_call_target="tpu_custom_call" | custom-call | flops 1048576 | bytes 1048576 | tf_op jit(solution)/shard_map/pack_ends/pallas_call | solution.py:571
  4.7 0.7 %collective-permute-start = (bf16[80,128]{1,0:T(8,128)(2,1)S(1)}, bf16[80,128]{1,0:T(8,128)(2,1)S(1)}, u32[]{:S(2)}, u32[]{:S(2)}) collective-permute-start(bf16[80,128]{1,0:T(8,128)(2,1)S(1)} %get-tuple-element.24), channel_id=1, source_target_pairs={{1,2},{2,1},{5,6},{6,5},{9,10},{10,9},{13,14},{14,13},{17,18},{18,... | collective-permute-start | bytes 61448 | tf_op jit(solution)/shard_map/ppermute | solution.py:579
  5.4 0.0 collective-permute-done.after_ref.second_ref.refs_9_
  5.4 7.5 %collective-permute-start.3 = (bf16[64,128]{1,0:T(8,128)(2,1)S(1)}, bf16[64,128]{1,0:T(8,128)(2,1)S(1)}, u32[]{:S(2)}, u32[]{:S(2)}) collective-permute-start(bf16[64,128]{1,0:T(8,128)(2,1)S(1)} %relay.1), channel_id=1, source_target_pairs={{1,0},{2,3},{3,2},{5,4},{6,7},{7,6},{9,8},{10,11},{11,10},{13,12},... | collective-permute-start | bytes 49160 | tf_op jit(solution)/shard_map/ppermute | solution.py:581
  13.0 0.0 copy-done.3
  13.0 0.1 copy.6.eligible_ref.refs_7_
  13.1 0.0 copy-done.2
  13.1 0.0 copy-done.1
  13.1 0.1 pack_sides.1
  13.2 1.9 %collective-permute-start.1 = (bf16[912,128]{1,0:T(8,128)(2,1)S(1)}, bf16[912,128]{1,0:T(8,128)(2,1)S(1)}, u32[]{:S(2)}, u32[]{:S(2)}) collective-permute-start(bf16[912,128]{1,0:T(8,128)(2,1)S(1)} %get-tuple-element.25), channel_id=1, source_target_pairs={{4,8},{8,4},{12,16},{16,12},{20,24},{24,20},{5,9},{9,5},{13,17},{1... | collective-permute-start | bytes 700424 | tf_op jit(solution)/shard_map/ppermute | solution.py:587
  15.1 0.0 collective-permute-done.3.refs_8_.first_ref
  15.2 1.7 %collective-permute-start.2 = (bf16[912,128]{1,0:T(8,128)(2,1)S(1)}, bf16[912,128]{1,0:T(8,128)(2,1)S(1)}, u32[]{:S(2)}, u32[]{:S(2)}) collective-permute-start(bf16[912,128]{1,0:T(8,128)(2,1)S(1)} %get-tuple-element.26), channel_id=1, source_target_pairs={{0,4},{4,0},{8,12},{12,8},{16,20},{20,16},{24,28},{28,24},{1,5},{5... | collective-permute-start | bytes 700424 | tf_op jit(solution)/shard_map/ppermute | solution.py:588
  16.8 1.8 %collective-permute-done.6.refs_3_ = bf16[800,128]{1,0:T(8,128)(2,1)S(1)} collective-permute-done((bf16[800,128]{1,0:T(8,128)(2,1)S(1)}, bf16[800,128]{1,0:T(8,128)(2,1)S(1)}, u32[]{:S(2)}, u32[]{:S(2)}) %collective-permute-start.6) | collective-permute-done | bytes 204832 | tf_op jit(solution)/shard_map/ppermute | solution.py:569
  18.7 0.0 collective-permute-done.5.refs_2_
  18.7 0.0 collective-permute-done.4.refs_1_.strip_ref
  18.7 0.4 %prepare.1 = (f32[6,80,128]{2,1,0:T(8,128)S(1)}, f32[4,80,128]{2,1,0:T(8,128)S(1)}, f32[16,128]{1,0:T(8,128)S(1)}, bf16[400,128]{1,0:T(8,128)(2,1)S(1)}, bf16[40...) custom-call(bf16[816,128]{1,0:T(8,128)(2,1)S(1)} %get-tuple-element.29.refs_0_, ...), custom_call_target="tpu_custom_call" | custom-call | flops 1048576 | bytes 1048576 | tf_op jit(solution)/shard_map/prepare/pallas_call | solution.py:591
  19.1 1.9 %collective-permute-start.7 = (bf16[400,128]{1,0:T(8,128)(2,1)S(1)}, bf16[400,128]{1,0:T(8,128)(2,1)S(1)}, u32[]{:S(2)}, u32[]{:S(2)}) collective-permute-start(bf16[400,128]{1,0:T(8,128)(2,1)S(1)} %get-tuple-element.38), channel_id=1, source_target_pairs={{4,8},{8,4},{12,16},{16,12},{20,24},{24,20},{5,9},{9,5},{13,17},{1... | collective-permute-start | bytes 307208 | tf_op jit(solution)/shard_map/ppermute | solution.py:604
  21.0 1.7 %collective-permute-start.8 = (bf16[400,128]{1,0:T(8,128)(2,1)S(1)}, bf16[400,128]{1,0:T(8,128)(2,1)S(1)}, u32[]{:S(2)}, u32[]{:S(2)}) collective-permute-start(bf16[400,128]{1,0:T(8,128)(2,1)S(1)} %get-tuple-element.39), channel_id=1, source_target_pairs={{0,4},{4,0},{8,12},{12,8},{16,20},{20,16},{24,28},{28,24},{1,5},{5... | collective-permute-start | bytes 307208 | tf_op jit(solution)/shard_map/ppermute | solution.py:605
  22.7 0.5 %interior.1 = (f32[2,8,80,128]{3,2,1,0:T(8,128)S(1)}, f32[2,80,128]{2,1,0:T(8,128)S(1)}, f32[2,80,128]{2,1,0:T(8,128)S(1)}, f32[2,80,128]{2,1,0:T(8,128)S(1)}, f32[8,128]{1,0:T(8,128)S(1)}) custom-call(f32[12,80,128]{2,1,0:T(8,128)S(1)} %get-tuple-element.32.frame.refs_1_, f32[16,128]{1,0:T(8,128)S(1)} %get-tuple-element.33.layer_ref, ...), custom_call_target="tpu_custom_call" | custom-call | flops 1048576 | bytes 1048576 | tf_op jit(solution)/shard_map/interior/pallas_call | solution.py:607
  23.2 0.0 collective-permute-done.1.far_ref.refs_4_
  23.2 0.0 collective-permute-done.2.near_ref.refs_5_
  23.2 2.0 %advance.1 = f32[3,4,256,128]{3,2,1,0:T(8,128)} custom-call(f32[3,4,256,128]{3,2,1,0:T(8,128)S(1)} %copy-done, bf16[912,128]{1,0:T(8,128)(2,1)S(1)} %collective-permute-done.1.far_ref.refs_4_, bf16[912,128]{1,0:T(8,128)(2,1)S(1)} %collective-permute-done.2.near_ref.refs_5_, bf16[64,128]{1,0:T(8,128)(2,1)S(1)} %collective-permute-done.3.refs_8_.first_ref, ...), custom_call_target="tpu_custom_call" | custom-call | flops 1048576 | bytes 1048576 | tf_op jit(solution)/shard_map/advance/pallas_call | solution.py:610
  25.2 1.0 %collective-permute-done.7.refs_6_ = bf16[400,128]{1,0:T(8,128)(2,1)S(1)} collective-permute-done((bf16[400,128]{1,0:T(8,128)(2,1)S(1)}, bf16[400,128]{1,0:T(8,128)(2,1)S(1)}, u32[]{:S(2)}, u32[]{:S(2)}) %collective-permute-start.7) | collective-permute-done | bytes 102432 | tf_op jit(solution)/shard_map/ppermute | solution.py:604
  26.2 0.0 collective-permute-done.8.refs_7_
  26.2 1.2 %transport.1 = f32[4,64,128]{2,1,0:T(8,128)} custom-call(f32[6,80,128]{2,1,0:T(8,128)S(1)} %get-tuple-element.37.refs_0_, f32[12,80,128]{2,1,0:T(8,128)S(1)} %get-tuple-element.32.frame.refs_1_, f32[4,80,128]{2,1,0:T(8,128)S(1)} %get-tuple-element.34.conc_ref.refs_2_, f32[16,128]{1,0:T(8,128)S(1)} %get-tuple-element.35.cols_ref.refs_3_, ...), custom_call_target="tpu_custom_call" | custom-call | flops 1048576 | bytes 1048576 | tf_op jit(solution)/shard_map/transport/pallas_call | solution.py:619
  (1 shorter events, 0.0 us)
Async XLA Ops:
  0.6 12.5 %copy-start.2 = (s32[4,64]{1,0:T(4,128)S(1)}, s32[4,64]{1,0:T(4,128)}, u32[]{:S(2)}) copy-start(s32[4,64]{1,0:T(4,128)} %refs_6_.1) | copy-start | bytes 3076
  0.6 12.4 %copy-start.1 = (f32[4,64,128]{2,1,0:T(8,128)S(1)}, f32[4,64,128]{2,1,0:T(8,128)}, u32[]{:S(2)}) copy-start(f32[4,64,128]{2,1,0:T(8,128)} %refs_5_.1) | copy-start | bytes 393220
  0.7 3.0 %copy-start = (f32[3,4,256,128]{3,2,1,0:T(8,128)S(1)}, f32[3,4,256,128]{3,2,1,0:T(8,128)}, u32[]{:S(2)}) copy-start(f32[3,4,256,128]{3,2,1,0:T(8,128)} %v_ref.7) | copy-start | bytes 4718596
  0.7 12.3 %copy-start.3 = (s32[4,2]{0,1:T(2,128)S(1)}, s32[4,2]{0,1:T(2,128)}, u32[]{:S(2)}) copy-start(s32[4,2]{0,1:T(2,128)} %param.6) | copy-start | bytes 100
  0.8 17.8 %collective-permute-start.4 = (bf16[864,128]{1,0:T(8,128)(2,1)S(1)}, bf16[864,128]{1,0:T(8,128)(2,1)S(1)}, u32[]{:S(2)}, u32[]{:S(2)}) collective-permute-start(bf16[864,128]{1,0:T(8,128)(2,1)S(1)} %get-tuple-element.28), channel_id=1, source_target_pairs={{0,1},{4,5},{8,9},{12,13},{16,17},{20,21},{24,25},{28,29}} | collective-permute-start | bytes 663560 | tf_op jit(solution)/shard_map/ppermute | solution.py:569
  1.6 17.0 %collective-permute-start.5 = (bf16[816,128]{1,0:T(8,128)(2,1)S(1)}, bf16[816,128]{1,0:T(8,128)(2,1)S(1)}, u32[]{:S(2)}, u32[]{:S(2)}) collective-permute-start(bf16[816,128]{1,0:T(8,128)(2,1)S(1)} %get-tuple-element.30), channel_id=1, source_target_pairs={{0,2},{4,6},{8,10},{12,14},{16,18},{20,22},{24,26},{28,30}} | collective-permute-start | bytes 626696 | tf_op jit(solution)/shard_map/ppermute | solution.py:569
  2.3 16.3 %collective-permute-start.6 = (bf16[800,128]{1,0:T(8,128)(2,1)S(1)}, bf16[800,128]{1,0:T(8,128)(2,1)S(1)}, u32[]{:S(2)}, u32[]{:S(2)}) collective-permute-start(bf16[800,128]{1,0:T(8,128)(2,1)S(1)} %get-tuple-element.23.after_ref), channel_id=1, source_target_pairs={{0,3},{4,7},{8,11},{12,15},{16,19},{20,23},{24,27},{28,31}} | collective-permute-start | bytes 614408 | tf_op jit(solution)/shard_map/ppermute | solution.py:569
  4.7 0.7 %collective-permute-start = (bf16[80,128]{1,0:T(8,128)(2,1)S(1)}, bf16[80,128]{1,0:T(8,128)(2,1)S(1)}, u32[]{:S(2)}, u32[]{:S(2)}) collective-permute-start(bf16[80,128]{1,0:T(8,128)(2,1)S(1)} %get-tuple-element.24), channel_id=1, source_target_pairs={{1,2},{2,1},{5,6},{6,5},{9,10},{10,9},{13,14},{14,13},{17,18},{18,... | collective-permute-start | bytes 61448 | tf_op jit(solution)/shard_map/ppermute | solution.py:579
  5.4 9.7 %collective-permute-start.3 = (bf16[64,128]{1,0:T(8,128)(2,1)S(1)}, bf16[64,128]{1,0:T(8,128)(2,1)S(1)}, u32[]{:S(2)}, u32[]{:S(2)}) collective-permute-start(bf16[64,128]{1,0:T(8,128)(2,1)S(1)} %relay.1), channel_id=1, source_target_pairs={{1,0},{2,3},{3,2},{5,4},{6,7},{7,6},{9,8},{10,11},{11,10},{13,12},... | collective-permute-start | bytes 49160 | tf_op jit(solution)/shard_map/ppermute | solution.py:581
  13.2 9.9 %collective-permute-start.1 = (bf16[912,128]{1,0:T(8,128)(2,1)S(1)}, bf16[912,128]{1,0:T(8,128)(2,1)S(1)}, u32[]{:S(2)}, u32[]{:S(2)}) collective-permute-start(bf16[912,128]{1,0:T(8,128)(2,1)S(1)} %get-tuple-element.25), channel_id=1, source_target_pairs={{4,8},{8,4},{12,16},{16,12},{20,24},{24,20},{5,9},{9,5},{13,17},{1... | collective-permute-start | bytes 700424 | tf_op jit(solution)/shard_map/ppermute | solution.py:587
  15.2 8.0 %collective-permute-start.2 = (bf16[912,128]{1,0:T(8,128)(2,1)S(1)}, bf16[912,128]{1,0:T(8,128)(2,1)S(1)}, u32[]{:S(2)}, u32[]{:S(2)}) collective-permute-start(bf16[912,128]{1,0:T(8,128)(2,1)S(1)} %get-tuple-element.26), channel_id=1, source_target_pairs={{0,4},{4,0},{8,12},{12,8},{16,20},{20,16},{24,28},{28,24},{1,5},{5... | collective-permute-start | bytes 700424 | tf_op jit(solution)/shard_map/ppermute | solution.py:588
  19.1 7.1 %collective-permute-start.7 = (bf16[400,128]{1,0:T(8,128)(2,1)S(1)}, bf16[400,128]{1,0:T(8,128)(2,1)S(1)}, u32[]{:S(2)}, u32[]{:S(2)}) collective-permute-start(bf16[400,128]{1,0:T(8,128)(2,1)S(1)} %get-tuple-element.38), channel_id=1, source_target_pairs={{4,8},{8,4},{12,16},{16,12},{20,24},{24,20},{5,9},{9,5},{13,17},{1... | collective-permute-start | bytes 307208 | tf_op jit(solution)/shard_map/ppermute | solution.py:604
  21.0 5.1 %collective-permute-start.8 = (bf16[400,128]{1,0:T(8,128)(2,1)S(1)}, bf16[400,128]{1,0:T(8,128)(2,1)S(1)}, u32[]{:S(2)}, u32[]{:S(2)}) collective-permute-start(bf16[400,128]{1,0:T(8,128)(2,1)S(1)} %get-tuple-element.39), channel_id=1, source_target_pairs={{0,4},{4,0},{8,12},{12,8},{16,20},{20,16},{24,28},{28,24},{1,5},{5... | collective-permute-start | bytes 307208 | tf_op jit(solution)/shard_map/ppermute | solution.py:605
